TPU v7x, 32 devices: a whole 2x2x4 slice. The times are simulated.
32 devices in a mesh: dp: 4 (over y, x), seq: 8 (over z, core).
Axes of the slice: x: 2, y: 2, z: 4, core: 2. Of those that a mesh axis runs over, the one named last changes fastest.
Arguments:
- tokens: bfloat16 [4, 1024, 768], P('dp', 'seq'), may hold values from -6 to 6
- lengths: int32 [4], P('dp'), may hold values from 256 to 1024, as said below
- buckets: int32 [4, 12, 1024], P('dp', None, 'seq'), may hold values from 0 to 7
- feature_proj: float32 [64, 256], replicated, may hold values from -5 to 5
- attn_gain: float32 [768], replicated, may hold values from 0.5 to 1.5
- qkv_weight: bfloat16 [768, 2304], replicated, may hold values from -0.21875 to 0.21875
- out_weight: bfloat16 [768, 768], replicated, may hold values from -0.875 to 0.875
- mlp_gain: float32 [768], replicated, may hold values from 0.5 to 1.5
- up_weight: bfloat16 [768, 3072], replicated, may hold values from -0.21875 to 0.21875
- down_weight: bfloat16 [3072, 768], replicated, may hold values from -0.109375 to 0.109375
- cotangent: bfloat16 [4, 1024, 768], P('dp', 'seq'), may hold values from -6 to 6
Outputs:
- layer_out: bfloat16 [4, 1024, 768], P('dp', 'seq')
- grad_tokens: float32 [4, 1024, 768], P('dp', 'seq')
- grad_qkv: float32 [768, 2304], P('seq')
- grad_out: float32 [768, 768], P('seq')
- grad_up: float32 [768, 3072], P('seq')
- grad_down: float32 [3072, 768], P('seq')
- grad_attn_gain: float32 [768], P('seq')
- grad_mlp_gain: float32 [768], P('seq')
Inputs may be any that keep to these rules, and one draw needn't show every extreme that they name: `lengths`: positions of a row below its length hold real tokens, the rest padding; some row of every draw has the full length 1024.
All inputs are finite; a program needn't handle non-finite values.
Results may differ from a plain program's by a relative error of at most 0.012.
The roundings to bfloat16 on the way count: a program that leaves them out, or rounds other values in their place, can miss the bound.
Values may be sent and summed in bfloat16 or wider, within the bound.
No kernel may reach another device: no remote copies, remote signals or barrier semaphores. Data moves between devices by JAX's collectives and lax.ppermute only.
A program may use at most 512 MiB of HBM per device.

v0:
```python
import jax
import jax.numpy as jnp
from jax import lax
from jax.sharding import PartitionSpec as P

SPARSE_BLOCK = 64


HIGH_PRECISION = lax.Precision.HIGHEST
EPS = 1e-05
FLOAT = jnp.float32
HALF = jnp.bfloat16


def from_behind(array, axis, by):
    size = lax.axis_size(axis)
    pairs = [(i, i + by) for i in range(size) if 0 <= i + by < size]
    return lax.ppermute(array, axis, pairs)


def prefix(value, axis, join, neutral, backward):
    count, mine = (lax.axis_size(axis), lax.axis_index(axis))
    pieces = jax.tree.map(lambda part: lax.all_gather(part, axis), value)
    if backward:
        pieces = jax.tree.map(lambda part: part[::-1], pieces)
        mine = count - 1 - mine
    so_far = jax.tree.map(
        lambda part, zero: jnp.full_like(part, 0) + jnp.asarray(zero, part.dtype), value, neutral
    )

    def hop(position, so_far):
        longer = join(so_far, jax.tree.map(lambda part: part[position], pieces))
        return jax.tree.map(lambda new, old: jnp.where(position < mine, new, old), longer, so_far)

    return lax.fori_loop(0, count - 1, hop, so_far)


def shortened(array):

    def short(part):
        return part.astype(jnp.bfloat16) if part.dtype == jnp.float32 else part

    return jax.tree.map(short, array)


def layer_norm(value_rows, gain):
    center = value_rows - jnp.mean(value_rows, -1, keepdims=True)
    spread = jnp.mean(center * center, -1, keepdims=True)
    return center * lax.rsqrt(spread + EPS) * gain


def feature_map(inputs, feature_proj):
    factor = feature_proj.shape[0] ** (-0.25)
    linear = jnp.einsum("rlhd,dm->rlhm", inputs, feature_proj, precision=HIGH_PRECISION) * factor
    square = 0.5 * factor * factor * jnp.sum(inputs * inputs, -1, keepdims=True)
    return jnp.exp(linear - square) * feature_proj.shape[1] ** (-0.5)


def feature_back(inputs, phi_vals, upstream, feature_proj):
    factor = feature_proj.shape[0] ** (-0.25)
    weighted = upstream * phi_vals
    linear = jnp.einsum("rlhm,dm->rlhd", weighted, feature_proj, precision=HIGH_PRECISION) * factor
    return linear - factor * factor * inputs * jnp.sum(weighted, -1, keepdims=True)


def add_pair(first, second):
    return (first[0] + second[0], first[1] + second[1])


def attention_parts(query, keys, tag_window, lengths, feature_proj, first_pos):
    tok_count = query.shape[1]
    key_count = keys.shape[1]
    query_pos = first_pos + jnp.arange(tok_count, dtype=jnp.int32)
    key_pos = first_pos - SPARSE_BLOCK + jnp.arange(key_count, dtype=jnp.int32)
    query_ok = query_pos[None, :] < lengths[:, None]
    key_ok = (key_pos[None, :] >= 0) & (key_pos[None, :] < lengths[:, None])
    own_flag = jnp.arange(key_count) >= SPARSE_BLOCK
    causal = key_pos[None, :] <= query_pos[:, None]
    near_block = key_pos[None, :] // SPARSE_BLOCK >= query_pos[:, None] // SPARSE_BLOCK - 1
    allowed = causal[None, None] & key_ok[:, None, None, :]
    matched = (
        (tag_window[:, :, SPARSE_BLOCK:, None] == tag_window[:, :, None, :])
        & allowed
        & near_block[None, None]
    )
    phi_query = feature_map(query.astype(FLOAT), feature_proj)
    phi_keys = feature_map(keys.astype(FLOAT), feature_proj)
    query_features = phi_query.astype(HALF)
    feat_keys = phi_keys.astype(HALF)
    scores = jnp.einsum(
        "rthd,rjhd->rhtj", query, keys, preferred_element_type=FLOAT
    ) * feature_proj.shape[0] ** (-0.5)
    exponent = jnp.exp(scores)
    approx = jnp.einsum("rthm,rjhm->rhtj", query_features, feat_keys, preferred_element_type=FLOAT)
    blended = jnp.where(
        matched,
        jnp.where(own_flag, exponent, exponent - approx),
        jnp.where(own_flag & allowed, approx, 0.0),
    )
    return (
        query_ok,
        key_ok,
        own_flag,
        allowed,
        matched,
        phi_query,
        phi_keys,
        query_features,
        feat_keys,
        exponent,
        blended,
    )


def per_device(
    tokens,
    lengths,
    buckets,
    feature_proj,
    attn_gain,
    qkv_weight,
    out_weight,
    mlp_gain,
    up_weight,
    down_weight,
    cotangent,
):
    row_count, tok_count, model_width = tokens.shape
    head_count = buckets.shape[1]
    head_size = model_width // head_count
    resid = tokens.astype(FLOAT)
    normed_in = layer_norm(resid, attn_gain).astype(HALF)
    projected = jnp.dot(normed_in, qkv_weight, preferred_element_type=FLOAT).astype(HALF)
    shaped = projected.reshape(row_count, tok_count, 3, head_count, head_size)
    query = shaped[:, :, 0]
    own_keys = shaped[:, :, 1]
    own_values = shaped[:, :, 2]
    tags = buckets.astype(HALF)
    edge_keys, edge_values, edge_tags = from_behind(
        (own_keys[:, -SPARSE_BLOCK:], own_values[:, -SPARSE_BLOCK:], tags[:, :, -SPARSE_BLOCK:]),
        "seq",
        1,
    )
    keys = jnp.concatenate([edge_keys, own_keys], 1)
    value_rows = jnp.concatenate([edge_values, own_values], 1)
    tag_window = jnp.concatenate([edge_tags, tags], 2)
    first_pos = lax.axis_index("seq") * tok_count
    (
        query_ok,
        key_ok,
        own_flag,
        allowed,
        matched,
        phi_query,
        phi_keys,
        query_features,
        feat_keys,
        exponent,
        blended,
    ) = attention_parts(query, keys, tag_window, lengths, feature_proj, first_pos)
    retained_features = jnp.where(
        key_ok[:, SPARSE_BLOCK:, None, None],
        feat_keys[:, SPARSE_BLOCK:],
        jnp.zeros_like(feat_keys[:, SPARSE_BLOCK:]),
    )
    sum_add = jnp.einsum(
        "rthm,rthd->rhmd", retained_features, own_values, preferred_element_type=FLOAT
    )
    norm_add = jnp.sum(retained_features.astype(FLOAT), 1)
    zero_sums = jnp.zeros_like(sum_add)
    zero_norms = jnp.zeros_like(norm_add)
    running_feature_sums, carry_norms = prefix(
        (sum_add, norm_add), "seq", add_pair, (zero_sums, zero_norms), False
    )
    feat_query_f = query_features.astype(FLOAT)
    blended_low = blended.astype(HALF)
    attention_numerator = jnp.einsum(
        "rthm,rhmd->rthd", feat_query_f, running_feature_sums, precision=HIGH_PRECISION
    )
    attention_numerator = attention_numerator + jnp.einsum(
        "rhtj,rjhd->rthd", blended_low, value_rows, preferred_element_type=FLOAT
    )
    denominator = jnp.einsum(
        "rthm,rhm->rth", feat_query_f, carry_norms, precision=HIGH_PRECISION
    ) + jnp.sum(blended, -1).transpose(0, 2, 1)
    den_safe = jnp.where(query_ok[..., None], denominator, 1.0)
    attended = jnp.where(query_ok[..., None, None], attention_numerator / den_safe[..., None], 0.0)
    attended_low = attended.reshape(row_count, tok_count, model_width).astype(HALF)
    mid_resid = resid + jnp.dot(attended_low, out_weight, preferred_element_type=FLOAT)
    normed_mid = layer_norm(mid_resid, mlp_gain).astype(HALF)
    pre_act = jnp.dot(normed_mid, up_weight, preferred_element_type=FLOAT)
    hidden = jax.nn.gelu(pre_act, approximate=True).astype(HALF)
    layer_out = (mid_resid + jnp.dot(hidden, down_weight, preferred_element_type=FLOAT)).astype(
        HALF
    )
    upstream = cotangent.astype(FLOAT)
    grad_down = jnp.einsum("rtf,rtd->fd", hidden, cotangent, preferred_element_type=FLOAT)
    grad_hidden = jnp.einsum("rtd,fd->rtf", cotangent, down_weight, preferred_element_type=FLOAT)
    gelu_vals, gelu_pull = jax.vjp(lambda inner: jax.nn.gelu(inner, approximate=True), pre_act)
    grad_pre = gelu_pull(grad_hidden)[0].astype(HALF)
    grad_up = jnp.einsum("rtd,rtf->df", normed_mid, grad_pre, preferred_element_type=FLOAT)
    grad_normed_mid = jnp.einsum("rtf,df->rtd", grad_pre, up_weight, preferred_element_type=FLOAT)
    mid_vals, mid_pull = jax.vjp(layer_norm, mid_resid, mlp_gain)
    grad_mid_part, grad_mlp_gain = mid_pull(grad_normed_mid)
    grad_mid = upstream + grad_mid_part
    grad_out = jnp.einsum(
        "rtd,rte->de", attended_low.astype(FLOAT), grad_mid, precision=HIGH_PRECISION
    )
    grad_att = jnp.einsum(
        "rte,de->rtd", grad_mid, out_weight.astype(FLOAT), precision=HIGH_PRECISION
    ).astype(HALF)
    grad_att = grad_att.astype(FLOAT).reshape(row_count, tok_count, head_count, head_size)
    grad_numer = jnp.where(query_ok[..., None, None], grad_att / den_safe[..., None], 0.0)
    grad_denom = -jnp.sum(grad_numer * attention_numerator, -1) / den_safe
    grad_feat_query = (
        jnp.einsum("rthd,rhmd->rthm", grad_numer, running_feature_sums, precision=HIGH_PRECISION)
        + grad_denom[..., None] * carry_norms[:, None]
    )
    grad_carry_sums = jnp.einsum(
        "rthm,rthd->rhmd", feat_query_f, grad_numer, precision=HIGH_PRECISION
    )
    grad_carry_norms = jnp.einsum(
        "rthm,rth->rhm", feat_query_f, grad_denom, precision=HIGH_PRECISION
    )
    later_sums, later_norms = prefix(
        (grad_carry_sums, grad_carry_norms), "seq", add_pair, (zero_sums, zero_norms), True
    )
    grad_blend = (
        jnp.einsum(
            "rthd,rjhd->rhtj", grad_numer, value_rows.astype(FLOAT), precision=HIGH_PRECISION
        )
        + grad_denom.transpose(0, 2, 1)[..., None]
    )
    grad_values = jnp.einsum(
        "rhtj,rthd->rjhd", blended_low.astype(FLOAT), grad_numer, precision=HIGH_PRECISION
    )
    grad_expo = jnp.where(matched, grad_blend, 0.0)
    grad_approx = jnp.where(
        matched,
        jnp.where(own_flag, 0.0, -grad_blend),
        jnp.where(own_flag & allowed, grad_blend, 0.0),
    )
    grad_scores = grad_expo * exponent * head_size ** (-0.5)
    grad_query = jnp.einsum(
        "rhtj,rjhd->rthd", grad_scores, keys.astype(FLOAT), precision=HIGH_PRECISION
    )
    grad_keys = jnp.einsum(
        "rhtj,rthd->rjhd", grad_scores, query.astype(FLOAT), precision=HIGH_PRECISION
    )
    grad_feat_query = grad_feat_query + jnp.einsum(
        "rhtj,rjhm->rthm", grad_approx, feat_keys.astype(FLOAT), precision=HIGH_PRECISION
    )
    grad_feat_keys = jnp.einsum(
        "rhtj,rthm->rjhm", grad_approx, feat_query_f, precision=HIGH_PRECISION
    )
    own_mask = key_ok[:, SPARSE_BLOCK:, None, None]
    carry_feat = (
        jnp.einsum(
            "rthd,rhmd->rthm", own_values.astype(FLOAT), later_sums, precision=HIGH_PRECISION
        )
        + later_norms[:, None]
    )
    carry_vals = jnp.einsum(
        "rthm,rhmd->rthd",
        feat_keys[:, SPARSE_BLOCK:].astype(FLOAT),
        later_sums,
        precision=HIGH_PRECISION,
    )
    grad_feat_keys = jnp.concatenate(
        [
            grad_feat_keys[:, :SPARSE_BLOCK],
            grad_feat_keys[:, SPARSE_BLOCK:] + jnp.where(own_mask, carry_feat, 0.0),
        ],
        1,
    )
    grad_values = jnp.concatenate(
        [
            grad_values[:, :SPARSE_BLOCK],
            grad_values[:, SPARSE_BLOCK:] + jnp.where(own_mask, carry_vals, 0.0),
        ],
        1,
    )
    grad_query = grad_query + feature_back(
        query.astype(FLOAT), phi_query, grad_feat_query, feature_proj
    )
    grad_keys = grad_keys + feature_back(keys.astype(FLOAT), phi_keys, grad_feat_keys, feature_proj)
    back_keys, back_values = from_behind(
        (shortened(grad_keys[:, :SPARSE_BLOCK]), shortened(grad_values[:, :SPARSE_BLOCK])),
        "seq",
        -1,
    )
    own_grad_keys = grad_keys[:, SPARSE_BLOCK:]
    own_grad_values = grad_values[:, SPARSE_BLOCK:]
    own_grad_keys = jnp.concatenate(
        [
            own_grad_keys[:, : tok_count - SPARSE_BLOCK],
            own_grad_keys[:, tok_count - SPARSE_BLOCK :] + back_keys,
        ],
        1,
    )
    own_grad_values = jnp.concatenate(
        [
            own_grad_values[:, : tok_count - SPARSE_BLOCK],
            own_grad_values[:, tok_count - SPARSE_BLOCK :] + back_values,
        ],
        1,
    )
    grad_proj = (
        jnp.stack([grad_query, own_grad_keys, own_grad_values], 2)
        .reshape(row_count, tok_count, 3 * model_width)
        .astype(HALF)
    )
    grad_qkv = jnp.einsum("rtd,rte->de", normed_in, grad_proj, preferred_element_type=FLOAT)
    grad_normed_in = jnp.einsum("rte,de->rtd", grad_proj, qkv_weight, preferred_element_type=FLOAT)
    in_vals, in_pull = jax.vjp(layer_norm, resid, attn_gain)
    grad_in_part, grad_attn_gain = in_pull(grad_normed_in)
    grad_tokens = grad_mid + grad_in_part
    shares = (
        lax.psum_scatter(grad_qkv, "seq", scatter_dimension=0, tiled=True),
        lax.psum_scatter(grad_out, "seq", scatter_dimension=0, tiled=True),
        lax.psum_scatter(grad_up, "seq", scatter_dimension=0, tiled=True),
        lax.psum_scatter(grad_down, "seq", scatter_dimension=0, tiled=True),
        lax.psum_scatter(grad_attn_gain, "seq", scatter_dimension=0, tiled=True),
        lax.psum_scatter(grad_mlp_gain, "seq", scatter_dimension=0, tiled=True),
    )
    totals = lax.psum((shares[0], shares[1], shares[2], shares[3], shares[4], shares[5]), "dp")
    return (
        layer_out,
        grad_tokens,
        totals[0],
        totals[1],
        totals[2],
        totals[3],
        totals[4],
        totals[5],
    )


def solution(mesh):
    in_specs = (
        P("dp", "seq", None),
        P("dp"),
        P("dp", None, "seq"),
        P(),
        P(),
        P(),
        P(),
        P(),
        P(),
        P(),
        P("dp", "seq", None),
    )
    out_specs = (
        P("dp", "seq", None),
        P("dp", "seq", None),
        P("seq", None),
        P("seq", None),
        P("seq", None),
        P("seq", None),
        P("seq"),
        P("seq"),
    )
    return jax.shard_map(
        per_device, mesh=mesh, in_specs=in_specs, out_specs=out_specs, check_vma=False
    )
```

profile of v0, /device:TPU:0, one launch (start us, length us, event | category | flops | bytes accessed | tf_op | source)
XLA Modules:
  0.0 683.5 jit_solution(12422036931514061457)
XLA Ops:
  10.6 2.4 convolution_convert_fusion
  13.1 2.1 copy.43
  18.5 3.0 collective-permute-start
  23.5 4.2 fusion
  28.7 2.2 fusion.57
  32.2 6.7 collective-permute-start.2
  40.7 4.5 collective-permute-start.1
  47.0 3.3 fusion.145
  54.5 15.8 %all-gather.4 = f32[8,12,256]{2,1,0:T(8,128)} all-gather(f32[1,12,256]{2,1,0:T(8,128)S(1)} %bitcast.349), channel_id=3, replica_groups=mesh['dp'=4,'seq'=8] {'seq'}, dimensions={0}, use_global_device_ids=true | all-gather | bytes 110592 | tf_op jit(solution)/shard_map/all_gather | solution.py:23
  73.1 2.2 fusion.141
  75.2 27.8 %all-gather.9.cloned.1.call-done = f32[96,256,64]{1,2,0:T(8,128)} async-done(((f32[12,256,64]{1,2,0:T(8,128)}), f32[96,256,64]{1,2,0:T(8,128)}) %all-gather.9.cloned.1.call-update) | async-done | bytes 6291472 | tf_op jit(solution)/shard_map/all_gather | solution.py:23
  103.1 61.3 %while.32 = (s32[]{:T(128)}, f32[1,12,256,64]{3,2,1,0:T(8,128)}, f32[1,12,256]{2,1,0:T(8,128)S(1)}, s32[]{:T(128)}, f32[8,1,12,256,64]{3,4,2,0,1:T(8,128)}, /*index=5*/f32[8,1,12,256]{3,2,1,0:T(8,128)}, s32[]{:T(128)}, s32[]{:T(128)}) while((s32[]{:T(128)}, f32[1,12,256,64]{3,2,1,0:T(8,128)}, f32[1,12,256]{2,1,0:T(8,128)S(1)}, ...), condition=%wide.region_5.6_spmd.clone, body=%wide.region_4.5_spmd.clone.sunk | while | flops 599044 | bytes 5542003 | solution.py:35
  105.1 2.7 copy.85
  107.9 2.8 add_select_fusion.8
  113.5 2.7 copy.85
  116.2 3.3 add_select_fusion.8
  122.3 2.7 copy.85
  125.0 3.3 add_select_fusion.8
  131.1 2.7 copy.85
  133.8 3.3 add_select_fusion.8
  139.9 2.7 copy.85
  142.7 3.3 add_select_fusion.8
  148.7 2.7 copy.85
  151.5 3.3 add_select_fusion.8
  157.6 2.7 copy.85
  160.3 3.3 add_select_fusion.8
  164.4 3.2 fusion.19
  168.3 2.2 select_convert_fusion
  171.3 3.3 fusion.137
  174.6 4.8 fusion.7
  179.4 2.3 fusion.77
  182.7 2.1 fusion.46
  186.7 2.7 fusion.139
  189.5 3.7 fusion.78
  193.7 6.6 fusion.135
  200.4 6.6 fusion.90
  214.2 23.9 %all-gather.5 = f32[8,12,256]{2,1,0:T(8,128)S(1)} all-gather(f32[1,12,256]{2,1,0:T(8,128)S(1)} %bitcast.350), channel_id=5, replica_groups=mesh['dp'=4,'seq'=8] {'seq'}, dimensions={0}, use_global_device_ids=true | all-gather | bytes 110592 | tf_op jit(solution)/shard_map/all_gather | solution.py:23
  240.7 2.2 fusion.59
  243.0 2.2 fusion.147
  245.2 2.7 fusion.36
  252.3 2.9 fusion.41
  257.1 9.8 %copy.52 = f32[8,1,12,256,64]{4,3,2,1,0:T(8,128)} copy(f32[8,1,12,256,64]{3,4,2,0,1:T(8,128)} %bitcast.329) | data formatting | bytes 12582912 | tf_op jit(solution)/shard_map/all_gather | solution.py:23
  266.8 10.8 %rev.6 = f32[8,1,12,256,64]{4,3,2,1,0:T(8,128)} reverse(f32[8,1,12,256,64]{4,3,2,1,0:T(8,128)} %copy.52), dimensions={0} | reverse | bytes 12582912 | tf_op jit(solution)/shard_map/rev | solution.py:25
  277.6 28.1 %while.33 = (s32[]{:T(128)}, f32[1,12,256,64]{3,2,1,0:T(8,128)}, f32[1,12,256]{2,1,0:T(8,128)S(1)}, s32[]{:T(128)}, f32[8,1,12,256,64]{4,3,2,1,0:T(8,128)}, /*index=5*/f32[8,1,12,256]{3,2,1,0:T(8,128)}, s32[]{:T(128)}, s32[]{:T(128)}) while((s32[]{:T(128)}, f32[1,12,256,64]{3,2,1,0:T(8,128)}, f32[1,12,256]{2,1,0:T(8,128)S(1)}, ...), condition=%wide.region_15.16_spmd.clone, body=%wide.region_14.15_spmd.clone.sunk | while | flops 599044 | bytes 2396275 | solution.py:35
  277.6 2.8 add_select_fusion.10
  281.1 3.3 add_select_fusion.10
  285.1 3.3 add_select_fusion.10
  289.1 3.3 add_select_fusion.10
  293.1 3.3 add_select_fusion.10
  297.1 3.2 add_select_fusion.10
  301.1 3.9 add_select_fusion.10
  305.7 3.2 fusion.8
  312.6 3.2 convolution_multiply_fusion.1
  316.0 2.6 fusion.26
  323.3 4.0 fusion.131
  327.5 70.0 %reduce-scatter.9.cloned.1.call-done = f32[96,3072]{1,0:T(8,128)} async-done(((f32[768,3072]{1,0:T(8,128)}), f32[96,3072]{1,0:T(8,128)}) %reduce-scatter.9.cloned.1.call-update) | async-done | bytes 1179664 | tf_op jit(solution)/shard_map/reduce_scatter | solution.py:321
  397.5 99.9 %reduce-scatter.11.cloned.1.call-done = f32[384,768]{1,0:T(8,128)} async-done(((f32[3072,768]{1,0:T(8,128)}), f32[384,768]{1,0:T(8,128)}) %reduce-scatter.11.cloned.1.call-update) | async-done | bytes 1179664 | tf_op jit(solution)/shard_map/reduce_scatter | solution.py:322
  497.3 77.8 %reduce-scatter.5.cloned.1.call-done = f32[96,2304]{1,0:T(8,128)} async-done(((f32[768,2304]{1,0:T(8,128)}), f32[96,2304]{1,0:T(8,128)}) %reduce-scatter.5.cloned.1.call-update) | async-done | bytes 884752 | tf_op jit(solution)/shard_map/reduce_scatter | solution.py:319
  577.0 4.7 fusion.45
  584.0 14.5 %all-reduce.2 = (f32[768]{0:T(1024)}, f32[768]{0:T(1024)}) all-reduce(f32[768]{0:T(1024)S(1)} %get-tuple-element.300, f32[768]{0:T(1024)} %get-tuple-element.298), channel_id=10, replica_groups=mesh['dp'=4,'seq'=8] {'seq'}, use_global_device_ids=true, to_apply=%region_28.29.clone | all-reduce | flops 1536 | bytes 12288
  600.5 10.6 %all-reduce.3 = (f32[96]{0:T(128)}, f32[96]{0:T(128)}) all-reduce(f32[96]{0:T(128)S(1)} %dynamic-slice.1, f32[96]{0:T(128)} %dynamic-slice.3), channel_id=1, replica_groups=mesh['dp'=4,'seq'=8] {'dp'}, use_global_device_ids=true, to_apply=%region_29.30 | all-reduce | flops 192 | bytes 1536 | tf_op jit(solution)/shard_map/psum | solution.py:326
  611.7 2.3 add_add_fusion.2
  614.0 57.5 %all-reduce.7.cloned.1.call-done = (f32[96,2304]{1,0:T(8,128)}, f32[96,768]{1,0:T(8,128)}, f32[96,3072]{1,0:T(8,128)}, f32[384,768]{1,0:T(8,128)}) async-done(((f32[96,2304]{1,0:T(8,128)}, f32[96,768]{1,0:T(8,128)}, f32[96,3072]{1,0:T(8,128)}, f32[384,768]{1,0:T(8,128)}), (f32[96,2304]{1,0:T(8,128)}, f32[96,768]{1,0:T(8,128)}, f32[96,3072]{1,0:T(8,128)}, f32[384,768]{1,0:T(8,128)})) %all-reduce.7.cloned.1.call-update) | async-done | bytes 3538960 | tf_op jit(solution)/shard_map/psum | solution.py:326
  671.5 2.2 copy.109
  (302 shorter events, 83.4 us)
Async XLA Ops:
  7.2 3.5 copy-start
  7.2 95.9 %all-gather.9.cloned.1.call-start = ((), (), s32[]{:S(2)}) async-start(), calls=%async_computation.8 | async-start | bytes 7077888 | tf_op jit(solution)/shard_map/all_gather | solution.py:23
  18.5 3.7 collective-permute-start
  22.2 5.5 copy-start.80
  23.5 4.2 copy-start.53
  27.7 3.2 copy-start.78
  30.9 226.2 %all-gather.11.cloned.1.call-start = ((), (), s32[]{:S(2)}) async-start(), calls=%async_computation.9 | async-start | bytes 7077888 | tf_op jit(solution)/shard_map/all_gather | solution.py:23
  32.2 19.9 %collective-permute-start.2 = (bf16[1,12,64]{2,0,1:T(2,128)(2,1)}, bf16[1,12,64]{2,0,1:T(2,128)(2,1)}, u32[]{:S(2)}, u32[]{:S(2)}) collective-permute-start(bf16[1,12,64]{2,0,1:T(2,128)(2,1)} %slice.81), channel_id=1, source_target_pairs={{0,1},{1,2},{2,3},{3,4},{4,5},{5,6},{6,7},{8,9},{9,10},{10,11},{11... | collective-permute-start | bytes 4616 | tf_op jit(solution)/shard_map/ppermute | solution.py:18
  40.7 127.6 %collective-permute-start.1 = (bf16[1,64,12,64]{1,3,2,0:T(8,128)(2,1)}, bf16[1,64,12,64]{1,3,2,0:T(8,128)(2,1)}, u32[]{:S(2)}, u32[]{:S(2)}) collective-permute-start(bf16[1,64,12,64]{1,3,2,0:T(8,128)(2,1)} %slice.80), channel_id=1, source_target_pairs={{0,1},{1,2},{2,3},{3,4},{4,5},{5,6},{6,7},{8,9},{9,10},{10,11},{11... | collective-permute-start | bytes 294920 | tf_op jit(solution)/shard_map/ppermute | solution.py:18
  52.1 20.9 %copy-start.4 = (bf16[128,12,256]{2,0,1:T(8,128)(2,1)S(1)}, bf16[128,12,256]{2,0,1:T(8,128)(2,1)}, u32[]{:S(2)}) copy-start(bf16[128,12,256]{2,0,1:T(8,128)(2,1)} %get-tuple-element.347) | copy-start | bytes 2359300
  52.1 20.9 %copy-start.22 = (bf16[192,12,256]{2,0,1:T(8,128)(2,1)S(1)}, bf16[192,12,256]{2,0,1:T(8,128)(2,1)}, u32[]{:S(2)}) copy-start(bf16[192,12,256]{2,0,1:T(8,128)(2,1)} %copy-done.21) | copy-start | bytes 3538948
  52.1 20.9 %copy-start.46 = (pred[128,192]{0,1:T(8,128)(4,1)S(1)}, pred[128,192]{0,1:T(8,128)(4,1)}, u32[]{:S(2)}) copy-start(pred[128,192]{0,1:T(8,128)(4,1)} %get-tuple-element.345) | copy-start | bytes 73732
  52.1 20.9 %copy-start.49 = (pred[128,192]{0,1:T(8,128)(4,1)S(1)}, pred[128,192]{0,1:T(8,128)(4,1)}, u32[]{:S(2)}) copy-start(pred[128,192]{0,1:T(8,128)(4,1)} %get-tuple-element.360) | copy-start | bytes 73732
  52.1 20.9 %copy-start.60 = (pred[128,192]{0,1:T(8,128)(4,1)S(1)}, pred[128,192]{0,1:T(8,128)(4,1)}, u32[]{:S(2)}) copy-start(pred[128,192]{0,1:T(8,128)(4,1)} %get-tuple-element.346) | copy-start | bytes 73732
  52.1 20.9 %copy-start.65 = (bf16[1,12,128]{2,1,0:T(8,128)(2,1)S(1)}, bf16[1,12,128]{2,1,0:T(8,128)(2,1)}, u32[]{:S(2)}) copy-start(bf16[1,12,128]{2,1,0:T(8,128)(2,1)} %copy.83) | copy-start | bytes 9220
  52.2 20.9 %copy-start.84 = (pred[192]{0:T(512)(128)(4,1)S(1)}, pred[192]{0:T(512)(128)(4,1)}, u32[]{:S(2)}) copy-start(pred[192]{0:T(512)(128)(4,1)} %copy-done.83) | copy-start | bytes 580
  53.1 18.9 %copy-start.57 = (bf16[1,12,192]{2,1,0:T(8,128)(2,1)}, bf16[1,12,192]{2,1,0:T(8,128)(2,1)S(1)}, u32[]{:S(2)}) copy-start(bf16[1,12,192]{2,1,0:T(8,128)(2,1)S(1)} %copy.82) | copy-start | bytes 13828
  164.3 3.2 copy-start.5
  164.3 3.9 copy-start.69
  164.3 3.9 copy-start.76
  164.3 4.0 copy-start.38
  164.3 4.0 copy-start.89
  171.0 10.7 %copy-start.7 = (f32[1,128,768]{2,1,0:T(8,128)}, f32[1,128,768]{2,1,0:T(8,128)S(1)}, u32[]{:S(2)}) copy-start(f32[1,128,768]{2,1,0:T(8,128)S(1)} %get-tuple-element.354) | copy-start | bytes 1179652
  171.0 10.7 %copy-start.72 = (f32[128]{0:T(128)}, f32[128]{0:T(128)S(1)}, u32[]{:S(2)}) copy-start(f32[128]{0:T(128)S(1)} %broadcast_multiply_fusion.4) | copy-start | bytes 1540
  171.2 10.5 %copy-start.75 = (f32[128]{0:T(128)}, f32[128]{0:T(128)S(1)}, u32[]{:S(2)}) copy-start(f32[128]{0:T(128)S(1)} %fusion.118) | copy-start | bytes 1540
  171.2 3.3 copy-start.32
  171.2 8.2 %slice-start = ((s8[4718592]{0:T(1024)(128)(4,1)}), s8[4194304]{0:T(1024)(128)(4,1)S(1)}, s32[]{:S(2)}) async-start(s8[4718592]{0:T(1024)(128)(4,1)} %bitcast.316), calls=%async_computation.11 | async-start | bytes 8388608
  174.6 4.8 copy-start.17
  174.6 4.8 slice-start.1
  189.5 138.0 %reduce-scatter.7.cloned.1.call-start = ((), (), s32[]{:S(2)}) async-start(), calls=%async_computation.5 | async-start | bytes 2654208 | tf_op jit(solution)/shard_map/reduce_scatter | solution.py:320
  193.3 204.2 %reduce-scatter.9.cloned.1.call-start = ((), (), s32[]{:S(2)}) async-start(), calls=%async_computation.6 | async-start | bytes 10616832 | tf_op jit(solution)/shard_map/reduce_scatter | solution.py:321
  200.3 297.0 %reduce-scatter.11.cloned.1.call-start = ((), (), s32[]{:S(2)}) async-start(), calls=%async_computation.7 | async-start | bytes 10616832 | tf_op jit(solution)/shard_map/reduce_scatter | solution.py:322
  207.0 368.2 %reduce-scatter.5.cloned.1.call-start = ((), (), s32[]{:S(2)}) async-start(), calls=%async_computation.4 | async-start | bytes 7962624 | tf_op jit(solution)/shard_map/reduce_scatter | solution.py:319
  207.0 3.6 copy-start.31
  207.0 3.6 copy-start.64
  207.1 3.6 copy-start.77
  207.1 3.6 copy-start.90
  209.1 29.7 %copy-start.39 = (bf16[1,128,12,64]{1,3,2,0:T(8,128)(2,1)S(1)}, bf16[1,128,12,64]{1,3,2,0:T(8,128)(2,1)}, u32[]{:S(2)}) copy-start(bf16[1,128,12,64]{1,3,2,0:T(8,128)(2,1)} %get-tuple-element.341) | copy-start | bytes 589828
  212.0 28.7 %copy-start.23 = (bf16[192,12,256]{2,0,1:T(8,128)(2,1)S(1)}, bf16[192,12,256]{2,0,1:T(8,128)(2,1)}, u32[]{:S(2)}) copy-start(bf16[192,12,256]{2,0,1:T(8,128)(2,1)} %copy-done.21) | copy-start | bytes 3538948
  212.0 28.7 %copy-start.47 = (pred[128,192]{0,1:T(8,128)(4,1)S(1)}, pred[128,192]{0,1:T(8,128)(4,1)}, u32[]{:S(2)}) copy-start(pred[128,192]{0,1:T(8,128)(4,1)} %get-tuple-element.345) | copy-start | bytes 73732
  212.0 28.7 %copy-start.50 = (pred[128,192]{0,1:T(8,128)(4,1)S(1)}, pred[128,192]{0,1:T(8,128)(4,1)}, u32[]{:S(2)}) copy-start(pred[128,192]{0,1:T(8,128)(4,1)} %get-tuple-element.360) | copy-start | bytes 73732
  212.0 28.7 %copy-start.58 = (bf16[1,12,192]{2,1,0:T(8,128)(2,1)S(1)}, bf16[1,12,192]{2,1,0:T(8,128)(2,1)}, u32[]{:S(2)}) copy-start(bf16[1,12,192]{2,1,0:T(8,128)(2,1)} %copy-done.57) | copy-start | bytes 13828
  212.0 28.7 %copy-start.61 = (pred[128,192]{0,1:T(8,128)(4,1)S(1)}, pred[128,192]{0,1:T(8,128)(4,1)}, u32[]{:S(2)}) copy-start(pred[128,192]{0,1:T(8,128)(4,1)} %get-tuple-element.346) | copy-start | bytes 73732
  212.0 28.7 %copy-start.66 = (bf16[1,12,128]{2,1,0:T(8,128)(2,1)S(1)}, bf16[1,12,128]{2,1,0:T(8,128)(2,1)}, u32[]{:S(2)}) copy-start(bf16[1,12,128]{2,1,0:T(8,128)(2,1)} %copy.83) | copy-start | bytes 9220
  212.0 28.7 %copy-start.85 = (pred[192]{0:T(512)(128)(4,1)S(1)}, pred[192]{0:T(512)(128)(4,1)}, u32[]{:S(2)}) copy-start(pred[192]{0:T(512)(128)(4,1)} %copy-done.83) | copy-start | bytes 580
  212.8 107.4 %collective-permute-start.4 = (bf16[1,64,12,64]{1,3,2,0:T(8,128)(2,1)}, bf16[1,64,12,64]{1,3,2,0:T(8,128)(2,1)}, u32[]{:S(2)}, u32[]{:S(2)}) collective-permute-start(bf16[1,64,12,64]{1,3,2,0:T(8,128)(2,1)} %slice.135), channel_id=1, source_target_pairs={{1,0},{2,1},{3,2},{4,3},{5,4},{6,5},{7,6},{9,8},{10,9},{11,10},{12... | collective-permute-start | bytes 294920 | tf_op jit(solution)/shard_map/ppermute | solution.py:18
  240.7 11.0 %copy-start.14 = (f32[12,128,192]{1,2,0:T(8,128)}, f32[12,128,192]{1,2,0:T(8,128)S(1)}, u32[]{:S(2)}) copy-start(f32[12,128,192]{1,2,0:T(8,128)S(1)} %convolution_add_fusion) | copy-start | bytes 3538948
  266.8 10.8 %copy-start.43 = (f32[1,12,256]{2,1,0:T(8,128)S(1)}, f32[1,12,256]{2,1,0:T(8,128)}, u32[]{:S(2)}) copy-start(f32[1,12,256]{2,1,0:T(8,128)} %custom-call.3) | copy-start | bytes 36868
  305.7 3.3 copy-start.3
  305.7 3.3 copy-start.20
  305.7 3.3 copy-start.54
  312.6 3.3 copy-start.13
  312.6 3.3 copy-start.15
  312.6 3.3 copy-start.42
  312.6 3.3 copy-start.48
  312.6 3.3 copy-start.51
  312.6 3.3 copy-start.59
  312.6 3.3 copy-start.67
  318.7 3.7 copy-start.40
  318.8 3.5 collective-permute-start.3
  327.4 344.1 %all-reduce.7.cloned.1.call-start = ((), (), s32[]{:S(2)}) async-start(), calls=%async_computation.10 | async-start | bytes 7077888 | tf_op jit(solution)/shard_map/psum | solution.py:326
  577.0 4.7 copy-start.10
  577.0 4.7 copy-start.28
  671.5 3.0 copy-start.35
  (41 other events, 63.7 us)
Sparse Core Ops, SparseCore 0:
  31.0 71.9 all-gather.8
  189.6 67.4 all-gather.10
  259.4 34.9 reduce-scatter.6
  296.6 100.8 reduce-scatter.8
  399.6 97.6 reduce-scatter.10
  499.5 75.5 reduce-scatter.4
  578.6 92.8 all-reduce.6
where the time goes:
time: 691 us; the launch traced here: 683 us
  waiting for transfers between devices  336 us (49%)
  matrix products  91.2 us (13%)
  local copies, waits for them, and re-layouts  84.4 us (12%)
  other arithmetic  72.8 us (11%)
  blocking collectives  64.7 us (9%)
  starting transfers between devices  17.8 us (3%)
  between operations  16.9 us (2%)
    reduce_scatter x1, waiting for transfers between devices, per_device(): lax.psum_scatter(grad_down, 'seq', scatter_dimension=0, tiled=True)  99.9 us
    reduce_scatter x1, waiting for transfers between devices, per_device(): lax.psum_scatter(grad_qkv, 'seq', scatter_dimension=0, tiled=True)  77.8 us
    reduce_scatter x1, waiting for transfers between devices, per_device(): lax.psum_scatter(grad_up, 'seq', scatter_dimension=0, tiled=True)  70 us
    psum x1, waiting for transfers between devices, per_device(): lax.psum((shares[0], shares[1], shares[2], shares[3], shares[4], shares[5...  57.5 us
    select_n x28, other arithmetic, hop(): jnp.where(position < mine, new, old)  55.8 us
    all_gather x2, blocking collectives, prefix(): pieces = jax.tree.map(lambda part: lax.all_gather(part, axis), value)  39.6 us
    dynamic_slice x14, local copies, waits for them, and re-layouts, hop(): longer = join(so_far, jax.tree.map(lambda part: part[position], pieces))  33.6 us
    all_gather x2, waiting for transfers between devices, prefix(): pieces = jax.tree.map(lambda part: lax.all_gather(part, axis), value)  29.7 us
  transfers between devices with their start and end apart: 12, of which 7 were waited for; matrix products, arithmetic and copies ran while one was open for 29% of the time, Pallas kernels for 0%

commit v1 on v0

--- a/solution.py
+++ b/solution.py
@@ -1,13 +1,823 @@
+import functools
+
 import jax
 import jax.numpy as jnp
 from jax import lax
+from jax.experimental import pallas as pl
+from jax.experimental.pallas import tpu as pltpu
 from jax.sharding import PartitionSpec as P
 
+EPS = 1e-05
+F32 = jnp.float32
+BF = jnp.bfloat16
+T = 128
+D = 768
+H = 12
+HD = 64
+M = 256
+HM = H * M
+PAIRS = H // 2
+EDGE = 64
+WIN = 640
+ROWS_1 = 120
+ROWS_2 = 96
+ROWS_B = 104
+MIB = 1 << 20
+
+
+def nn(a, b):
+    return lax.dot_general(a, b, (((1,), (0,)), ((), ())), preferred_element_type=F32)
+
+
+def nt(a, b):
+    return lax.dot_general(a, b, (((1,), (1,)), ((), ())), preferred_element_type=F32)
+
+
+def tn(a, b):
+    return lax.dot_general(a, b, (((0,), (0,)), ((), ())), preferred_element_type=F32)
+
+
+def split(a):
+    high = a.astype(BF)
+    return high, (a - high.astype(F32)).astype(BF)
+
+
+def iota(shape, axis):
+    return lax.broadcasted_iota(jnp.int32, shape, axis)
+
+
+def lanes(*parts):
+    return jnp.concatenate(parts, axis=1)
+
+
+def norm_parts(value):
+    center = value - jnp.mean(value, -1, keepdims=True)
+    scale = lax.rsqrt(jnp.mean(center * center, -1, keepdims=True) + EPS)
+    return center * scale, scale
+
+
+def norm_back(unit, scale, gain, upstream):
+    inner = upstream * gain
+    return scale * (
+        inner
+        - jnp.mean(inner, -1, keepdims=True)
+        - unit * jnp.mean(inner * unit, -1, keepdims=True)
+    )
+
+
+def phi_pair(pair, proj):
+    linear = nn(lanes(pair, pair), proj)
+    wide = pair.astype(F32)
+    square = wide * wide
+    first = iota(square.shape, 1) < HD
+    out = []
+    for half in range(2):
+        mine = first if half == 0 else ~first
+        total = jnp.sum(jnp.where(mine, square, 0.0), -1, keepdims=True)
+        out.append(
+            jnp.exp(linear[:, half * M : half * M + M] - total * (0.5 * HD**-0.5)) * M**-0.5
+        )
+    return out
+
+
+def phi_back(pair, grads, phis, proj):
+    weighted = [grad * phi for grad, phi in zip(grads, phis)]
+    joined = lanes(*weighted)
+    high, low = split(joined)
+    linear = nt(high, proj[:128]) + nt(high, proj[128:]) + nt(low, proj[:128])
+    sums = [jnp.sum(part, -1, keepdims=True) for part in weighted]
+    first = iota(pair.shape, 1) < HD
+    return linear - HD**-0.5 * pair.astype(F32) * jnp.where(first, sums[0], sums[1])
+
+
+def pick(first, two):
+    return jnp.where(first, two[0], two[1])
+
+
+def masked(first, half, value):
+    zero = jnp.zeros_like(value)
+    return jnp.where(first, value, zero) if half == 0 else jnp.where(first, zero, value)
+
+
+def columns_to(acc, head, column):
+    return jnp.where(iota(acc.shape, 1) == head, column, acc)
+
+
+def rounded(value):
+    return value.astype(BF)
+
+
+def call(kernel, scalars, args, in_specs, outs, out_specs, grid, scratch=(), flops=0, size=0, vmem=48, aliases=None):
+    return pl.pallas_call(
+        kernel,
+        out_shape=outs,
+        grid_spec=pltpu.PrefetchScalarGridSpec(
+            num_scalar_prefetch=1,
+            grid=grid,
+            in_specs=in_specs,
+            out_specs=out_specs,
+            scratch_shapes=list(scratch),
+        ),
+        input_output_aliases=aliases or {},
+        compiler_params=pltpu.CompilerParams(vmem_limit_bytes=vmem * MIB),
+        cost_estimate=pl.CostEstimate(flops=flops // 1000, bytes_accessed=size // 1000, transcendentals=0),
+    )(scalars, *args)
+
+
+def whole(shape):
+    return pl.BlockSpec(memory_space=pltpu.VMEM)
+
+
+def sds(shape, dtype):
+    return jax.ShapeDtypeStruct(shape, dtype)
+
+
+def projection(feature_proj):
+    scaled = feature_proj * HD ** (-0.25)
+    high, low = split(scaled)
+    none = jnp.zeros((HD, M), BF)
+    return jnp.concatenate([lanes(high, none), lanes(none, high), lanes(low, none), lanes(none, low)], 0)
+
+
+def own_kernel(
+    sc, x_ref, gain_ref, w_ref, feature_ref, g_ref, tag_ref,
+    pay_ref, qkv_ref, phiq_ref, phik_ref, expo_ref, blend_ref, num_ref, den_ref, proj_ref, tags_ref,
+):
+    unit, _ = norm_parts(x_ref[...].astype(F32))
+    normed = unit * gain_ref[...]
+    low = normed.astype(BF)
+    pay_ref[0:D, :] = normed.T.astype(BF)
+    for t in range(6):
+        pay_ref[D + 128 * t : D + 128 * t + 128, :] = g_ref[:, 128 * t : 128 * t + 128]
+    qkv_ref[...] = nn(low, w_ref[...]).astype(BF)
+    rows = jnp.concatenate([tag_ref[...].astype(F32), jnp.zeros((4, T), F32)], 0)
+    tags_ref[...] = rows.astype(BF)
+    cols = rows.T
+    first = iota((T, 128), 1) < HD
+    query_at, key_at = iota((T, T), 0), iota((T, T), 1)
+    allowed = (key_at <= query_at) & (key_at + sc[0] * T < sc[1])
+    dens = jnp.zeros((T, 128), F32)
+    proj = projection(feature_ref[...])
+    proj_ref[...] = proj
+    for p in range(PAIRS):
+        at = slice(128 * p, 128 * p + 128)
+        query, key, value = (
+            qkv_ref[:, part * D + 128 * p : part * D + 128 * p + 128] for part in range(3)
+        )
+        phi_q, phi_k = phi_pair(query, proj), phi_pair(key, proj)
+        nums = []
+        for half in range(2):
+            h = 2 * p + half
+            phiq_ref[:, M * h : M * h + M] = phi_q[half]
+            phik_ref[:, M * h : M * h + M] = phi_k[half]
+            expo = jnp.exp(nt(masked(first, half, query), key) * HD**-0.5)
+            approx = nt(phi_q[half].astype(BF), phi_k[half].astype(BF))
+            matched = allowed & (cols[:, h : h + 1] == rows[h : h + 1, :])
+            blend = jnp.where(matched, expo, jnp.where(allowed, approx, 0.0))
+            expo_ref[h] = jnp.where(matched, expo, 0.0)
+            blend_ref[h] = blend.astype(BF)
+            nums.append(nn(blend.astype(BF), value))
+            dens = columns_to(dens, h, jnp.sum(blend, -1, keepdims=True))
+        num_ref[:, at] = pick(first, nums)
+    den_ref[...] = dens
+
+
+def own_forward(scalars, own, gain, qkv_weight, feature_proj, cotangent, tags):
+    outs = (
+        sds((2 * D, 128), BF), sds((T, 3 * D), BF), sds((T, HM), F32), sds((T, HM), F32),
+        sds((H, T, T), F32), sds((H, T, T), BF), sds((T, D), F32), sds((T, 128), F32),
+        sds((2 * 128, 2 * M), BF), sds((16, T), BF),
+    )
+    args = (own, gain, qkv_weight, feature_proj, cotangent, tags)
+    return call(
+        own_kernel, scalars, args, [whole(a.shape) for a in args], outs,
+        [whole(o.shape) for o in outs], (1,), vmem=6, flops=2_000_000_000, size=9_000_000,
+    )
+
+
+def others_kernel(begin, sc, x_ref, gain_ref, w_ref, proj_ref, *refs):
+    u_ref, v_ref, phi_ref, sums_ref, norms_ref = refs[-5:]
+    slot = pl.program_id(0)
+    span = sc[8 + begin + slot]
+
+    @pl.when(slot == 0)
+    def _():
+        if begin:
+            sums_ref[...], norms_ref[...] = refs[3][...], refs[4][...]
+        else:
+            sums_ref[...] = jnp.zeros_like(sums_ref)
+            norms_ref[...] = jnp.zeros_like(norms_ref)
+
+    unit, _ = norm_parts(x_ref[0].astype(F32))
+    low = (unit * gain_ref[...]).astype(BF)
+    earlier = span < sc[0]
+    offset = pl.multiple_of(jnp.where(earlier, D, 0), D)
+    u_ref[0] = nn(low, w_ref[:, pl.ds(offset, D)]).astype(BF)
+    proj = proj_ref[...]
+    for p in range(PAIRS):
+        phis = phi_pair(u_ref[0, :, 128 * p : 128 * p + 128], proj)
+        for half in range(2):
+            h = 2 * p + half
+            phi_ref[0, :, M * h : M * h + M] = phis[half].astype(BF)
+
+    @pl.when(earlier)
+    def _():
+        value = nn(low, w_ref[:, 2 * D : 3 * D])
+        v_ref[0] = value.astype(BF)
+        valid = iota((D, T), 1) + span * T < sc[1]
+        turned = jnp.where(valid, value.T, 0.0).astype(BF)
+        for h in range(H):
+            sums_ref[HD * h : HD * h + HD, :] += nn(
+                turned[HD * h : HD * h + HD, :], phi_ref[0, :, M * h : M * h + M]
+            )
+        ones = jnp.where(iota((8, T), 1) + span * T < sc[1], 1.0, 0.0).astype(BF)
+        norms_ref[...] += nn(ones, phi_ref[0])
+
+    @pl.when(~earlier)
+    def _():
+        v_ref[0] = jnp.zeros((T, D), BF)
+
+
+def others_forward(scalars, begin, pieces, gain, qkv_weight, proj, so_far=()):
+    count, spans = pieces.shape[0], 7
+    outs = (
+        sds((spans, T, D), BF), sds((spans, T, D), BF), sds((spans, T, HM), BF),
+        sds((D, M), F32), sds((8, HM), F32),
+    )
+    step = lambda i, sc: (begin + i, 0, 0)
+    specs = [pl.BlockSpec((1, T, D), lambda i, sc: (i, 0, 0))]
+    specs += [whole(a.shape) for a in (gain, qkv_weight, proj)]
+    aliases = {}
+    if so_far:
+        specs += [pl.BlockSpec(memory_space=pl.ANY)] * 3 + [whole(a.shape) for a in so_far[3:]]
+        aliases = {5: 0, 6: 1, 7: 2}
+    return call(
+        functools.partial(others_kernel, begin), scalars, (pieces, gain, qkv_weight, proj, *so_far), specs,
+        outs,
+        [pl.BlockSpec((1, T, D), step), pl.BlockSpec((1, T, D), step), pl.BlockSpec((1, T, HM), step),
+         whole((D, M)), whole((8, HM))],
+        (count,), vmem=8, flops=count * 600_000_000, size=count * 1_400_000 + 3_500_000, aliases=aliases,
+    )
+
+
+def own_cols(tags_ref):
+    return tags_ref[...].astype(F32).T.astype(BF)
+
+
+def middle_kernel(
+    sc, x_ref, qkv_ref, phiq_ref, sums_ref, norms_ref, numl_ref, denl_ref, tags_ref, tags_prev,
+    up_prev, vp_prev, phi_prev, gain_ref, wo_ref, wup_ref, wdown_ref, g_ref,
+    a0, a1, a2, a3, b0, b1, b2, b3, out_ref, dmid_ref, dn_low_ref, dn_ref, dd_ref, expo_ref, blend_ref, gain_out,
+    mid_s, nm_s, acc_s, dnm_s, num_s, den_s, turn_s,
+):
+    first_pay, second_pay = (a0, a1, a2, a3), (b0, b1, b2, b3)
+    step = pl.program_id(0)
+    me = sc[6]
+    first = iota((T, 128), 1) < HD
+    valid = iota((T, 1), 0) + sc[0] * T < sc[1]
+
+    @pl.when(step == 0)
+    def _():
+        own = tags_ref[...].astype(F32).T
+        prev = tags_prev[...].astype(F32)
+        prev_tag = [prev[h : h + 1, EDGE:T] for h in range(H)]
+        edge_first = iota((EDGE, 128), 1) < HD
+        edge_ok = (sc[4] > 0) & (iota((EDGE, EDGE), 1) + (sc[0] * T - EDGE) < sc[1])
+        dens = denl_ref[...]
+        zeros = jnp.zeros((EDGE, 128), F32)
+        for p in range(PAIRS):
+            at = slice(128 * p, 128 * p + 128)
+            high, lowp = split(sums_ref[at, :])
+            query = qkv_ref[0:EDGE, at]
+            key, value = up_prev[0, :, at], vp_prev[0, :, at]
+            nums = []
+            for half in range(2):
+                h = 2 * p + half
+                hm = slice(M * h, M * h + M)
+                phi_q = phiq_ref[:, hm].astype(BF)
+                total = nt(phi_q, high) + nt(phi_q, lowp)
+                den = jnp.sum(phi_q.astype(F32) * norms_ref[0:1, hm], -1, keepdims=True)
+                expo = jnp.exp(nt(masked(edge_first, half, query), key) * HD**-0.5)
+                approx = nt(phi_q[0:EDGE], phi_prev[0, :, hm])
+                matched = edge_ok & (own[0:EDGE, h : h + 1] == prev_tag[h])
+                blend = jnp.where(matched, expo - approx, 0.0)
+                expo_ref[h] = jnp.where(matched, expo, 0.0)
+                blend_ref[h] = blend.astype(BF)
+                total = total + jnp.concatenate([nn(blend.astype(BF), value), zeros], 0)
+                den = den + jnp.concatenate(
+                    [jnp.sum(blend, -1, keepdims=True), jnp.zeros((EDGE, 1), F32)], 0
+                )
+                nums.append(total)
+                dens = jnp.where(iota(dens.shape, 1) == h, dens + den, dens)
+            num_s[:, at] = numl_ref[:, at] + pick(first, nums)
+        dens = jnp.where(valid, dens, 1.0)
+        den_s[...] = dens
+        for p in range(PAIRS):
+            at = slice(128 * p, 128 * p + 128)
+            den = jnp.where(first, dens[:, 2 * p : 2 * p + 1], dens[:, 2 * p + 1 : 2 * p + 2])
+            mid_s[:, at] = jnp.where(valid, num_s[:, at] / den, 0.0)
+        attended = mid_s[...].astype(BF)
+        turned = mid_s[...].T.astype(BF)
+        for k in range(4):
+            upper = (me ^ k) >= 2
+            for s in range(8):
+                first_pay[k][768 + 48 * s : 768 + 48 * s + 48, :] = jnp.where(
+                    upper, turned[96 * s + 48 : 96 * s + 96, :], turned[96 * s : 96 * s + 48, :]
+                )
+        mid = x_ref[...].astype(F32) + nn(attended, wo_ref[...])
+        mid_s[...] = mid
+        unit, _ = norm_parts(mid)
+        normed = unit * gain_ref[...]
+        nm_s[...] = normed.astype(BF)
+        turned = normed.T.astype(BF)
+        for k in range(4):
+            second_pay[k][0:D, :] = turned
+        acc_s[...] = jnp.zeros_like(acc_s)
+        dnm_s[...] = jnp.zeros_like(dnm_s)
+
+    pre = nn(nm_s[...], wup_ref[...])
+    grad_hidden = nt(g_ref[...], wdown_ref[...])
+    root = (2.0 / jnp.pi) ** 0.5
+    inner = root * (pre + 0.044715 * (pre * pre * pre))
+    tanh = jnp.tanh(inner)
+    half_up = 0.5 * (1.0 + tanh)
+    hidden = pre * half_up
+    slope = half_up + 0.5 * pre * (1.0 - tanh * tanh) * (root * (1.0 + 3 * 0.044715 * (pre * pre)))
+    grad_pre = (grad_hidden * slope).astype(BF)
+    hidden_low = hidden.astype(BF)
+    acc_s[...] += nn(hidden_low, wdown_ref[...])
+    dnm_s[...] += nt(grad_pre, wup_ref[...])
+    turn_s[...] = hidden.T.astype(BF)
+    for k in range(4):
+        for s in range(2):
+            base = pl.multiple_of(192 * step + 96 * s, 96)
+            begin = pl.multiple_of(384 * s + 96 * (k ^ me), 96)
+            first_pay[k][pl.ds(base, 96), :] = turn_s[pl.ds(begin, 96), :]
+
+        @pl.when((step ^ me) == k)
+        def _():
+            for t in range(6):
+                second_pay[k][D + 128 * t : D + 128 * t + 128, :] = grad_pre[:, 128 * t : 128 * t + 128]
+
+    @pl.when(step == 3)
+    def _():
+        mid = mid_s[...]
+        out_ref[...] = (mid + acc_s[...]).astype(BF)
+        unit, scale = norm_parts(mid)
+        grad = dnm_s[...]
+        gain_out[...] = jnp.broadcast_to(jnp.sum(grad * unit, 0, keepdims=True), (8, D))
+        dmid = g_ref[...].astype(F32) + norm_back(unit, scale, gain_ref[...], grad)
+        dmid_ref[...] = dmid
+        high, low = split(dmid)
+        for k in range(4):
+            right = ((me ^ k) & 1) > 0
+            for t in range(3):
+                first_pay[k][1152 + 128 * t : 1152 + 128 * t + 128, :] = jnp.where(
+                    right, high[:, 384 + 128 * t : 512 + 128 * t], high[:, 128 * t : 128 * t + 128]
+                )
+        datt = (nt(high, wo_ref[...]) + nt(low, wo_ref[...])).astype(BF).astype(F32)
+        dens = den_s[...]
+        ddens = jnp.zeros((T, 128), F32)
+        for p in range(PAIRS):
+            at = slice(128 * p, 128 * p + 128)
+            den = jnp.where(first, dens[:, 2 * p : 2 * p + 1], dens[:, 2 * p + 1 : 2 * p + 2])
+            dnum = jnp.where(valid, datt[:, at] / den, 0.0)
+            dn_ref[:, at] = dnum
+            dn_low_ref[:, at] = dnum.astype(BF)
+            prod = dnum * num_s[:, at]
+            for half in range(2):
+                h = 2 * p + half
+                total = jnp.sum(masked(first, half, prod), -1, keepdims=True)
+                ddens = columns_to(ddens, h, -total / dens[:, h : h + 1])
+        dd_ref[...] = ddens
+        dn_low_ref[:, D : D + 16] = ddens[:, 0:16].astype(BF)
+        dn_low_ref[:, D + 16 : D + 32] = own_cols(tags_ref)
+        dn_low_ref[:, D + 32 : D + 128] = jnp.zeros((T, 96), BF)
+
+
+def middle(scalars, own, qkv, phi_q, sums, norms, num, den, tags, tags_prev, others, gain, wo, wup, wdown, cot):
+    u, v, phi = others
+    prev = lambda i, sc: (sc[2], 1, 0)
+    outs = tuple([sds((2 * D, 128), BF)] * 8) + (
+        sds((T, D), BF), sds((T, D), F32), sds((T, D + 128), BF),
+        sds((T, D), F32), sds((T, 128), F32), sds((H, EDGE, EDGE), F32), sds((H, EDGE, EDGE), BF),
+        sds((8, D), F32),
+    )
+    args = (own, qkv, phi_q, sums, norms, num, den, tags, tags_prev, u, v, phi, gain, wo, wup, wdown, cot)
+    specs = [whole(a.shape) for a in args[:9]] + [
+        pl.BlockSpec((1, EDGE, D), prev), pl.BlockSpec((1, EDGE, D), prev),
+        pl.BlockSpec((1, EDGE, HM), prev),
+        whole(gain.shape), whole(wo.shape),
+        pl.BlockSpec((D, D), lambda i, sc: (0, i)), pl.BlockSpec((D, D), lambda i, sc: (i, 0)),
+        whole(cot.shape),
+    ]
+    scratch = [
+        pltpu.VMEM((T, D), F32), pltpu.VMEM((T, D), BF), pltpu.VMEM((T, D), F32),
+        pltpu.VMEM((T, D), F32), pltpu.VMEM((T, D), F32), pltpu.VMEM((T, 128), F32),
+        pltpu.VMEM((D, T), BF),
+    ]
+    return call(
+        middle_kernel, scalars, args, specs, outs, [whole(o.shape) for o in outs], (4,), scratch,
+        vmem=12, flops=3_500_000_000, size=20_000_000,
+    )
+
+
+def own_back_kernel(
+    sc, tags_ref, tags_prev, qkv_ref, phiq_ref, phik_ref, proj_ref, expo_ref, blend_ref, dn_ref, dd_ref,
+    sums_ref, norms_ref, up_prev, vp_prev, phi_prev, expo_e, blend_e,
+    dq_ref, dk_ref, dv_ref, dphi_ref,
+):
+    rows = tags_ref[...].astype(F32)
+    cols = rows.T
+    first = iota((T, 128), 1) < HD
+    query_at, key_at = iota((T, T), 0), iota((T, T), 1)
+    allowed = (key_at <= query_at) & (key_at + sc[0] * T < sc[1])
+    prev_tag = tags_prev[...].astype(F32)
+    edge_first = iota((EDGE, 128), 1) < HD
+    edge_ok = (sc[4] > 0) & (iota((EDGE, EDGE), 1) + (sc[0] * T - EDGE) < sc[1])
+    proj = proj_ref[...]
+    for p in range(PAIRS):
+        at = slice(128 * p, 128 * p + 128)
+        query, key, value = (
+            qkv_ref[:, part * D + 128 * p : part * D + 128 * p + 128] for part in range(3)
+        )
+        key_e, value_e = up_prev[0, :, at], vp_prev[0, :, at]
+        high, low = split(dn_ref[:, at])
+        both = lanes(high, low)
+        s_high, s_low = split(sums_ref[at, :])
+        grads, phis, dqs, dks, dvs = [], [], [], [], []
+        for half in range(2):
+            h = 2 * p + half
+            hm = slice(M * h, M * h + M)
+            dden = dd_ref[:, h : h + 1]
+            mine = lanes(masked(first, half, high), masked(first, half, low))
+            phi_q, phi_k = phiq_ref[:, hm], phik_ref[:, hm]
+            dw = nt(mine, lanes(value, value)) + dden
+            matched = cols[:, h : h + 1] == rows[h : h + 1, :]
+            ds = (dw * expo_ref[h] * HD**-0.5).astype(BF)
+            da = jnp.where(allowed & ~matched, dw, 0.0).astype(BF)
+            dq = nn(ds, key)
+            dks.append(tn(ds, query))
+            dv = tn(blend_ref[h], both)
+            dvs.append(dv[:, 0:128] + dv[:, 128:256])
+            dphi = nn(da, phi_k.astype(BF)) + dden * norms_ref[0:1, hm]
+            dphi = dphi + nn(mine, jnp.concatenate([s_high, s_high], 0))
+            dphi = dphi + nn(mine[:, 0:128], s_low)
+            dphi_ref[:, hm] = tn(da, phi_q.astype(BF))
+            edge = nt(mine[0:EDGE], lanes(value_e, value_e)) + dden[0:EDGE]
+            matched_e = edge_ok & (cols[0:EDGE, h : h + 1] == prev_tag[h : h + 1, EDGE:T])
+            ds_e = (edge * expo_e[h] * HD**-0.5).astype(BF)
+            da_e = jnp.where(matched_e, -edge, 0.0).astype(BF)
+            dqs.append(dq + jnp.concatenate([nn(ds_e, key_e), jnp.zeros((EDGE, 128), F32)], 0))
+            grads.append(
+                dphi + jnp.concatenate([nn(da_e, phi_prev[0, :, hm]), jnp.zeros((EDGE, M), F32)], 0)
+            )
+            phis.append(phi_q)
+        dq_ref[:, at] = (pick(first, dqs) + phi_back(query, grads, phis, proj)).astype(BF)
+        dk_ref[:, at] = pick(first, dks)
+        dv_ref[:, at] = pick(first, dvs)
+
+
+def own_back(scalars, tags, tags_prev, qkv, phi_q, phi_k, proj, expo, blend, dnum, dden, sums, norms, others, expo_e, blend_e):
+    u, v, phi = others
+    prev = lambda i, sc: (sc[2], 1, 0)
+    args = (
+        tags, tags_prev, qkv, phi_q, phi_k, proj, expo, blend, dnum, dden, sums, norms, u, v, phi, expo_e,
+        blend_e,
+    )
+    specs = [whole(a.shape) for a in args[:12]] + [
+        pl.BlockSpec((1, EDGE, D), prev), pl.BlockSpec((1, EDGE, D), prev),
+        pl.BlockSpec((1, EDGE, HM), prev),
+        whole(expo_e.shape), whole(blend_e.shape),
+    ]
+    outs = (sds((T, D), BF), sds((T, D), F32), sds((T, D), F32), sds((T, HM), F32))
+    return call(
+        own_back_kernel, scalars, args, specs, outs, [whole(o.shape) for o in outs], (1,),
+        vmem=8, flops=3_000_000_000, size=9_000_000,
+    )
+
+
+def last_kernel(
+    sc, dn_slot, phi_slot, x_ref, tags_ref, qkv_ref, phik_ref, proj_ref, dq_ref, dk_ref, dv_ref, dphi_ref,
+    u_next, phi_next, dn_next, dmid_ref, gain_ref, w_ref, gmlp_ref,
+    a0, a1, a2, a3, grad_ref, sums_s, norms_s, dqkv_s,
+):
+    slot = pl.program_id(0)
+    span = sc[24 + slot]
+
+    @pl.when(slot == 0)
+    def _():
+        sums_s[...] = jnp.zeros_like(sums_s)
+        norms_s[...] = jnp.zeros_like(norms_s)
+
+    @pl.when(span > sc[0])
+    def _():
+        turned = dn_slot[0].astype(F32).T.astype(BF)
+        for h in range(H):
+            hm = slice(M * h, M * h + M)
+            sums_s[HD * h : HD * h + HD, :] += nn(turned[HD * h : HD * h + HD, :], phi_slot[0, :, hm])
+        norms_s[...] += nn(turned[D : D + 16, :], phi_slot[0])
+
+    @pl.when(slot == pl.num_programs(0) - 1)
+    def _():
+        me = sc[6]
+        rows = tags_ref[...].astype(F32)
+        next_cols = dn_next[0, :, D + 16 : D + 32].astype(F32)
+        first = iota((T, 128), 1) < HD
+        edge_first = iota((EDGE, 128), 1) < HD
+        valid = iota((T, 1), 0) + sc[0] * T < sc[1]
+        edge_ok = (sc[5] > 0) & (iota((EDGE, EDGE), 1) + (sc[0] * T + EDGE) < sc[1])
+        proj = proj_ref[...]
+        ddn = dn_next[0, :, D : D + 128].astype(F32)
+        dqkv_s[:, 0:D] = dq_ref[...]
+        for p in range(PAIRS):
+            at = slice(128 * p, 128 * p + 128)
+            key, value = (qkv_ref[:, part * D + 128 * p : part * D + 128 * p + 128] for part in (1, 2))
+            high, low = split(sums_s[at, :])
+            query_n, dnum_n = u_next[0, :, at], dn_next[0, :, at]
+            grads, phis, dks, dvs = [], [], [], []
+            for half in range(2):
+                h = 2 * p + half
+                hm = slice(M * h, M * h + M)
+                phi_k = phik_ref[:, hm]
+                phi_kb = phi_k.astype(BF)
+                mine = masked(first, half, value)
+                carry = nn(mine, high) + nn(mine, low) + norms_s[h : h + 1, hm]
+                dv = nt(phi_kb, high) + nt(phi_kb, low)
+                q_h, d_h = masked(edge_first, half, query_n), masked(edge_first, half, dnum_n)
+                phi_n = phi_next[0, :, hm]
+                expo = jnp.exp(nt(q_h, key[EDGE:]) * HD**-0.5)
+                approx = nt(phi_n, phi_kb[EDGE:])
+                matched = edge_ok & (next_cols[0:EDGE, h : h + 1] == rows[h : h + 1, EDGE:128])
+                blend = jnp.where(matched, expo - approx, 0.0).astype(BF)
+                dw = nt(d_h, value[EDGE:]) + ddn[:, h : h + 1]
+                ds = jnp.where(matched, dw * expo * HD**-0.5, 0.0).astype(BF)
+                da = jnp.where(matched, -dw, 0.0).astype(BF)
+                none = jnp.zeros((EDGE, 128), F32)
+                dks.append(jnp.concatenate([none, tn(ds, query_n)], 0))
+                dvs.append(jnp.where(valid, dv, 0.0) + jnp.concatenate([none, tn(blend, dnum_n)], 0))
+                grads.append(
+                    dphi_ref[:, hm] + jnp.where(valid, carry, 0.0)
+                    + jnp.concatenate([jnp.zeros((EDGE, M), F32), tn(da, phi_n)], 0)
+                )
+                phis.append(phi_k)
+            dqkv_s[:, D + 128 * p : D + 128 * p + 128] = (
+                dk_ref[:, at] + pick(first, dks) + phi_back(key, grads, phis, proj)
+            ).astype(BF)
+            dqkv_s[:, 2 * D + 128 * p : 2 * D + 128 * p + 128] = (dv_ref[:, at] + pick(first, dvs)).astype(BF)
+        grad = nt(dqkv_s[...], w_ref[...])
+        unit, scale = norm_parts(x_ref[...].astype(F32))
+        grad_ref[...] = dmid_ref[...] + norm_back(unit, scale, gain_ref[...], grad)
+        attn = jnp.sum(grad * unit, 0, keepdims=True)
+        mlp = gmlp_ref[0:1, :]
+        row = iota((8, WIN), 0)
+        gains = jnp.zeros((8, WIN), F32)
+        tail = jnp.zeros((1, 2 * WIN - D), F32)
+        for at, part in enumerate((attn, mlp)):
+            gains = jnp.where(row == 2 * at, part[:, 0:WIN], gains)
+            gains = jnp.where(row == 2 * at + 1, lanes(part[:, WIN:D], tail), gains)
+        for k, pay_ref in enumerate((a0, a1, a2, a3)):
+            mate = me ^ k
+            begin = pl.multiple_of(jnp.where(mate == 0, 0, 128 * (4 * mate + 1)), 128)
+            pay_ref[0:T, :] = dqkv_s[:, pl.ds(begin, WIN)]
+            pay_ref[T : T + 8, :] = gains.astype(BF)
+
+
+def last(scalars, dn_pieces, others, own, tags, qkv, phi_k, proj, dq, dk, dv, dphi, dmid, gain, qkv_weight, gmlp):
+    u, v, phi = others
+    count = dn_pieces.shape[0] - 1
+    follow = lambda i, sc: (sc[3], 0, 0)
+    args = (
+        dn_pieces, phi, own, tags, qkv, phi_k, proj, dq, dk, dv, dphi, u, phi, dn_pieces, dmid, gain,
+        qkv_weight, gmlp,
+    )
+    specs = [
+        pl.BlockSpec((1, T, D + 128), lambda i, sc: (i + 1, 0, 0)),
+        pl.BlockSpec((1, T, HM), lambda i, sc: (sc[40 + i], 0, 0)),
+    ]
+    specs += [whole(a.shape) for a in args[2:11]]
+    specs += [
+        pl.BlockSpec((1, EDGE, D), follow), pl.BlockSpec((1, EDGE, HM), follow),
+        pl.BlockSpec((1, EDGE, D + 128), lambda i, sc: (sc[7], 0, 0)),
+    ] + [whole(a.shape) for a in args[14:]]
+    outs = tuple([sds((T + 8, WIN), BF)] * 4) + (sds((T, D), F32),)
+    return call(
+        last_kernel, scalars, args, specs, outs, [whole(o.shape) for o in outs], (count,),
+        [pltpu.VMEM((D, M), F32), pltpu.VMEM((16, HM), F32), pltpu.VMEM((T, 3 * D), BF)],
+        vmem=10, flops=3_000_000_000, size=count * 1_000_000 + 10_000_000,
+    )
+
+
+def reverse3(at):
+    return ((at & 1) << 2) | (at & 2) | (at >> 2)
+
+
+def place(sc, chunk_of, keep_ref, send_ref):
+    for r in range(8):
+        block = reverse3(r) ^ sc[0]
+        target = keep_ref.at[r] if r < 4 else send_ref.at[r - 4]
+        chunk_of(block, target)
+
+
+def joined(parts, begin, size):
+    return lanes(*[part[begin : begin + size, :] for part in parts])
+
+
+def tiles(part, begin, count):
+    return lanes(*[part[begin + 128 * t : begin + 128 * t + 128, :] for t in range(count)])
+
+
+def product(lefts, rights):
+    first = nn(lanes(lefts[0], lefts[1]), jnp.concatenate(rights[0:2], 0))
+    return first + nn(lanes(lefts[2], lefts[3]), jnp.concatenate(rights[2:4], 0))
+
+
+def first_kernel(sc, p0, p1, p2, p3, e0, e1, e2, e3, keep_ref, send_ref, down_s, out_s):
+    parts = (p0, p1, p2, p3)
+    cots = [e[D : 2 * D, :] for e in (e0, e1, e2, e3)]
+    down_s[...] = product([a[0:768, :] for a in parts], [tiles(a, 0, 6) for a in cots])
+    out_s[...] = product([a[768:1152, :] for a in parts], [tiles(a, 1152, 3) for a in parts])
+
+    def chunk(block, target):
+        at = pl.multiple_of(96 * block, 96)
+        target[0:96, :] = down_s[pl.ds(at, 96), :].astype(target.dtype)
+        at = pl.multiple_of(48 * block, 48)
+        target[96:120, 0:384] = out_s[pl.ds(at, 24), :].astype(target.dtype)
+        at = pl.multiple_of(48 * block + 24, 24)
+        target[96:120, 384:768] = out_s[pl.ds(at, 24), :].astype(target.dtype)
+
+    place(sc, chunk, keep_ref, send_ref)
+
+
+def second_kernel(sc, p0, p1, p2, p3, keep_ref, send_ref, up_s):
+    parts = (p0, p1, p2, p3)
+    up_s[...] = product([a[0:768, :] for a in parts], [tiles(a, 768, 6) for a in parts])
+
+    def chunk(block, target):
+        at = pl.multiple_of(96 * block, 96)
+        target[...] = up_s[pl.ds(at, 96), :].astype(target.dtype)
+
+    place(sc, chunk, keep_ref, send_ref)
+
+
+def third_kernel(sc, p0, p1, p2, p3, e0, e1, e2, e3, keep_ref, send_ref, res_s):
+    parts = (p0, p1, p2, p3)
+    res_s[...] = product([e[0:D, :] for e in (e0, e1, e2, e3)], [a[0:T, :] for a in parts])
+    gains = sum(a[T : T + 8, :].astype(F32) for a in parts)
+
+    def chunk(block, target):
+        at = pl.multiple_of(96 * block, 96)
+        target[0:96, :] = res_s[pl.ds(at, 96), :].astype(target.dtype)
+        target[96:104, :] = gains.astype(target.dtype)
+
+    place(sc, chunk, keep_ref, send_ref)
+
+
+def weights(kernel, scalars, args, rows, width, scratch):
+    outs = (sds((4, rows, width), F32), sds((4, rows, width), BF))
+    return call(
+        kernel, scalars, args, [whole(a.shape) for a in args], outs, [whole(o.shape) for o in outs], (1,),
+        [pltpu.VMEM(shape, F32) for shape in scratch], vmem=8, flops=600_000_000, size=5_000_000,
+    )
+
+
+def spread_kernel(fill, sc, *refs):
+    for k, part in enumerate(refs[0:4]):
+        quarter = sc[6] ^ k
+        for j in range(4):
+            @pl.when(quarter == j)
+            def _():
+                fill(j, part, *refs[4:])
+
+
+def spread(fill, scalars, parts, shapes):
+    outs = tuple(sds(shape, F32) for shape in shapes)
+    return call(
+        functools.partial(spread_kernel, fill), scalars, parts, [whole(a.shape) for a in parts], outs,
+        [whole(o.shape) for o in outs], (1,), vmem=4, size=2_000_000,
+    )
+
+
+def fill_first(j, part, down_ref, out_ref):
+    down_ref[96 * j : 96 * j + 96, :] = part[0:96, :].astype(F32)
+    row, col = 48 * (j >> 1), 384 * (j & 1)
+    out_ref[row : row + 24, col : col + 384] = part[96:120, 0:384].astype(F32)
+    out_ref[row + 24 : row + 48, col : col + 384] = part[96:120, 384:768].astype(F32)
+
+
+def fill_second(j, part, up_ref):
+    up_ref[:, 768 * j : 768 * j + 768] = part[...].astype(F32)
+
+
+def fill_third(j, part, qkv_ref, gain_ref):
+    skip = 128 if j >= 2 else 0
+    begin = 0 if j == 0 else 128 * (4 * j + 1)
+    qkv_ref[:, begin + skip : begin + WIN] = part[0:96, skip:WIN].astype(F32)
+    if j == 0:
+        gain_ref[...] = part[96:104, :].astype(F32)
+
+
+def swap(array, axis, bits):
+    size = lax.axis_size(axis)
+    return lax.ppermute(array, axis, [(i, i ^ bits) for i in range(size)])
+
+
+def reduce_spans(keep, send, steps=(1, 2, 4)):
+    for bits in steps:
+        total = keep + swap(send, "seq", bits).astype(F32)
+        half = total.shape[0] // 2
+        if half:
+            keep, send = total[:half], total[half:].astype(BF)
+    return total[0].astype(BF)
+
+
+def per_device_fast(
+    tokens, lengths, buckets, feature_proj, attn_gain, qkv_weight, out_weight, mlp_gain, up_weight,
+    down_weight, cotangent,
+):
+    seq, row = lax.axis_index("seq"), lax.axis_index("dp")
+    spans = lax.axis_size("seq")
+    token_order, grad_order = (1, 2, 3, 4, 6, 5, 7), (2, 4, 6, 1, 3, 5, 7)
+    before, after = seq ^ jnp.maximum(seq - 1, 0), seq ^ jnp.minimum(seq + 1, spans - 1)
+    scalars = jnp.stack(
+        [
+            seq, lengths[0], jnp.maximum(before - 1, 0), jnp.maximum(after - 1, 0),
+            seq > 0, seq < spans - 1, row,
+            jnp.where(after == 7, 7, jnp.where(after == 3, 5, 4)),
+            *[seq ^ k for k in token_order], *[0] * 9,
+            *[seq ^ k for k in grad_order], *[0] * 9,
+            *[token_order.index(k) for k in grad_order],
+        ]
+    ).astype(jnp.int32)
+    own, cot = tokens[0], cotangent[0]
+    gain_in, gain_mid = attn_gain[None], mlp_gain[None]
+
+    near, far_a, far_b, mate = (swap(own, "seq", bits) for bits in (2, 4, 6, 1))
+    early, qkv, phi_q, phi_k, expo, blend, num, den, proj, tags = own_forward(
+        scalars, own, gain_in, qkv_weight, feature_proj, cot, buckets[0]
+    )
+    near, early = lax.optimization_barrier((near, early))
+    early_1, early_2 = swap(early, "dp", 1), swap(early, "dp", 2)
+    tags_prev = from_behind(tags, "seq", 1)
+    some = others_forward(
+        scalars, 0, jnp.stack([mate, near, swap(near, "seq", 1)]), gain_in, qkv_weight, proj
+    )
+    far, some, late = lax.optimization_barrier((jnp.stack([far_a, far_b]), some, (early, early_1, early_2)))
+    early_3 = swap(late[0], "dp", 3)
+    u, v, phi, sums, norms = others_forward(
+        scalars, 3, jnp.concatenate([far, swap(far, "seq", 1)], 0), gain_in, qkv_weight, proj, some
+    )
+    others = (u, v, phi)
+    sums, early = lax.optimization_barrier((sums, (early, early_1, early_2, early_3)))
+    results = middle(
+        scalars, own, qkv, phi_q, sums, norms, num, den, tags, tags_prev, others, gain_mid, out_weight,
+        up_weight, down_weight, cot,
+    )
+    pay_1, pay_2 = results[0:4], results[4:8]
+    layer_out, dmid, dn_low, dnum, dden, expo_e, blend_e, gmlp = results[8:]
+    dn_far = [swap(dn_low, "seq", bits) for bits in (2, 4, 6)]
+    parts_1 = [pay_1[0], swap(pay_1[1], "dp", 1), swap(pay_1[2], "dp", 2)]
+    dq, dk, dv, dphi = own_back(
+        scalars, tags, tags_prev, qkv, phi_q, phi_k, proj, expo, blend, dnum, dden, sums, norms, others,
+        expo_e, blend_e,
+    )
+    dn_half, parts_1, last_1, dk = lax.optimization_barrier(
+        (jnp.stack([dn_low, *dn_far]), parts_1, pay_1[3], dk)
+    )
+    parts_1.append(swap(last_1, "dp", 3))
+    dn_pieces = jnp.concatenate([dn_half, swap(dn_half, "seq", 1)], 0)
+    parts_1, pay_2 = lax.optimization_barrier((parts_1, pay_2))
+    parts_2 = [pay_2[0]] + [swap(pay_2[k], "dp", k) for k in (1, 2, 3)]
+    keep, send = weights(first_kernel, scalars, (*parts_1, *early), ROWS_1, D, [(D, D), (384, 384)])
+    total_1 = keep + swap(send, "seq", 1).astype(F32)
+    total_1, dn_pieces = lax.optimization_barrier((total_1, dn_pieces))
+    *pay_3, grad_tokens = last(
+        scalars, dn_pieces, others, own, tags, qkv, phi_k, proj, dq, dk, dv, dphi, dmid, gain_in,
+        qkv_weight, gmlp,
+    )
+    pay_3, parts_2 = lax.optimization_barrier((pay_3, parts_2))
+    share_1 = reduce_spans(total_1[0:2], total_1[2:4].astype(BF), (2, 4))
+    parts_3 = [pay_3[0]] + [swap(pay_3[k], "dp", k) for k in (1, 2, 3)]
+    share_2 = reduce_spans(*weights(second_kernel, scalars, parts_2, ROWS_2, D, [(D, D)]))
+    share_3 = reduce_spans(*weights(third_kernel, scalars, (*parts_3, *early), ROWS_B, WIN, [(D, WIN)]))
+
+    def everywhere(share):
+        return [share] + [swap(share, "dp", k) for k in (1, 2, 3)]
+
+    down, out = spread(fill_first, scalars, everywhere(share_1), [(384, D), (96, D)])
+    (up,) = spread(fill_second, scalars, everywhere(share_2), [(96, 4 * D)])
+    grad_qkv, gains = spread(fill_third, scalars, everywhere(share_3), [(96, 3 * D), (8, WIN)])
+    gains = gains[0:4].reshape(2, 2 * WIN)[:, 0:D]
+    mine = lax.dynamic_slice_in_dim(gains, seq * 96, 96, 1)
+    return (
+        layer_out[None], grad_tokens[None], grad_qkv, out, up, down, mine[0], mine[1],
+    )
+
+
 SPARSE_BLOCK = 64
 
 
 HIGH_PRECISION = lax.Precision.HIGHEST
-EPS = 1e-05
 FLOAT = jnp.float32
 HALF = jnp.bfloat16
 
@@ -360,6 +1170,8 @@
         P("seq"),
         P("seq"),
     )
+    shape = dict(mesh.shape)
+    fast = shape == {"dp": 4, "seq": 8}
     return jax.shard_map(
-        per_device, mesh=mesh, in_specs=in_specs, out_specs=out_specs, check_vma=False
-    )
+        per_device_fast if fast else per_device, mesh=mesh, in_specs=in_specs, out_specs=out_specs, check_vma=False
+    )

time: 691 us -> 174 us (0.25); the launches traced: 683 us -> 174 us
  waiting for transfers between devices: 336 us -> 58.2 us
  matrix products: 91.2 us -> 0 us
  local copies, waits for them, and re-layouts: 84.4 us -> 6.11 us
  other arithmetic: 72.8 us -> 1.18 us
  blocking collectives: 64.7 us -> 0 us
  Pallas kernels: 0 us -> 53.2 us
  starting transfers between devices: 17.8 us -> 53.4 us
  between operations: 16.9 us -> 1.78 us
    reduce_scatter x4 -> x0, waiting for transfers between devices: 248 us -> none  [the longest x1 99.9 us: per_device(): lax.psum_scatter(grad_down, 'seq', scatter_dimension=0, tiled=True)]
    dot_general x33 -> x0, matrix products: 91.2 us -> none  [the longest x2 7.42 us: feature_map(): jnp.einsum('rlhd,dm->rlhm', inputs, feature_proj, precision=HIGH_PRECISION)]
    ppermute x0 -> x40, waiting for transfers between devices: none -> 58.2 us  [swap(): return lax.ppermute(array, axis, [(i, i ^ bits) for i in range(size)])]
    psum x1 -> x0, waiting for transfers between devices: 57.5 us -> none  [per_device(): lax.psum((shares[0], shares[1], shares[2], shares[3], shares[4], shares[5...]
    select_n x29 -> x0, other arithmetic: 55.8 us -> none  [the longest x28 55.8 us: hop(): jnp.where(position < mine, new, old)]
    pallas_call x0 -> x12, Pallas kernels: none -> 53.2 us  [call(): pl.pallas_call(kernel, out_shape=outs, grid_spec=pltpu.PrefetchScalarGrid...]
    ppermute x0 -> x40, starting transfers between devices: none -> 51.1 us  [swap(): return lax.ppermute(array, axis, [(i, i ^ bits) for i in range(size)])]
    all_gather x2 -> x0, blocking collectives: 39.6 us -> none  [prefix(): pieces = jax.tree.map(lambda part: lax.all_gather(part, axis), value)]
  transfers between devices with their start and end apart: 12 -> 41, of which waited for: 7 -> 17; matrix products, arithmetic and copies ran while one was open for 29% -> 2% of each run, Pallas kernels for 0% -> 22%
where the time goes in v1:
time: 174 us
  waiting for transfers between devices  58.2 us (33%)
  starting transfers between devices  53.4 us (31%)
  Pallas kernels  53.2 us (31%)
  local copies, waits for them, and re-layouts  6.11 us (4%)
  between operations  1.78 us (1%)
    ppermute x40, waiting for transfers between devices, swap(): return lax.ppermute(array, axis, [(i, i ^ bits) for i in range(size)])  58.2 us
    pallas_call x12, Pallas kernels, call(): pl.pallas_call(kernel, out_shape=outs, grid_spec=pltpu.PrefetchScalarGrid...  53.2 us
    ppermute x40, starting transfers between devices, swap(): return lax.ppermute(array, axis, [(i, i ^ bits) for i in range(size)])  51.1 us
    unnamed x23, local copies, waits for them, and re-layouts  4.51 us
  transfers between devices with their start and end apart: 41, of which 17 were waited for; matrix products, arithmetic and copies ran while one was open for 2% of the time, Pallas kernels for 22%

profile of v1, /device:TPU:0, one launch (start us, length us, event | category | flops | bytes accessed | tf_op | source)
XLA Modules:
  0.0 173.8 jit_solution(10508876574733384479)
XLA Ops:
  0.6 3.1 %collective-permute-start.3 = (bf16[128,768]{1,0:T(8,128)(2,1)}, bf16[128,768]{1,0:T(8,128)(2,1)S(1)}, u32[]{:S(2)}, u32[]{:S(2)}) collective-permute-start(bf16[128,768]{1,0:T(8,128)(2,1)} %bitcast.14.x_ref), channel_id=1, source_target_pairs={{0,2},{1,3},{2,0},{3,1},{4,6},{5,7},{6,4},{7,5},{8,10},{9,11},{10,... | collective-permute-start | bytes 589832 | tf_op jit(solution)/shard_map/ppermute | solution.py:722
  3.7 2.6 %collective-permute-start = (bf16[128,768]{1,0:T(8,128)(2,1)}, bf16[128,768]{1,0:T(8,128)(2,1)S(1)}, u32[]{:S(2)}, u32[]{:S(2)}) collective-permute-start(bf16[128,768]{1,0:T(8,128)(2,1)} %bitcast.14.x_ref), channel_id=1, source_target_pairs={{0,4},{1,5},{2,6},{3,7},{4,0},{5,1},{6,2},{7,3},{8,12},{9,13},{10,... | collective-permute-start | bytes 589832 | tf_op jit(solution)/shard_map/ppermute | solution.py:722
  7.0 0.7 broadcast_in_dim.12.gain_ref
  7.7 0.7 copy.24
  8.5 2.0 %copy-done = bf16[768,2304]{1,0:T(8,128)(2,1)S(1)} copy-done((bf16[768,2304]{1,0:T(8,128)(2,1)S(1)}, bf16[768,2304]{1,0:T(8,128)(2,1)}, u32[]{:S(2)}) %copy-start) | copy-done | bytes 3538968
  10.5 0.9 copy-done.3
  11.4 0.8 copy-done.5
  12.2 5.9 %shard_map.170 = (bf16[1536,128]{1,0:T(8,128)(2,1)S(1)}, bf16[128,2304]{1,0:T(8,128)(2,1)S(1)}, f32[128,3072]{1,0:T(8,128)S(1)}, f32[128,3072]{1,0:T(8,128)S(1)}...) custom-call(s32[47]{0:T(128)S(1)} %stack.110.sc, ...), custom_call_target="tpu_custom_call" | custom-call | flops 2000000 | bytes 9000 | tf_op jit(solution)/shard_map/pallas_call | solution.py:111
  18.1 1.8 %collective-permute-start.5 = (bf16[1536,128]{1,0:T(8,128)(2,1)S(1)}, bf16[1536,128]{1,0:T(8,128)(2,1)S(1)}, u32[]{:S(2)}, u32[]{:S(2)}) collective-permute-start(bf16[1536,128]{1,0:T(8,128)(2,1)S(1)} %get-tuple-element.154.e0), channel_id=1, source_target_pairs={{0,8},{8,0},{16,24},{24,16},{1,9},{9,1},{17,25},{25,17},{2,10},{10... | collective-permute-start | bytes 1179656 | tf_op jit(solution)/shard_map/ppermute | solution.py:722
  19.9 1.5 collective-permute-start.6
  21.4 0.5 collective-permute-start.4
  22.0 1.3 collective-permute-done.2
  23.4 3.3 %shard_map.171 = (bf16[7,128,768]{2,1,0:T(8,128)(2,1)S(1)}, bf16[7,128,768]{2,1,0:T(8,128)(2,1)S(1)}, bf16[7,128,3072]{2,1,0:T(8,128)(2,1)S(1)}, f32[768,256]{1,0:T(8,128)S(1)}, f32[8,3072]{1,0:T(8,128)S(1)}) custom-call(s32[47]{0:T(128)S(1)} %stack.110.sc, bf16[3,128,768]{2,1,0:T(8,128)(2,1)S(1)} %pad_maximum_fusion.3.x_ref, ...), custom_call_target="tpu_custom_call" | custom-call | flops 1800000 | bytes 7700 | tf_op jit(solution)/shard_map/pallas_call | solution.py:111
  26.7 1.8 %collective-permute-done.5.e1 = bf16[1536,128]{1,0:T(8,128)(2,1)S(1)} collective-permute-done((bf16[1536,128]{1,0:T(8,128)(2,1)S(1)}, bf16[1536,128]{1,0:T(8,128)(2,1)S(1)}, u32[]{:S(2)}, u32[]{:S(2)}) %collective-permute-start.5) | collective-permute-done | bytes 393248 | tf_op jit(solution)/shard_map/ppermute | solution.py:722
  28.5 1.2 collective-permute-done.6.e2
  29.7 1.5 collective-permute-start.8
  31.2 2.3 %collective-permute-start.9 = (bf16[16,128]{1,0:T(8,128)(2,1)S(1)}, bf16[16,128]{1,0:T(8,128)(2,1)S(1)}, u32[]{:S(2)}, u32[]{:S(2)}) collective-permute-start(bf16[16,128]{1,0:T(8,128)(2,1)S(1)} %get-tuple-element.124.tags_ref), channel_id=1, source_target_pairs={{0,1},{1,2},{2,3},{3,4},{4,5},{5,6},{6,7},{8,9},{9,10},{10,11},{11... | collective-permute-start | bytes 12296 | tf_op jit(solution)/shard_map/ppermute | solution.py:828
  33.7 4.2 %shard_map.172 = (bf16[7,128,768]{2,1,0:T(8,128)(2,1)S(1)}, bf16[7,128,768]{2,1,0:T(8,128)(2,1)S(1)}, bf16[7,128,3072]{2,1,0:T(8,128)(2,1)S(1)}, f32[768,256]{1,0:T(8,128)S(1)}, f32[8,3072]{1,0:T(8,128)S(1)}) custom-call(s32[47]{0:T(128)S(1)} %stack.110.sc, ...), custom_call_target="tpu_custom_call", output_to_operand_aliasing={{0}: (5, {}), {1}: (6, {}), {2}: (7, {})} | custom-call | flops 2400000 | bytes 9100 | tf_op jit(solution)/shard_map/pallas_call | solution.py:111
  37.9 4.2 %collective-permute-done.8.e3 = bf16[1536,128]{1,0:T(8,128)(2,1)S(1)} collective-permute-done((bf16[1536,128]{1,0:T(8,128)(2,1)S(1)}, bf16[1536,128]{1,0:T(8,128)(2,1)S(1)}, u32[]{:S(2)}, u32[]{:S(2)}) %collective-permute-start.8) | collective-permute-done | bytes 393248 | tf_op jit(solution)/shard_map/ppermute | solution.py:722
  42.2 12.6 %shard_map.173 = (bf16[1536,128]{1,0:T(8,128)(2,1)S(1)}, bf16[1536,128]{1,0:T(8,128)(2,1)S(1)}, bf16[1536,128]{1,0:T(8,128)(2,1)S(1)}, bf16[1536,128]{1,0:T(8,12...) custom-call(s32[47]{0:T(128)S(1)} %stack.110.sc, ...), custom_call_target="tpu_custom_call" | custom-call | flops 3500000 | bytes 20000 | tf_op jit(solution)/shard_map/pallas_call | solution.py:111
  54.8 0.5 collective-permute-start.13
  55.3 1.5 collective-permute-start.14
  56.9 0.6 collective-permute-start.10
  57.5 3.5 %collective-permute-start.11 = (bf16[128,896]{1,0:T(8,128)(2,1)S(1)}, bf16[128,896]{1,0:T(8,128)(2,1)S(1)}, u32[]{:S(2)}, u32[]{:S(2)}) collective-permute-start(bf16[128,896]{1,0:T(8,128)(2,1)S(1)} %get-tuple-element.129), channel_id=1, source_target_pairs={{0,4},{1,5},{2,6},{3,7},{4,0},{5,1},{6,2},{7,3},{8,12},{9,13},{10,... | collective-permute-start | bytes 688136 | tf_op jit(solution)/shard_map/ppermute | solution.py:722
  61.0 0.3 collective-permute-start.12
  61.2 6.4 %shard_map.174 = (bf16[128,768]{1,0:T(8,128)(2,1)S(1)}, f32[128,768]{1,0:T(8,128)S(1)}, f32[128,768]{1,0:T(8,128)S(1)}, f32[128,3072]{1,0:T(8,128)S(1)}) custom-call(s32[47]{0:T(128)S(1)} %stack.110.sc, bf16[16,128]{1,0:T(8,128)(2,1)S(1)} %get-tuple-element.124.tags_ref, bf16[16,128]{1,0:T(8,128)(2,1)S(1)} %collective-permute-done.9.tags_prev, ...), custom_call_target="tpu_custom_call" | custom-call | flops 3000000 | bytes 9000 | tf_op jit(solution)/shard_map/pallas_call | solution.py:111
  67.6 9.7 %collective-permute-done.11 = bf16[128,896]{1,0:T(8,128)(2,1)S(1)} collective-permute-done((bf16[128,896]{1,0:T(8,128)(2,1)S(1)}, bf16[128,896]{1,0:T(8,128)(2,1)S(1)}, u32[]{:S(2)}, u32[]{:S(2)}) %collective-permute-start.11) | collective-permute-done | bytes 229408 | tf_op jit(solution)/shard_map/ppermute | solution.py:722
  77.5 1.5 collective-permute-start.15
  79.0 7.5 %collective-permute-done.15.p3 = bf16[1536,128]{1,0:T(8,128)(2,1)S(1)} collective-permute-done((bf16[1536,128]{1,0:T(8,128)(2,1)S(1)}, bf16[1536,128]{1,0:T(8,128)(2,1)S(1)}, u32[]{:S(2)}, u32[]{:S(2)}) %collective-permute-start.15) | collective-permute-done | bytes 393248 | tf_op jit(solution)/shard_map/ppermute | solution.py:722
  86.5 1.7 shard_map.175
  88.3 1.5 collective-permute-start.18
  89.7 1.3 collective-permute-start.19
  91.0 1.4 collective-permute-start.20
  92.8 4.7 %collective-permute-start.30 = (bf16[2,120,768]{2,1,0:T(8,128)(2,1)S(1)}, bf16[2,120,768]{2,1,0:T(8,128)(2,1)S(1)}, u32[]{:S(2)}, u32[]{:S(2)}) collective-permute-start(bf16[2,120,768]{2,1,0:T(8,128)(2,1)S(1)} %slice.108), channel_id=1, source_target_pairs={{0,2},{1,3},{2,0},{3,1},{4,6},{5,7},{6,4},{7,5},{8,10},{9,11},{10,... | collective-permute-start | bytes 1105928 | tf_op jit(solution)/shard_map/ppermute | solution.py:722
  97.5 11.1 %shard_map.176 = (bf16[136,640]{1,0:T(8,128)(2,1)S(1)}, bf16[136,640]{1,0:T(8,128)(2,1)S(1)}, bf16[136,640]{1,0:T(8,128)(2,1)S(1)}, bf16[136,640]{1,0:T(8,128)(2,1)S(1)}, f32[128,768]{1,0:T(8,128)}) custom-call(s32[47]{0:T(128)S(1)} %stack.110.sc, bf16[8,128,896]{2,1,0:T(8,128)(2,1)S(1)} %pad_maximum_fusion.dn_slot.dn_next, ...), custom_call_target="tpu_custom_call" | custom-call | flops 3000000 | bytes 17000 | tf_op jit(solution)/shard_map/pallas_call | solution.py:111
  108.5 1.7 collective-permute-done.20.p3
  110.2 1.4 shard_map.180
  111.8 0.6 collective-permute-start.21
  112.4 1.7 %collective-permute-start.22 = (bf16[136,640]{1,0:T(8,128)(2,1)S(1)}, bf16[136,640]{1,0:T(8,128)(2,1)S(1)}, u32[]{:S(2)}, u32[]{:S(2)}) collective-permute-start(bf16[136,640]{1,0:T(8,128)(2,1)S(1)} %get-tuple-element.179), channel_id=1, source_target_pairs={{0,16},{8,24},{16,0},{24,8},{1,17},{9,25},{17,1},{25,9},{2,18},{10... | collective-permute-start | bytes 522248 | tf_op jit(solution)/shard_map/ppermute | solution.py:722
  114.2 1.2 collective-permute-start.23
  115.3 3.7 %collective-permute-done.21.p1 = bf16[136,640]{1,0:T(8,128)(2,1)S(1)} collective-permute-done((bf16[136,640]{1,0:T(8,128)(2,1)S(1)}, bf16[136,640]{1,0:T(8,128)(2,1)S(1)}, u32[]{:S(2)}, u32[]{:S(2)}) %collective-permute-start.21) | collective-permute-done | bytes 174112 | tf_op jit(solution)/shard_map/ppermute | solution.py:722
  119.1 3.6 %collective-permute-done.22.p2 = bf16[136,640]{1,0:T(8,128)(2,1)S(1)} collective-permute-done((bf16[136,640]{1,0:T(8,128)(2,1)S(1)}, bf16[136,640]{1,0:T(8,128)(2,1)S(1)}, u32[]{:S(2)}, u32[]{:S(2)}) %collective-permute-start.22) | collective-permute-done | bytes 174112 | tf_op jit(solution)/shard_map/ppermute | solution.py:722
  122.6 1.5 shard_map.177
  124.3 6.6 %collective-permute-start.31 = (bf16[1,120,768]{2,1,0:T(8,128)(2,1)S(1)}, bf16[1,120,768]{2,1,0:T(8,128)(2,1)S(1)}, u32[]{:S(2)}, u32[]{:S(2)}) collective-permute-start(bf16[1,120,768]{2,1,0:T(8,128)(2,1)S(1)} %slice.111), channel_id=1, source_target_pairs={{0,4},{1,5},{2,6},{3,7},{4,0},{5,1},{6,2},{7,3},{8,12},{9,13},{10,... | collective-permute-start | bytes 552968 | tf_op jit(solution)/shard_map/ppermute | solution.py:722
  131.3 2.1 %collective-permute-start.25 = (bf16[2,104,640]{2,1,0:T(8,128)(2,1)S(1)}, bf16[2,104,640]{2,1,0:T(8,128)(2,1)S(1)}, u32[]{:S(2)}, u32[]{:S(2)}) collective-permute-start(bf16[2,104,640]{2,1,0:T(8,128)(2,1)S(1)} %slice.110), channel_id=1, source_target_pairs={{0,2},{1,3},{2,0},{3,1},{4,6},{5,7},{6,4},{7,5},{8,10},{9,11},{10,... | collective-permute-start | bytes 798728 | tf_op jit(solution)/shard_map/ppermute | solution.py:722
  133.4 6.8 %collective-permute-done.31 = bf16[1,120,768]{2,1,0:T(8,128)(2,1)S(1)} collective-permute-done((bf16[1,120,768]{2,1,0:T(8,128)(2,1)S(1)}, bf16[1,120,768]{2,1,0:T(8,128)(2,1)S(1)}, u32[]{:S(2)}, u32[]{:S(2)}) %collective-permute-start.31) | collective-permute-done | bytes 184352 | tf_op jit(solution)/shard_map/ppermute | solution.py:722
  140.3 1.5 collective-permute-start.32
  141.8 0.6 collective-permute-start.33
  142.4 1.5 collective-permute-start.34
  143.8 0.8 collective-permute-done.36
  144.9 6.3 %collective-permute-done.25 = bf16[2,104,640]{2,1,0:T(8,128)(2,1)S(1)} collective-permute-done((bf16[2,104,640]{2,1,0:T(8,128)(2,1)S(1)}, bf16[2,104,640]{2,1,0:T(8,128)(2,1)S(1)}, u32[]{:S(2)}, u32[]{:S(2)}) %collective-permute-start.25) | collective-permute-done | bytes 266272 | tf_op jit(solution)/shard_map/ppermute | solution.py:722
  151.3 4.9 %collective-permute-done.37 = bf16[1,96,768]{2,1,0:T(8,128)(2,1)S(1)} collective-permute-done((bf16[1,96,768]{2,1,0:T(8,128)(2,1)S(1)}, bf16[1,96,768]{2,1,0:T(8,128)(2,1)S(1)}, u32[]{:S(2)}, u32[]{:S(2)}) %collective-permute-start.37) | collective-permute-done | bytes 147488 | tf_op jit(solution)/shard_map/ppermute | solution.py:722
  156.3 2.1 %collective-permute-start.39 = (bf16[96,768]{1,0:T(8,128)(2,1)S(1)}, bf16[96,768]{1,0:T(8,128)(2,1)S(1)}, u32[]{:S(2)}, u32[]{:S(2)}) collective-permute-start(bf16[96,768]{1,0:T(8,128)(2,1)S(1)} %fusion.4.refs_0_), channel_id=1, source_target_pairs={{0,16},{8,24},{16,0},{24,8},{1,17},{9,25},{17,1},{25,9},{2,18},{10... | collective-permute-start | bytes 442376 | tf_op jit(solution)/shard_map/ppermute | solution.py:722
  158.4 0.7 collective-permute-done.26
  159.1 1.5 collective-permute-start.40
  160.6 1.8 %collective-permute-start.27 = (bf16[104,640]{1,0:T(8,128)(2,1)S(1)}, bf16[104,640]{1,0:T(8,128)(2,1)S(1)}, u32[]{:S(2)}, u32[]{:S(2)}) collective-permute-start(bf16[104,640]{1,0:T(8,128)(2,1)S(1)} %fusion.5.refs_0_), channel_id=1, source_target_pairs={{0,8},{8,0},{16,24},{24,16},{1,9},{9,1},{17,25},{25,17},{2,10},{10... | collective-permute-start | bytes 399368 | tf_op jit(solution)/shard_map/ppermute | solution.py:722
  162.7 1.5 collective-permute-start.29
  164.1 1.8 %shard_map.179 = (f32[384,768]{1,0:T(8,128)}, f32[96,768]{1,0:T(8,128)}) custom-call(s32[47]{0:T(128)S(1)} %stack.110.sc, bf16[120,768]{1,0:T(8,128)(2,1)S(1)} %fusion.3.refs_0_, bf16[120,768]{1,0:T(8,128)(2,1)S(1)} %collective-permute-done.32.refs_1_, bf16[120,768]{1,0:T(8,128)(2,1)S(1)} %collective-permute-done.33.refs_2_, ...), custom_call_target="tpu_custom_call" | custom-call | bytes 2000 | tf_op jit(solution)/shard_map/pallas_call | solution.py:111
  165.9 0.7 collective-permute-done.40.refs_3_
  166.6 1.7 shard_map.181
  168.4 1.5 collective-permute-done.27.refs_1_
  169.9 1.7 collective-permute-done.29.refs_3_
  171.6 1.6 shard_map.178
  173.3 0.5 slice_bitcast_fusion
  (84 shorter events, 2.5 us)
Async XLA Ops:
  0.6 17.5 %collective-permute-start.3 = (bf16[128,768]{1,0:T(8,128)(2,1)}, bf16[128,768]{1,0:T(8,128)(2,1)S(1)}, u32[]{:S(2)}, u32[]{:S(2)}) collective-permute-start(bf16[128,768]{1,0:T(8,128)(2,1)} %bitcast.14.x_ref), channel_id=1, source_target_pairs={{0,2},{1,3},{2,0},{3,1},{4,6},{5,7},{6,4},{7,5},{8,10},{9,11},{10,... | collective-permute-start | bytes 589832 | tf_op jit(solution)/shard_map/ppermute | solution.py:722
  3.7 17.7 %collective-permute-start = (bf16[128,768]{1,0:T(8,128)(2,1)}, bf16[128,768]{1,0:T(8,128)(2,1)S(1)}, u32[]{:S(2)}, u32[]{:S(2)}) collective-permute-start(bf16[128,768]{1,0:T(8,128)(2,1)} %bitcast.14.x_ref), channel_id=1, source_target_pairs={{0,4},{1,5},{2,6},{3,7},{4,0},{5,1},{6,2},{7,3},{8,12},{9,13},{10,... | collective-permute-start | bytes 589832 | tf_op jit(solution)/shard_map/ppermute | solution.py:722
  6.3 15.6 %collective-permute-start.1 = (bf16[128,768]{1,0:T(8,128)(2,1)}, bf16[128,768]{1,0:T(8,128)(2,1)S(1)}, u32[]{:S(2)}, u32[]{:S(2)}) collective-permute-start(bf16[128,768]{1,0:T(8,128)(2,1)} %bitcast.14.x_ref), channel_id=1, source_target_pairs={{0,6},{1,7},{2,4},{3,5},{4,2},{5,3},{6,0},{7,1},{8,14},{9,15},{10,... | collective-permute-start | bytes 589832 | tf_op jit(solution)/shard_map/ppermute | solution.py:722
  8.5 2.0 %copy-start = (bf16[768,2304]{1,0:T(8,128)(2,1)S(1)}, bf16[768,2304]{1,0:T(8,128)(2,1)}, u32[]{:S(2)}) copy-start(bf16[768,2304]{1,0:T(8,128)(2,1)} %w_ref.7) | copy-start | bytes 10616836
  10.5 0.9 copy-start.3
  11.4 0.8 copy-start.5
  12.2 11.1 %copy-start.1 = (bf16[768,2304]{1,0:T(8,128)(2,1)S(1)}, bf16[768,2304]{1,0:T(8,128)(2,1)}, u32[]{:S(2)}) copy-start(bf16[768,2304]{1,0:T(8,128)(2,1)} %w_ref.7) | copy-start | bytes 10616836
  18.1 10.4 %collective-permute-start.5 = (bf16[1536,128]{1,0:T(8,128)(2,1)S(1)}, bf16[1536,128]{1,0:T(8,128)(2,1)S(1)}, u32[]{:S(2)}, u32[]{:S(2)}) collective-permute-start(bf16[1536,128]{1,0:T(8,128)(2,1)S(1)} %get-tuple-element.154.e0), channel_id=1, source_target_pairs={{0,8},{8,0},{16,24},{24,16},{1,9},{9,1},{17,25},{25,17},{2,10},{10... | collective-permute-start | bytes 1179656 | tf_op jit(solution)/shard_map/ppermute | solution.py:722
  19.9 9.8 %collective-permute-start.6 = (bf16[1536,128]{1,0:T(8,128)(2,1)S(1)}, bf16[1536,128]{1,0:T(8,128)(2,1)S(1)}, u32[]{:S(2)}, u32[]{:S(2)}) collective-permute-start(bf16[1536,128]{1,0:T(8,128)(2,1)S(1)} %get-tuple-element.154.e0), channel_id=1, source_target_pairs={{0,16},{8,24},{16,0},{24,8},{1,17},{9,25},{17,1},{25,9},{2,18},{10... | collective-permute-start | bytes 1179656 | tf_op jit(solution)/shard_map/ppermute | solution.py:722
  21.4 1.9 %collective-permute-start.2 = (bf16[128,768]{1,0:T(8,128)(2,1)}, bf16[128,768]{1,0:T(8,128)(2,1)S(1)}, u32[]{:S(2)}, u32[]{:S(2)}) collective-permute-start(bf16[128,768]{1,0:T(8,128)(2,1)} %bitcast.14.x_ref), channel_id=1, source_target_pairs={{0,1},{1,0},{2,3},{3,2},{4,5},{5,4},{6,7},{7,6},{8,9},{9,8},{10,11... | collective-permute-start | bytes 589832 | tf_op jit(solution)/shard_map/ppermute | solution.py:722
  21.4 1.9 %collective-permute-start.4 = (bf16[128,768]{1,0:T(8,128)(2,1)S(1)}, bf16[128,768]{1,0:T(8,128)(2,1)S(1)}, u32[]{:S(2)}, u32[]{:S(2)}) collective-permute-start(bf16[128,768]{1,0:T(8,128)(2,1)S(1)} %collective-permute-done.3), channel_id=1, source_target_pairs={{0,1},{1,0},{2,3},{3,2},{4,5},{5,4},{6,7},{7,6},{8,9},{9,8},{10,11... | collective-permute-start | bytes 589832 | tf_op jit(solution)/shard_map/ppermute | solution.py:722
  23.4 10.1 %copy-start.6 = (f32[768]{0:T(1024)S(1)}, f32[768]{0:T(1024)}, u32[]{:S(2)}) copy-start(f32[768]{0:T(1024)} %param.18) | copy-start | bytes 9220
  29.7 3.8 %collective-permute-start.7 = (bf16[2,128,768]{2,1,0:T(8,128)(2,1)S(1)}, bf16[2,128,768]{2,1,0:T(8,128)(2,1)S(1)}, u32[]{:S(2)}, u32[]{:S(2)}) collective-permute-start(bf16[2,128,768]{2,1,0:T(8,128)(2,1)S(1)} %pad_maximum_fusion.4), channel_id=1, source_target_pairs={{0,1},{1,0},{2,3},{3,2},{4,5},{5,4},{6,7},{7,6},{8,9},{9,8},{10,11... | collective-permute-start | bytes 1179656 | tf_op jit(solution)/shard_map/ppermute | solution.py:722
  29.7 12.4 %collective-permute-start.8 = (bf16[1536,128]{1,0:T(8,128)(2,1)S(1)}, bf16[1536,128]{1,0:T(8,128)(2,1)S(1)}, u32[]{:S(2)}, u32[]{:S(2)}) collective-permute-start(bf16[1536,128]{1,0:T(8,128)(2,1)S(1)} %get-tuple-element.154.e0), channel_id=1, source_target_pairs={{0,24},{8,16},{16,8},{24,0},{1,25},{9,17},{17,9},{25,1},{2,26},{10... | collective-permute-start | bytes 1179656 | tf_op jit(solution)/shard_map/ppermute | solution.py:722
  31.2 10.9 %collective-permute-start.9 = (bf16[16,128]{1,0:T(8,128)(2,1)S(1)}, bf16[16,128]{1,0:T(8,128)(2,1)S(1)}, u32[]{:S(2)}, u32[]{:S(2)}) collective-permute-start(bf16[16,128]{1,0:T(8,128)(2,1)S(1)} %get-tuple-element.124.tags_ref), channel_id=1, source_target_pairs={{0,1},{1,2},{2,3},{3,4},{4,5},{5,6},{6,7},{8,9},{9,10},{10,11},{11... | collective-permute-start | bytes 12296 | tf_op jit(solution)/shard_map/ppermute | solution.py:828
  33.5 8.6 %slice-start = ((s8[4718592]{0:T(1024)(128)(4,1)}), s8[4194304]{0:T(1024)(128)(4,1)S(1)}, s32[]{:S(2)}) async-start(s8[4718592]{0:T(1024)(128)(4,1)} %bitcast.40), calls=%async_computation | async-start | bytes 8388608
  33.5 8.6 %slice-start.2 = ((s8[4718592]{0:T(1024)(128)(4,1)}), s8[4194304]{0:T(1024)(128)(4,1)S(1)}, s32[]{:S(2)}) async-start(s8[4718592]{0:T(1024)(128)(4,1)} %bitcast.42), calls=%async_computation.2 | async-start | bytes 8388608
  33.6 8.5 %slice-start.1 = ((s8[4718592]{0:T(1024)(128)(4,1)}), s8[524288]{0:T(1024)(128)(4,1)S(1)}, s32[]{:S(2)}) async-start(s8[4718592]{0:T(1024)(128)(4,1)} %bitcast.40), calls=%async_computation.1 | async-start | bytes 1048576
  33.6 8.5 %slice-start.3 = ((s8[4718592]{0:T(1024)(128)(4,1)}), s8[524288]{0:T(1024)(128)(4,1)S(1)}, s32[]{:S(2)}) async-start(s8[4718592]{0:T(1024)(128)(4,1)} %bitcast.42), calls=%async_computation.3 | async-start | bytes 1048576
  33.7 8.5 %copy-start.2 = (bf16[768,768]{1,0:T(8,128)(2,1)S(1)}, bf16[768,768]{1,0:T(8,128)(2,1)}, u32[]{:S(2)}) copy-start(bf16[768,768]{1,0:T(8,128)(2,1)} %wo_ref.1) | copy-start | bytes 3538948
  33.7 8.5 %copy-start.4 = (bf16[1,128,768]{2,1,0:T(8,128)(2,1)S(1)}, bf16[1,128,768]{2,1,0:T(8,128)(2,1)}, u32[]{:S(2)}) copy-start(bf16[1,128,768]{2,1,0:T(8,128)(2,1)} %param.21) | copy-start | bytes 589828
  54.8 22.7 %collective-permute-start.13 = (bf16[1536,128]{1,0:T(8,128)(2,1)S(1)}, bf16[1536,128]{1,0:T(8,128)(2,1)S(1)}, u32[]{:S(2)}, u32[]{:S(2)}) collective-permute-start(bf16[1536,128]{1,0:T(8,128)(2,1)S(1)} %get-tuple-element.131), channel_id=1, source_target_pairs={{0,8},{8,0},{16,24},{24,16},{1,9},{9,1},{17,25},{25,17},{2,10},{10... | collective-permute-start | bytes 1179656 | tf_op jit(solution)/shard_map/ppermute | solution.py:722
  55.3 22.1 %collective-permute-start.14 = (bf16[1536,128]{1,0:T(8,128)(2,1)S(1)}, bf16[1536,128]{1,0:T(8,128)(2,1)S(1)}, u32[]{:S(2)}, u32[]{:S(2)}) collective-permute-start(bf16[1536,128]{1,0:T(8,128)(2,1)S(1)} %get-tuple-element.132), channel_id=1, source_target_pairs={{0,16},{8,24},{16,0},{24,8},{1,17},{9,25},{17,1},{25,9},{2,18},{10... | collective-permute-start | bytes 1179656 | tf_op jit(solution)/shard_map/ppermute | solution.py:722
  56.9 10.8 %collective-permute-start.10 = (bf16[128,896]{1,0:T(8,128)(2,1)S(1)}, bf16[128,896]{1,0:T(8,128)(2,1)S(1)}, u32[]{:S(2)}, u32[]{:S(2)}) collective-permute-start(bf16[128,896]{1,0:T(8,128)(2,1)S(1)} %get-tuple-element.129), channel_id=1, source_target_pairs={{0,2},{1,3},{2,0},{3,1},{4,6},{5,7},{6,4},{7,5},{8,10},{9,11},{10,... | collective-permute-start | bytes 688136 | tf_op jit(solution)/shard_map/ppermute | solution.py:722
  57.5 19.8 %collective-permute-start.11 = (bf16[128,896]{1,0:T(8,128)(2,1)S(1)}, bf16[128,896]{1,0:T(8,128)(2,1)S(1)}, u32[]{:S(2)}, u32[]{:S(2)}) collective-permute-start(bf16[128,896]{1,0:T(8,128)(2,1)S(1)} %get-tuple-element.129), channel_id=1, source_target_pairs={{0,4},{1,5},{2,6},{3,7},{4,0},{5,1},{6,2},{7,3},{8,12},{9,13},{10,... | collective-permute-start | bytes 688136 | tf_op jit(solution)/shard_map/ppermute | solution.py:722
  61.0 16.4 %collective-permute-start.12 = (bf16[128,896]{1,0:T(8,128)(2,1)S(1)}, bf16[128,896]{1,0:T(8,128)(2,1)S(1)}, u32[]{:S(2)}, u32[]{:S(2)}) collective-permute-start(bf16[128,896]{1,0:T(8,128)(2,1)S(1)} %get-tuple-element.129), channel_id=1, source_target_pairs={{0,6},{1,7},{2,4},{3,5},{4,2},{5,3},{6,0},{7,1},{8,14},{9,15},{10,... | collective-permute-start | bytes 688136 | tf_op jit(solution)/shard_map/ppermute | solution.py:722
  77.5 9.0 %collective-permute-start.15 = (bf16[1536,128]{1,0:T(8,128)(2,1)S(1)}, bf16[1536,128]{1,0:T(8,128)(2,1)S(1)}, u32[]{:S(2)}, u32[]{:S(2)}) collective-permute-start(bf16[1536,128]{1,0:T(8,128)(2,1)S(1)} %get-tuple-element.145), channel_id=1, source_target_pairs={{0,24},{8,16},{16,8},{24,0},{1,25},{9,17},{17,9},{25,1},{2,26},{10... | collective-permute-start | bytes 1179656 | tf_op jit(solution)/shard_map/ppermute | solution.py:722
  79.0 13.4 %collective-permute-start.17 = (bf16[4,128,896]{2,1,0:T(8,128)(2,1)S(1)}, bf16[4,128,896]{2,1,0:T(8,128)(2,1)S(1)}, u32[]{:S(2)}, u32[]{:S(2)}) collective-permute-start(bf16[4,128,896]{2,1,0:T(8,128)(2,1)S(1)} %pad_maximum_fusion.1), channel_id=1, source_target_pairs={{0,1},{1,0},{2,3},{3,2},{4,5},{5,4},{6,7},{7,6},{8,9},{9,8},{10,11... | collective-permute-start | bytes 2752520 | tf_op jit(solution)/shard_map/ppermute | solution.py:722
  88.2 4.4 %collective-permute-start.16 = (bf16[4,120,768]{2,1,0:T(8,128)(2,1)S(1)}, bf16[4,120,768]{2,1,0:T(8,128)(2,1)S(1)}, u32[]{:S(2)}, u32[]{:S(2)}) collective-permute-start(bf16[4,120,768]{2,1,0:T(8,128)(2,1)S(1)} %get-tuple-element.159), channel_id=1, source_target_pairs={{0,1},{1,0},{2,3},{3,2},{4,5},{5,4},{6,7},{7,6},{8,9},{9,8},{10,11... | collective-permute-start | bytes 2211848 | tf_op jit(solution)/shard_map/ppermute | solution.py:722
  88.3 20.3 %collective-permute-start.18 = (bf16[1536,128]{1,0:T(8,128)(2,1)S(1)}, bf16[1536,128]{1,0:T(8,128)(2,1)S(1)}, u32[]{:S(2)}, u32[]{:S(2)}) collective-permute-start(bf16[1536,128]{1,0:T(8,128)(2,1)S(1)} %get-tuple-element.174), channel_id=1, source_target_pairs={{0,8},{8,0},{16,24},{24,16},{1,9},{9,1},{17,25},{25,17},{2,10},{10... | collective-permute-start | bytes 1179656 | tf_op jit(solution)/shard_map/ppermute | solution.py:722
  89.7 18.8 %collective-permute-start.19 = (bf16[1536,128]{1,0:T(8,128)(2,1)S(1)}, bf16[1536,128]{1,0:T(8,128)(2,1)S(1)}, u32[]{:S(2)}, u32[]{:S(2)}) collective-permute-start(bf16[1536,128]{1,0:T(8,128)(2,1)S(1)} %get-tuple-element.175), channel_id=1, source_target_pairs={{0,16},{8,24},{16,0},{24,8},{1,17},{9,25},{17,1},{25,9},{2,18},{10... | collective-permute-start | bytes 1179656 | tf_op jit(solution)/shard_map/ppermute | solution.py:722
  91.0 19.2 %collective-permute-start.20 = (bf16[1536,128]{1,0:T(8,128)(2,1)S(1)}, bf16[1536,128]{1,0:T(8,128)(2,1)S(1)}, u32[]{:S(2)}, u32[]{:S(2)}) collective-permute-start(bf16[1536,128]{1,0:T(8,128)(2,1)S(1)} %get-tuple-element.176), channel_id=1, source_target_pairs={{0,24},{8,16},{16,8},{24,0},{1,25},{9,17},{17,9},{25,1},{2,26},{10... | collective-permute-start | bytes 1179656 | tf_op jit(solution)/shard_map/ppermute | solution.py:722
  92.8 31.4 %collective-permute-start.30 = (bf16[2,120,768]{2,1,0:T(8,128)(2,1)S(1)}, bf16[2,120,768]{2,1,0:T(8,128)(2,1)S(1)}, u32[]{:S(2)}, u32[]{:S(2)}) collective-permute-start(bf16[2,120,768]{2,1,0:T(8,128)(2,1)S(1)} %slice.108), channel_id=1, source_target_pairs={{0,2},{1,3},{2,0},{3,1},{4,6},{5,7},{6,4},{7,5},{8,10},{9,11},{10,... | collective-permute-start | bytes 1105928 | tf_op jit(solution)/shard_map/ppermute | solution.py:722
  111.7 19.2 %collective-permute-start.35 = (bf16[4,96,768]{2,1,0:T(8,128)(2,1)S(1)}, bf16[4,96,768]{2,1,0:T(8,128)(2,1)S(1)}, u32[]{:S(2)}, u32[]{:S(2)}) collective-permute-start(bf16[4,96,768]{2,1,0:T(8,128)(2,1)S(1)} %get-tuple-element.191), channel_id=1, source_target_pairs={{0,1},{1,0},{2,3},{3,2},{4,5},{5,4},{6,7},{7,6},{8,9},{9,8},{10,11... | collective-permute-start | bytes 1769480 | tf_op jit(solution)/shard_map/ppermute | solution.py:722
  111.8 7.3 %collective-permute-start.21 = (bf16[136,640]{1,0:T(8,128)(2,1)S(1)}, bf16[136,640]{1,0:T(8,128)(2,1)S(1)}, u32[]{:S(2)}, u32[]{:S(2)}) collective-permute-start(bf16[136,640]{1,0:T(8,128)(2,1)S(1)} %get-tuple-element.178), channel_id=1, source_target_pairs={{0,8},{8,0},{16,24},{24,16},{1,9},{9,1},{17,25},{25,17},{2,10},{10... | collective-permute-start | bytes 522248 | tf_op jit(solution)/shard_map/ppermute | solution.py:722
  112.4 10.2 %collective-permute-start.22 = (bf16[136,640]{1,0:T(8,128)(2,1)S(1)}, bf16[136,640]{1,0:T(8,128)(2,1)S(1)}, u32[]{:S(2)}, u32[]{:S(2)}) collective-permute-start(bf16[136,640]{1,0:T(8,128)(2,1)S(1)} %get-tuple-element.179), channel_id=1, source_target_pairs={{0,16},{8,24},{16,0},{24,8},{1,17},{9,25},{17,1},{25,9},{2,18},{10... | collective-permute-start | bytes 522248 | tf_op jit(solution)/shard_map/ppermute | solution.py:722
  114.2 8.5 %collective-permute-start.23 = (bf16[136,640]{1,0:T(8,128)(2,1)S(1)}, bf16[136,640]{1,0:T(8,128)(2,1)S(1)}, u32[]{:S(2)}, u32[]{:S(2)}) collective-permute-start(bf16[136,640]{1,0:T(8,128)(2,1)S(1)} %get-tuple-element.180), channel_id=1, source_target_pairs={{0,24},{8,16},{16,8},{24,0},{1,25},{9,17},{17,9},{25,1},{2,26},{10... | collective-permute-start | bytes 522248 | tf_op jit(solution)/shard_map/ppermute | solution.py:722
  124.1 7.1 %collective-permute-start.24 = (bf16[4,104,640]{2,1,0:T(8,128)(2,1)S(1)}, bf16[4,104,640]{2,1,0:T(8,128)(2,1)S(1)}, u32[]{:S(2)}, u32[]{:S(2)}) collective-permute-start(bf16[4,104,640]{2,1,0:T(8,128)(2,1)S(1)} %get-tuple-element.182), channel_id=1, source_target_pairs={{0,1},{1,0},{2,3},{3,2},{4,5},{5,4},{6,7},{7,6},{8,9},{9,8},{10,11... | collective-permute-start | bytes 1597448 | tf_op jit(solution)/shard_map/ppermute | solution.py:722
  124.3 16.0 %collective-permute-start.31 = (bf16[1,120,768]{2,1,0:T(8,128)(2,1)S(1)}, bf16[1,120,768]{2,1,0:T(8,128)(2,1)S(1)}, u32[]{:S(2)}, u32[]{:S(2)}) collective-permute-start(bf16[1,120,768]{2,1,0:T(8,128)(2,1)S(1)} %slice.111), channel_id=1, source_target_pairs={{0,4},{1,5},{2,6},{3,7},{4,0},{5,1},{6,2},{7,3},{8,12},{9,13},{10,... | collective-permute-start | bytes 552968 | tf_op jit(solution)/shard_map/ppermute | solution.py:722
  131.1 13.6 %collective-permute-start.36 = (bf16[2,96,768]{2,1,0:T(8,128)(2,1)S(1)}, bf16[2,96,768]{2,1,0:T(8,128)(2,1)S(1)}, u32[]{:S(2)}, u32[]{:S(2)}) collective-permute-start(bf16[2,96,768]{2,1,0:T(8,128)(2,1)S(1)} %slice.109), channel_id=1, source_target_pairs={{0,2},{1,3},{2,0},{3,1},{4,6},{5,7},{6,4},{7,5},{8,10},{9,11},{10,... | collective-permute-start | bytes 884744 | tf_op jit(solution)/shard_map/ppermute | solution.py:722
  131.3 19.8 %collective-permute-start.25 = (bf16[2,104,640]{2,1,0:T(8,128)(2,1)S(1)}, bf16[2,104,640]{2,1,0:T(8,128)(2,1)S(1)}, u32[]{:S(2)}, u32[]{:S(2)}) collective-permute-start(bf16[2,104,640]{2,1,0:T(8,128)(2,1)S(1)} %slice.110), channel_id=1, source_target_pairs={{0,2},{1,3},{2,0},{3,1},{4,6},{5,7},{6,4},{7,5},{8,10},{9,11},{10,... | collective-permute-start | bytes 798728 | tf_op jit(solution)/shard_map/ppermute | solution.py:722
  140.3 16.0 %collective-permute-start.32 = (bf16[120,768]{1,0:T(8,128)(2,1)S(1)}, bf16[120,768]{1,0:T(8,128)(2,1)S(1)}, u32[]{:S(2)}, u32[]{:S(2)}) collective-permute-start(bf16[120,768]{1,0:T(8,128)(2,1)S(1)} %fusion.3.refs_0_), channel_id=1, source_target_pairs={{0,8},{8,0},{16,24},{24,16},{1,9},{9,1},{17,25},{25,17},{2,10},{10... | collective-permute-start | bytes 552968 | tf_op jit(solution)/shard_map/ppermute | solution.py:722
  141.8 18.8 %collective-permute-start.33 = (bf16[120,768]{1,0:T(8,128)(2,1)S(1)}, bf16[120,768]{1,0:T(8,128)(2,1)S(1)}, u32[]{:S(2)}, u32[]{:S(2)}) collective-permute-start(bf16[120,768]{1,0:T(8,128)(2,1)S(1)} %fusion.3.refs_0_), channel_id=1, source_target_pairs={{0,16},{8,24},{16,0},{24,8},{1,17},{9,25},{17,1},{25,9},{2,18},{10... | collective-permute-start | bytes 552968 | tf_op jit(solution)/shard_map/ppermute | solution.py:722
  142.4 20.0 %collective-permute-start.34 = (bf16[120,768]{1,0:T(8,128)(2,1)S(1)}, bf16[120,768]{1,0:T(8,128)(2,1)S(1)}, u32[]{:S(2)}, u32[]{:S(2)}) collective-permute-start(bf16[120,768]{1,0:T(8,128)(2,1)S(1)} %fusion.3.refs_0_), channel_id=1, source_target_pairs={{0,24},{8,16},{16,8},{24,0},{1,25},{9,17},{17,9},{25,1},{2,26},{10... | collective-permute-start | bytes 552968 | tf_op jit(solution)/shard_map/ppermute | solution.py:722
  144.8 11.4 %collective-permute-start.37 = (bf16[1,96,768]{2,1,0:T(8,128)(2,1)S(1)}, bf16[1,96,768]{2,1,0:T(8,128)(2,1)S(1)}, u32[]{:S(2)}, u32[]{:S(2)}) collective-permute-start(bf16[1,96,768]{2,1,0:T(8,128)(2,1)S(1)} %slice.112), channel_id=1, source_target_pairs={{0,4},{1,5},{2,6},{3,7},{4,0},{5,1},{6,2},{7,3},{8,12},{9,13},{10,... | collective-permute-start | bytes 442376 | tf_op jit(solution)/shard_map/ppermute | solution.py:722
  151.2 7.8 %collective-permute-start.26 = (bf16[1,104,640]{2,1,0:T(8,128)(2,1)S(1)}, bf16[1,104,640]{2,1,0:T(8,128)(2,1)S(1)}, u32[]{:S(2)}, u32[]{:S(2)}) collective-permute-start(bf16[1,104,640]{2,1,0:T(8,128)(2,1)S(1)} %slice.113), channel_id=1, source_target_pairs={{0,4},{1,5},{2,6},{3,7},{4,0},{5,1},{6,2},{7,3},{8,12},{9,13},{10,... | collective-permute-start | bytes 399368 | tf_op jit(solution)/shard_map/ppermute | solution.py:722
  156.2 6.4 %collective-permute-start.38 = (bf16[96,768]{1,0:T(8,128)(2,1)S(1)}, bf16[96,768]{1,0:T(8,128)(2,1)S(1)}, u32[]{:S(2)}, u32[]{:S(2)}) collective-permute-start(bf16[96,768]{1,0:T(8,128)(2,1)S(1)} %fusion.4.refs_0_), channel_id=1, source_target_pairs={{0,8},{8,0},{16,24},{24,16},{1,9},{9,1},{17,25},{25,17},{2,10},{10... | collective-permute-start | bytes 442376 | tf_op jit(solution)/shard_map/ppermute | solution.py:722
  156.3 9.6 %collective-permute-start.39 = (bf16[96,768]{1,0:T(8,128)(2,1)S(1)}, bf16[96,768]{1,0:T(8,128)(2,1)S(1)}, u32[]{:S(2)}, u32[]{:S(2)}) collective-permute-start(bf16[96,768]{1,0:T(8,128)(2,1)S(1)} %fusion.4.refs_0_), channel_id=1, source_target_pairs={{0,16},{8,24},{16,0},{24,8},{1,17},{9,25},{17,1},{25,9},{2,18},{10... | collective-permute-start | bytes 442376 | tf_op jit(solution)/shard_map/ppermute | solution.py:722
  159.1 7.6 %collective-permute-start.40 = (bf16[96,768]{1,0:T(8,128)(2,1)S(1)}, bf16[96,768]{1,0:T(8,128)(2,1)S(1)}, u32[]{:S(2)}, u32[]{:S(2)}) collective-permute-start(bf16[96,768]{1,0:T(8,128)(2,1)S(1)} %fusion.4.refs_0_), channel_id=1, source_target_pairs={{0,24},{8,16},{16,8},{24,0},{1,25},{9,17},{17,9},{25,1},{2,26},{10... | collective-permute-start | bytes 442376 | tf_op jit(solution)/shard_map/ppermute | solution.py:722
  160.6 9.3 %collective-permute-start.27 = (bf16[104,640]{1,0:T(8,128)(2,1)S(1)}, bf16[104,640]{1,0:T(8,128)(2,1)S(1)}, u32[]{:S(2)}, u32[]{:S(2)}) collective-permute-start(bf16[104,640]{1,0:T(8,128)(2,1)S(1)} %fusion.5.refs_0_), channel_id=1, source_target_pairs={{0,8},{8,0},{16,24},{24,16},{1,9},{9,1},{17,25},{25,17},{2,10},{10... | collective-permute-start | bytes 399368 | tf_op jit(solution)/shard_map/ppermute | solution.py:722
  162.4 7.5 %collective-permute-start.28 = (bf16[104,640]{1,0:T(8,128)(2,1)S(1)}, bf16[104,640]{1,0:T(8,128)(2,1)S(1)}, u32[]{:S(2)}, u32[]{:S(2)}) collective-permute-start(bf16[104,640]{1,0:T(8,128)(2,1)S(1)} %fusion.5.refs_0_), channel_id=1, source_target_pairs={{0,16},{8,24},{16,0},{24,8},{1,17},{9,25},{17,1},{25,9},{2,18},{10... | collective-permute-start | bytes 399368 | tf_op jit(solution)/shard_map/ppermute | solution.py:722
  162.7 8.9 %collective-permute-start.29 = (bf16[104,640]{1,0:T(8,128)(2,1)S(1)}, bf16[104,640]{1,0:T(8,128)(2,1)S(1)}, u32[]{:S(2)}, u32[]{:S(2)}) collective-permute-start(bf16[104,640]{1,0:T(8,128)(2,1)S(1)} %fusion.5.refs_0_), channel_id=1, source_target_pairs={{0,24},{8,16},{16,8},{24,0},{1,25},{9,17},{17,9},{25,1},{2,26},{10... | collective-permute-start | bytes 399368 | tf_op jit(solution)/shard_map/ppermute | solution.py:722

commit v2 on v1

--- a/solution.py
+++ b/solution.py
@@ -139,20 +139,38 @@
     return jnp.concatenate([lanes(high, none), lanes(none, high), lanes(low, none), lanes(none, low)], 0)
 
 
+def pack_kernel(sc, x_ref, tag_ref, out_ref):
+    out_ref[0:T, :] = x_ref[...]
+    tags = tag_ref[...].astype(F32)
+    wide = [lanes(*[tags[h : h + 1, :] for h in range(6 * r, 6 * r + 6)]) for r in range(2)]
+    out_ref[T : T + 8, :] = jnp.concatenate(wide + [jnp.zeros((6, D), F32)], 0).astype(BF)
+
+
+def packed(scalars, own, tags):
+    out = sds((T + 8, D), BF)
+    return call(
+        pack_kernel, scalars, (own, tags), [whole(own.shape), whole(tags.shape)], out, whole(out.shape), (1,),
+        vmem=2,
+    )
+
+
+def tag_pair(ref):
+    rows = jnp.concatenate([ref[...].astype(F32), jnp.zeros((4, T), F32)], 0)
+    return rows, rows.T
+
+
 def own_kernel(
     sc, x_ref, gain_ref, w_ref, feature_ref, g_ref, tag_ref,
-    pay_ref, qkv_ref, phiq_ref, phik_ref, expo_ref, blend_ref, num_ref, den_ref, proj_ref, tags_ref,
+    pay_ref, qkv_ref, phiq_ref, phik_ref, expo_ref, blend_ref, num_ref, den_ref, proj_ref,
 ):
-    unit, _ = norm_parts(x_ref[...].astype(F32))
+    unit, _ = norm_parts(x_ref[0:T, :].astype(F32))
     normed = unit * gain_ref[...]
     low = normed.astype(BF)
     pay_ref[0:D, :] = normed.T.astype(BF)
     for t in range(6):
         pay_ref[D + 128 * t : D + 128 * t + 128, :] = g_ref[:, 128 * t : 128 * t + 128]
     qkv_ref[...] = nn(low, w_ref[...]).astype(BF)
-    rows = jnp.concatenate([tag_ref[...].astype(F32), jnp.zeros((4, T), F32)], 0)
-    tags_ref[...] = rows.astype(BF)
-    cols = rows.T
+    rows, cols = tag_pair(tag_ref)
     first = iota((T, 128), 1) < HD
     query_at, key_at = iota((T, T), 0), iota((T, T), 1)
     allowed = (key_at <= query_at) & (key_at + sc[0] * T < sc[1])
@@ -186,7 +204,7 @@
     outs = (
         sds((2 * D, 128), BF), sds((T, 3 * D), BF), sds((T, HM), F32), sds((T, HM), F32),
         sds((H, T, T), F32), sds((H, T, T), BF), sds((T, D), F32), sds((T, 128), F32),
-        sds((2 * 128, 2 * M), BF), sds((16, T), BF),
+        sds((2 * 128, 2 * M), BF),
     )
     args = (own, gain, qkv_weight, feature_proj, cotangent, tags)
     return call(
@@ -196,19 +214,22 @@
 
 
 def others_kernel(begin, sc, x_ref, gain_ref, w_ref, proj_ref, *refs):
-    u_ref, v_ref, phi_ref, sums_ref, norms_ref = refs[-5:]
+    tags_ref, u_ref, v_ref, phi_ref, sums_ref, norms_ref = refs[-6:]
     slot = pl.program_id(0)
     span = sc[8 + begin + slot]
 
     @pl.when(slot == 0)
     def _():
         if begin:
-            sums_ref[...], norms_ref[...] = refs[3][...], refs[4][...]
+            sums_ref[...], norms_ref[...] = refs[4][...], refs[5][...]
         else:
             sums_ref[...] = jnp.zeros_like(sums_ref)
             norms_ref[...] = jnp.zeros_like(norms_ref)
 
-    unit, _ = norm_parts(x_ref[0].astype(F32))
+    unit, _ = norm_parts(x_ref[0, 0:T, :].astype(F32))
+    wide = x_ref[0, T : T + 8, :].astype(F32)
+    rows = [wide[h // 6 : h // 6 + 1, 128 * (h % 6) : 128 * (h % 6) + 128] for h in range(H)]
+    tags_ref[0] = jnp.concatenate(rows + [jnp.zeros((4, 128), F32)], 0)
     low = (unit * gain_ref[...]).astype(BF)
     earlier = span < sc[0]
     offset = pl.multiple_of(jnp.where(earlier, D, 0), D)
@@ -241,45 +262,43 @@
 def others_forward(scalars, begin, pieces, gain, qkv_weight, proj, so_far=()):
     count, spans = pieces.shape[0], 7
     outs = (
-        sds((spans, T, D), BF), sds((spans, T, D), BF), sds((spans, T, HM), BF),
+        sds((spans, 16, T), F32), sds((spans, T, D), BF), sds((spans, T, D), BF), sds((spans, T, HM), BF),
         sds((D, M), F32), sds((8, HM), F32),
     )
     step = lambda i, sc: (begin + i, 0, 0)
-    specs = [pl.BlockSpec((1, T, D), lambda i, sc: (i, 0, 0))]
+    specs = [pl.BlockSpec((1, T + 8, D), lambda i, sc: (i, 0, 0))]
     specs += [whole(a.shape) for a in (gain, qkv_weight, proj)]
     aliases = {}
     if so_far:
-        specs += [pl.BlockSpec(memory_space=pl.ANY)] * 3 + [whole(a.shape) for a in so_far[3:]]
-        aliases = {5: 0, 6: 1, 7: 2}
+        specs += [pl.BlockSpec(memory_space=pl.ANY)] * 4 + [whole(a.shape) for a in so_far[4:]]
+        aliases = {5: 0, 6: 1, 7: 2, 8: 3}
     return call(
         functools.partial(others_kernel, begin), scalars, (pieces, gain, qkv_weight, proj, *so_far), specs,
         outs,
-        [pl.BlockSpec((1, T, D), step), pl.BlockSpec((1, T, D), step), pl.BlockSpec((1, T, HM), step),
-         whole((D, M)), whole((8, HM))],
+        [pl.BlockSpec((1, 16, T), step), pl.BlockSpec((1, T, D), step), pl.BlockSpec((1, T, D), step),
+         pl.BlockSpec((1, T, HM), step), whole((D, M)), whole((8, HM))],
         (count,), vmem=8, flops=count * 600_000_000, size=count * 1_400_000 + 3_500_000, aliases=aliases,
     )
 
 
 def own_cols(tags_ref):
-    return tags_ref[...].astype(F32).T.astype(BF)
+    return tag_pair(tags_ref)[1].astype(BF)
 
 
 def middle_kernel(
-    sc, x_ref, qkv_ref, phiq_ref, sums_ref, norms_ref, numl_ref, denl_ref, tags_ref, tags_prev,
-    up_prev, vp_prev, phi_prev, gain_ref, wo_ref, wup_ref, wdown_ref, g_ref,
-    a0, a1, a2, a3, b0, b1, b2, b3, out_ref, dmid_ref, dn_low_ref, dn_ref, dd_ref, expo_ref, blend_ref, gain_out,
-    mid_s, nm_s, acc_s, dnm_s, num_s, den_s, turn_s,
+    sc, x_ref, qkv_ref, phiq_ref, sums_ref, norms_ref, numl_ref, denl_ref, tags_ref,
+    tags_prev, up_prev, vp_prev, phi_prev, gain_ref, wo_ref, wup_ref, wdown_ref, g_ref,
+    hid_ref, pre_ref, nm_ref, att_ref, out_ref, dmid_ref, dn_low_ref, dn_ref, dd_ref, expo_ref, blend_ref, gain_out,
+    mid_s, nm_s, acc_s, dnm_s, num_s, den_s,
 ):
-    first_pay, second_pay = (a0, a1, a2, a3), (b0, b1, b2, b3)
     step = pl.program_id(0)
-    me = sc[6]
     first = iota((T, 128), 1) < HD
     valid = iota((T, 1), 0) + sc[0] * T < sc[1]
 
     @pl.when(step == 0)
     def _():
-        own = tags_ref[...].astype(F32).T
-        prev = tags_prev[...].astype(F32)
+        _, own = tag_pair(tags_ref)
+        prev = tags_prev[0]
         prev_tag = [prev[h : h + 1, EDGE:T] for h in range(H)]
         edge_first = iota((EDGE, 128), 1) < HD
         edge_ok = (sc[4] > 0) & (iota((EDGE, EDGE), 1) + (sc[0] * T - EDGE) < sc[1])
@@ -317,21 +336,13 @@
             den = jnp.where(first, dens[:, 2 * p : 2 * p + 1], dens[:, 2 * p + 1 : 2 * p + 2])
             mid_s[:, at] = jnp.where(valid, num_s[:, at] / den, 0.0)
         attended = mid_s[...].astype(BF)
-        turned = mid_s[...].T.astype(BF)
-        for k in range(4):
-            upper = (me ^ k) >= 2
-            for s in range(8):
-                first_pay[k][768 + 48 * s : 768 + 48 * s + 48, :] = jnp.where(
-                    upper, turned[96 * s + 48 : 96 * s + 96, :], turned[96 * s : 96 * s + 48, :]
-                )
-        mid = x_ref[...].astype(F32) + nn(attended, wo_ref[...])
+        att_ref[...] = attended
+        mid = x_ref[0:T, :].astype(F32) + nn(attended, wo_ref[...])
         mid_s[...] = mid
         unit, _ = norm_parts(mid)
         normed = unit * gain_ref[...]
         nm_s[...] = normed.astype(BF)
-        turned = normed.T.astype(BF)
-        for k in range(4):
-            second_pay[k][0:D, :] = turned
+        nm_ref[...] = normed.astype(BF)
         acc_s[...] = jnp.zeros_like(acc_s)
         dnm_s[...] = jnp.zeros_like(dnm_s)
 
@@ -347,17 +358,8 @@
     hidden_low = hidden.astype(BF)
     acc_s[...] += nn(hidden_low, wdown_ref[...])
     dnm_s[...] += nt(grad_pre, wup_ref[...])
-    turn_s[...] = hidden.T.astype(BF)
-    for k in range(4):
-        for s in range(2):
-            base = pl.multiple_of(192 * step + 96 * s, 96)
-            begin = pl.multiple_of(384 * s + 96 * (k ^ me), 96)
-            first_pay[k][pl.ds(base, 96), :] = turn_s[pl.ds(begin, 96), :]
-
-        @pl.when((step ^ me) == k)
-        def _():
-            for t in range(6):
-                second_pay[k][D + 128 * t : D + 128 * t + 128, :] = grad_pre[:, 128 * t : 128 * t + 128]
+    hid_ref[...] = hidden_low
+    pre_ref[...] = grad_pre
 
     @pl.when(step == 3)
     def _():
@@ -369,12 +371,6 @@
         dmid = g_ref[...].astype(F32) + norm_back(unit, scale, gain_ref[...], grad)
         dmid_ref[...] = dmid
         high, low = split(dmid)
-        for k in range(4):
-            right = ((me ^ k) & 1) > 0
-            for t in range(3):
-                first_pay[k][1152 + 128 * t : 1152 + 128 * t + 128, :] = jnp.where(
-                    right, high[:, 384 + 128 * t : 512 + 128 * t], high[:, 128 * t : 128 * t + 128]
-                )
         datt = (nt(high, wo_ref[...]) + nt(low, wo_ref[...])).astype(BF).astype(F32)
         dens = den_s[...]
         ddens = jnp.zeros((T, 128), F32)
@@ -395,16 +391,18 @@
         dn_low_ref[:, D + 32 : D + 128] = jnp.zeros((T, 96), BF)
 
 
-def middle(scalars, own, qkv, phi_q, sums, norms, num, den, tags, tags_prev, others, gain, wo, wup, wdown, cot):
-    u, v, phi = others
+def middle(scalars, own, qkv, phi_q, sums, norms, num, den, tags, others, gain, wo, wup, wdown, cot):
+    tags_all, u, v, phi = others
     prev = lambda i, sc: (sc[2], 1, 0)
-    outs = tuple([sds((2 * D, 128), BF)] * 8) + (
+    outs = (
+        sds((T, 4 * D), BF), sds((T, 4 * D), BF), sds((T, D), BF), sds((T, D), BF),
         sds((T, D), BF), sds((T, D), F32), sds((T, D + 128), BF),
         sds((T, D), F32), sds((T, 128), F32), sds((H, EDGE, EDGE), F32), sds((H, EDGE, EDGE), BF),
         sds((8, D), F32),
     )
-    args = (own, qkv, phi_q, sums, norms, num, den, tags, tags_prev, u, v, phi, gain, wo, wup, wdown, cot)
-    specs = [whole(a.shape) for a in args[:9]] + [
+    args = (own, qkv, phi_q, sums, norms, num, den, tags, tags_all, u, v, phi, gain, wo, wup, wdown, cot)
+    specs = [whole(a.shape) for a in args[:8]] + [
+        pl.BlockSpec((1, 16, T), lambda i, sc: (sc[2], 0, 0)),
         pl.BlockSpec((1, EDGE, D), prev), pl.BlockSpec((1, EDGE, D), prev),
         pl.BlockSpec((1, EDGE, HM), prev),
         whole(gain.shape), whole(wo.shape),
@@ -414,25 +412,58 @@
     scratch = [
         pltpu.VMEM((T, D), F32), pltpu.VMEM((T, D), BF), pltpu.VMEM((T, D), F32),
         pltpu.VMEM((T, D), F32), pltpu.VMEM((T, D), F32), pltpu.VMEM((T, 128), F32),
-        pltpu.VMEM((D, T), BF),
     ]
     return call(
-        middle_kernel, scalars, args, specs, outs, [whole(o.shape) for o in outs], (4,), scratch,
+        middle_kernel, scalars, args, specs, outs,
+        [pl.BlockSpec((T, D), lambda i, sc: (0, i))] * 2 + [whole(o.shape) for o in outs[2:]], (4,), scratch,
         vmem=12, flops=3_500_000_000, size=20_000_000,
     )
 
 
+def exchange_kernel(sc, hid_ref, pre_ref, nm_ref, att_ref, dmid_ref, *refs):
+    first_pay, second_pay, turn_s = refs[0:4], refs[4:8], refs[8]
+    me = sc[6]
+    for b in range(4):
+        turn_s[D * b : D * b + D, :] = hid_ref[:, D * b : D * b + D].astype(F32).T.astype(BF)
+    turned_nm = nm_ref[...].astype(F32).T.astype(BF)
+    turned_att = att_ref[...].astype(F32).T.astype(BF)
+    dmid = dmid_ref[...].astype(BF)
+    for k in range(4):
+        mate = me ^ k
+        for s in range(8):
+            begin = pl.multiple_of(384 * s + 96 * mate, 96)
+            first_pay[k][96 * s : 96 * s + 96, :] = turn_s[pl.ds(begin, 96), :]
+            first_pay[k][768 + 48 * s : 768 + 48 * s + 48, :] = jnp.where(
+                mate >= 2, turned_att[96 * s + 48 : 96 * s + 96, :], turned_att[96 * s : 96 * s + 48, :]
+            )
+        for t in range(3):
+            first_pay[k][1152 + 128 * t : 1152 + 128 * t + 128, :] = jnp.where(
+                (mate & 1) > 0, dmid[:, 384 + 128 * t : 512 + 128 * t], dmid[:, 128 * t : 128 * t + 128]
+            )
+        second_pay[k][0:D, :] = turned_nm
+        for t in range(6):
+            begin = pl.multiple_of(D * mate + 128 * t, 128)
+            second_pay[k][D + 128 * t : D + 128 * t + 128, :] = pre_ref[:, pl.ds(begin, 128)]
+
+
+def exchange(scalars, *args):
+    outs = tuple([sds((2 * D, 128), BF)] * 8)
+    return call(
+        exchange_kernel, scalars, args, [whole(a.shape) for a in args], outs, [whole(o.shape) for o in outs],
+        (1,), [pltpu.VMEM((4 * D, T), BF)], vmem=8,
+    )
+
+
 def own_back_kernel(
-    sc, tags_ref, tags_prev, qkv_ref, phiq_ref, phik_ref, proj_ref, expo_ref, blend_ref, dn_ref, dd_ref,
-    sums_ref, norms_ref, up_prev, vp_prev, phi_prev, expo_e, blend_e,
+    sc, tags_ref, qkv_ref, phiq_ref, phik_ref, proj_ref, expo_ref, blend_ref, dn_ref, dd_ref,
+    sums_ref, norms_ref, tags_prev, up_prev, vp_prev, phi_prev, expo_e, blend_e,
     dq_ref, dk_ref, dv_ref, dphi_ref,
 ):
-    rows = tags_ref[...].astype(F32)
-    cols = rows.T
+    rows, cols = tag_pair(tags_ref)
     first = iota((T, 128), 1) < HD
     query_at, key_at = iota((T, T), 0), iota((T, T), 1)
     allowed = (key_at <= query_at) & (key_at + sc[0] * T < sc[1])
-    prev_tag = tags_prev[...].astype(F32)
+    prev_tag = tags_prev[0]
     edge_first = iota((EDGE, 128), 1) < HD
     edge_ok = (sc[4] > 0) & (iota((EDGE, EDGE), 1) + (sc[0] * T - EDGE) < sc[1])
     proj = proj_ref[...]
@@ -478,14 +509,15 @@
         dv_ref[:, at] = pick(first, dvs)
 
 
-def own_back(scalars, tags, tags_prev, qkv, phi_q, phi_k, proj, expo, blend, dnum, dden, sums, norms, others, expo_e, blend_e):
-    u, v, phi = others
+def own_back(scalars, tags, qkv, phi_q, phi_k, proj, expo, blend, dnum, dden, sums, norms, others, expo_e, blend_e):
+    tags_all, u, v, phi = others
     prev = lambda i, sc: (sc[2], 1, 0)
     args = (
-        tags, tags_prev, qkv, phi_q, phi_k, proj, expo, blend, dnum, dden, sums, norms, u, v, phi, expo_e,
+        tags, qkv, phi_q, phi_k, proj, expo, blend, dnum, dden, sums, norms, tags_all, u, v, phi, expo_e,
         blend_e,
     )
-    specs = [whole(a.shape) for a in args[:12]] + [
+    specs = [whole(a.shape) for a in args[:11]] + [
+        pl.BlockSpec((1, 16, T), lambda i, sc: (sc[2], 0, 0)),
         pl.BlockSpec((1, EDGE, D), prev), pl.BlockSpec((1, EDGE, D), prev),
         pl.BlockSpec((1, EDGE, HM), prev),
         whole(expo_e.shape), whole(blend_e.shape),
@@ -566,7 +598,7 @@
             ).astype(BF)
             dqkv_s[:, 2 * D + 128 * p : 2 * D + 128 * p + 128] = (dv_ref[:, at] + pick(first, dvs)).astype(BF)
         grad = nt(dqkv_s[...], w_ref[...])
-        unit, scale = norm_parts(x_ref[...].astype(F32))
+        unit, scale = norm_parts(x_ref[0:T, :].astype(F32))
         grad_ref[...] = dmid_ref[...] + norm_back(unit, scale, gain_ref[...], grad)
         attn = jnp.sum(grad * unit, 0, keepdims=True)
         mlp = gmlp_ref[0:1, :]
@@ -584,7 +616,7 @@
 
 
 def last(scalars, dn_pieces, others, own, tags, qkv, phi_k, proj, dq, dk, dv, dphi, dmid, gain, qkv_weight, gmlp):
-    u, v, phi = others
+    _, u, v, phi = others
     count = dn_pieces.shape[0] - 1
     follow = lambda i, sc: (sc[3], 0, 0)
     args = (
@@ -677,7 +709,7 @@
     outs = (sds((4, rows, width), F32), sds((4, rows, width), BF))
     return call(
         kernel, scalars, args, [whole(a.shape) for a in args], outs, [whole(o.shape) for o in outs], (1,),
-        [pltpu.VMEM(shape, F32) for shape in scratch], vmem=8, flops=600_000_000, size=5_000_000,
+        [pltpu.VMEM(shape, F32) for shape in scratch], vmem=8, flops=600_000_000, size=20_000_000_000,
     )
 
 
@@ -737,11 +769,15 @@
 ):
     seq, row = lax.axis_index("seq"), lax.axis_index("dp")
     spans = lax.axis_size("seq")
-    token_order, grad_order = (1, 2, 3, 4, 6, 5, 7), (2, 4, 6, 1, 3, 5, 7)
+    token_order, grad_order = (1, 2, 4, 6, 3, 5, 7), (2, 4, 6, 1, 3, 5, 7)
     before, after = seq ^ jnp.maximum(seq - 1, 0), seq ^ jnp.minimum(seq + 1, spans - 1)
+
+    def place_of(bits):
+        return jnp.where(bits == 7, 6, jnp.where(bits == 3, 4, 0))
+
     scalars = jnp.stack(
         [
-            seq, lengths[0], jnp.maximum(before - 1, 0), jnp.maximum(after - 1, 0),
+            seq, lengths[0], place_of(before), place_of(after),
             seq > 0, seq < spans - 1, row,
             jnp.where(after == 7, 7, jnp.where(after == 3, 5, 4)),
             *[seq ^ k for k in token_order], *[0] * 9,
@@ -752,39 +788,41 @@
     own, cot = tokens[0], cotangent[0]
     gain_in, gain_mid = attn_gain[None], mlp_gain[None]
 
-    near, far_a, far_b, mate = (swap(own, "seq", bits) for bits in (2, 4, 6, 1))
-    early, qkv, phi_q, phi_k, expo, blend, num, den, proj, tags = own_forward(
-        scalars, own, gain_in, qkv_weight, feature_proj, cot, buckets[0]
-    )
-    near, early = lax.optimization_barrier((near, early))
-    early_1, early_2 = swap(early, "dp", 1), swap(early, "dp", 2)
-    tags_prev = from_behind(tags, "seq", 1)
+    tags = buckets[0]
+    own = packed(scalars, own, tags)
+    mate, near, far_a, far_b = (swap(own, "seq", bits) for bits in (1, 2, 4, 6))
+    early, qkv, phi_q, phi_k, expo, blend, num, den, proj = own_forward(
+        scalars, own, gain_in, qkv_weight, feature_proj, cot, tags
+    )
+    mate, near, early = lax.optimization_barrier((mate, near, early))
     some = others_forward(
-        scalars, 0, jnp.stack([mate, near, swap(near, "seq", 1)]), gain_in, qkv_weight, proj
-    )
-    far, some, late = lax.optimization_barrier((jnp.stack([far_a, far_b]), some, (early, early_1, early_2)))
-    early_3 = swap(late[0], "dp", 3)
-    u, v, phi, sums, norms = others_forward(
-        scalars, 3, jnp.concatenate([far, swap(far, "seq", 1)], 0), gain_in, qkv_weight, proj, some
-    )
-    others = (u, v, phi)
-    sums, early = lax.optimization_barrier((sums, (early, early_1, early_2, early_3)))
+        scalars, 0, jnp.stack([mate, near]), gain_in, qkv_weight, proj
+    )
+    far_a, far_b, some, early = lax.optimization_barrier((far_a, far_b, some, early))
+    far = swap(jnp.stack([near, far_a, far_b]), "seq", 1)
+    early_parts = [swap(early, "dp", k) for k in (1, 2, 3)]
+    tags_all, u, v, phi, sums, norms = others_forward(
+        scalars, 2, jnp.concatenate([jnp.stack([far_a, far_b]), far], 0), gain_in, qkv_weight, proj, some
+    )
+    others = (tags_all, u, v, phi)
     results = middle(
-        scalars, own, qkv, phi_q, sums, norms, num, den, tags, tags_prev, others, gain_mid, out_weight,
+        scalars, own, qkv, phi_q, sums, norms, num, den, tags, others, gain_mid, out_weight,
         up_weight, down_weight, cot,
     )
-    pay_1, pay_2 = results[0:4], results[4:8]
-    layer_out, dmid, dn_low, dnum, dden, expo_e, blend_e, gmlp = results[8:]
+    results, early_parts = lax.optimization_barrier((results, early_parts))
+    early = (early, *early_parts)
+    layer_out, dmid, dn_low, dnum, dden, expo_e, blend_e, gmlp = results[4:]
+    pays = exchange(scalars, *results[0:4], dmid)
+    pay_1, pay_2 = pays[0:4], pays[4:8]
     dn_far = [swap(dn_low, "seq", bits) for bits in (2, 4, 6)]
     parts_1 = [pay_1[0], swap(pay_1[1], "dp", 1), swap(pay_1[2], "dp", 2)]
     dq, dk, dv, dphi = own_back(
-        scalars, tags, tags_prev, qkv, phi_q, phi_k, proj, expo, blend, dnum, dden, sums, norms, others,
+        scalars, tags, qkv, phi_q, phi_k, proj, expo, blend, dnum, dden, sums, norms, others,
         expo_e, blend_e,
     )
-    dn_half, parts_1, last_1, dk = lax.optimization_barrier(
-        (jnp.stack([dn_low, *dn_far]), parts_1, pay_1[3], dk)
-    )
+    parts_1, last_1, dk = lax.optimization_barrier((parts_1, pay_1[3], dk))
     parts_1.append(swap(last_1, "dp", 3))
+    dn_half = jnp.stack([dn_low, *dn_far])
     dn_pieces = jnp.concatenate([dn_half, swap(dn_half, "seq", 1)], 0)
     parts_1, pay_2 = lax.optimization_barrier((parts_1, pay_2))
     parts_2 = [pay_2[0]] + [swap(pay_2[k], "dp", k) for k in (1, 2, 3)]
@@ -798,7 +836,11 @@
     pay_3, parts_2 = lax.optimization_barrier((pay_3, parts_2))
     share_1 = reduce_spans(total_1[0:2], total_1[2:4].astype(BF), (2, 4))
     parts_3 = [pay_3[0]] + [swap(pay_3[k], "dp", k) for k in (1, 2, 3)]
-    share_2 = reduce_spans(*weights(second_kernel, scalars, parts_2, ROWS_2, D, [(D, D)]))
+    keep, send = weights(second_kernel, scalars, parts_2, ROWS_2, D, [(D, D)])
+    total_2 = keep + swap(send, "seq", 1).astype(F32)
+    total_2 = total_2[0:2] + swap(total_2[2:4].astype(BF), "seq", 2).astype(F32)
+    parts_3, share_1, total_2 = lax.optimization_barrier((parts_3, share_1, total_2))
+    share_2 = reduce_spans(total_2[0:1], total_2[1:2].astype(BF), (4,))
     share_3 = reduce_spans(*weights(third_kernel, scalars, (*parts_3, *early), ROWS_B, WIN, [(D, WIN)]))
 
     def everywhere(share):

time: 174 us -> 156 us (0.90)
  waiting for transfers between devices: 58.2 us -> 43.5 us
  starting transfers between devices: 53.4 us -> 50 us
    ppermute x40 -> x39, waiting for transfers between devices: 58.2 us -> 43.5 us  [swap(): return lax.ppermute(array, axis, [(i, i ^ bits) for i in range(size)])]
    ppermute x1 -> x0, starting transfers between devices: 2.3 us -> none  [from_behind(): return lax.ppermute(array, axis, pairs)]
    pallas_call x12 -> x14, Pallas kernels: 53.2 us -> 52 us  [call(): pl.pallas_call(kernel, out_shape=outs, grid_spec=pltpu.PrefetchScalarGrid...]
    ppermute x40 -> x39, starting transfers between devices: 51.1 us -> 50 us  [swap(): return lax.ppermute(array, axis, [(i, i ^ bits) for i in range(size)])]
    unnamed x23 -> x29, local copies, waits for them, and re-layouts: 4.51 us -> 5.54 us
  transfers between devices with their start and end apart: 41 -> 39, of which waited for: 17 -> 13; matrix products, arithmetic and copies ran while one was open for 2% -> 1% of each run, Pallas kernels for 22% -> 30%
where the time goes in v2:
time: 156 us
  Pallas kernels  52 us (33%)
  starting transfers between devices  50 us (32%)
  waiting for transfers between devices  43.5 us (28%)
  local copies, waits for them, and re-layouts  7.26 us (5%)
  between operations  1.82 us (1%)
    pallas_call x14, Pallas kernels, call(): pl.pallas_call(kernel, out_shape=outs, grid_spec=pltpu.PrefetchScalarGrid...  52 us
    ppermute x39, starting transfers between devices, swap(): return lax.ppermute(array, axis, [(i, i ^ bits) for i in range(size)])  50 us
    ppermute x39, waiting for transfers between devices, swap(): return lax.ppermute(array, axis, [(i, i ^ bits) for i in range(size)])  43.5 us
    unnamed x29, local copies, waits for them, and re-layouts  5.54 us
  transfers between devices with their start and end apart: 39, of which 13 were waited for; matrix products, arithmetic and copies ran while one was open for 1% of the time, Pallas kernels for 30%

profile of v2, /device:TPU:0, one launch (start us, length us, event | category | flops | bytes accessed | tf_op | source)
XLA Modules:
  0.0 155.7 jit_solution(4781015661468944752)
XLA Ops:
  1.3 0.7 copy.25
  2.1 0.9 copy-done.5
  3.1 0.6 shard_map.170.x_ref
  3.6 0.5 collective-permute-start.2
  4.1 2.6 %collective-permute-start.3 = (bf16[136,768]{1,0:T(8,128)(2,1)S(1)}, bf16[136,768]{1,0:T(8,128)(2,1)S(1)}, u32[]{:S(2)}, u32[]{:S(2)}) collective-permute-start(bf16[136,768]{1,0:T(8,128)(2,1)S(1)} %shard_map.170.x_ref), channel_id=1, source_target_pairs={{0,2},{1,3},{2,0},{3,1},{4,6},{5,7},{6,4},{7,5},{8,10},{9,11},{10,... | collective-permute-start | bytes 626696 | tf_op jit(solution)/shard_map/ppermute | solution.py:754
  6.8 2.6 %collective-permute-start = (bf16[136,768]{1,0:T(8,128)(2,1)S(1)}, bf16[136,768]{1,0:T(8,128)(2,1)S(1)}, u32[]{:S(2)}, u32[]{:S(2)}) collective-permute-start(bf16[136,768]{1,0:T(8,128)(2,1)S(1)} %shard_map.170.x_ref), channel_id=1, source_target_pairs={{0,4},{1,5},{2,6},{3,7},{4,0},{5,1},{6,2},{7,3},{8,12},{9,13},{10,... | collective-permute-start | bytes 626696 | tf_op jit(solution)/shard_map/ppermute | solution.py:754
  9.4 0.7 broadcast_in_dim.12.gain_ref
  10.1 2.0 %copy-done = bf16[768,2304]{1,0:T(8,128)(2,1)S(1)} copy-done((bf16[768,2304]{1,0:T(8,128)(2,1)S(1)}, bf16[768,2304]{1,0:T(8,128)(2,1)}, u32[]{:S(2)}) %copy-start) | copy-done | bytes 3538968
  12.1 0.9 copy-done.3
  13.0 0.8 copy-done.6
  13.8 4.7 %shard_map.171 = (bf16[1536,128]{1,0:T(8,128)(2,1)S(1)}, bf16[128,2304]{1,0:T(8,128)(2,1)S(1)}, f32[128,3072]{1,0:T(8,128)S(1)}, f32[128,3072]{1,0:T(8,128)S(1)}...) custom-call(s32[47]{0:T(128)S(1)} %stack.110.sc, ...), custom_call_target="tpu_custom_call" | custom-call | flops 2000000 | bytes 9000 | tf_op jit(solution)/shard_map/pallas_call | solution.py:111
  18.6 2.5 %shard_map.172 = (f32[7,16,128]{2,1,0:T(8,128)S(1)}, bf16[7,128,768]{2,1,0:T(8,128)(2,1)S(1)}, bf16[7,128,768]{2,1,0:T(8,128)(2,1)S(1)}, bf16[7,128,3072]{2,1,0:...) custom-call(s32[47]{0:T(128)S(1)} %stack.110.sc, bf16[2,136,768]{2,1,0:T(8,128)(2,1)S(1)} %pad_maximum_fusion.3.x_ref, ...), custom_call_target="tpu_custom_call" | custom-call | flops 1200000 | bytes 6300 | tf_op jit(solution)/shard_map/pallas_call | solution.py:111
  21.1 3.6 %collective-permute-done = bf16[136,768]{1,0:T(8,128)(2,1)S(1)} collective-permute-done((bf16[136,768]{1,0:T(8,128)(2,1)S(1)}, bf16[136,768]{1,0:T(8,128)(2,1)S(1)}, u32[]{:S(2)}, u32[]{:S(2)}) %collective-permute-start) | collective-permute-done | bytes 208928 | tf_op jit(solution)/shard_map/ppermute | solution.py:754
  24.9 1.6 collective-permute-start.5
  26.4 1.5 collective-permute-start.6
  27.9 0.5 collective-permute-start.7
  28.6 5.3 %shard_map.173 = (f32[7,16,128]{2,1,0:T(8,128)S(1)}, bf16[7,128,768]{2,1,0:T(8,128)(2,1)S(1)}, bf16[7,128,768]{2,1,0:T(8,128)(2,1)S(1)}, bf16[7,128,3072]{2,1,0:...) custom-call(s32[47]{0:T(128)S(1)} %stack.110.sc, ...), custom_call_target="tpu_custom_call", output_to_operand_aliasing={{0}: (5, {}), {1}: (6, {}), {2}: (7, {}), {3}: (8, {})} | custom-call | flops 3000000 | bytes 10500 | tf_op jit(solution)/shard_map/pallas_call | solution.py:111
  34.0 11.6 %shard_map.174 = (bf16[128,3072]{1,0:T(8,128)(2,1)S(1)}, bf16[128,3072]{1,0:T(8,128)(2,1)S(1)}, bf16[128,768]{1,0:T(8,128)(2,1)S(1)}, bf16[128,768]{1,0:T(8,128)...) custom-call(s32[47]{0:T(128)S(1)} %stack.110.sc, ...), custom_call_target="tpu_custom_call" | custom-call | flops 3500000 | bytes 20000 | tf_op jit(solution)/shard_map/pallas_call | solution.py:111
  45.6 0.4 collective-permute-done.6.e2
  46.0 1.2 shard_map.175
  47.2 1.3 collective-permute-start.8
  48.5 1.4 collective-permute-start.9
  49.9 4.9 %collective-permute-start.12 = (bf16[128,896]{1,0:T(8,128)(2,1)S(1)}, bf16[128,896]{1,0:T(8,128)(2,1)S(1)}, u32[]{:S(2)}, u32[]{:S(2)}) collective-permute-start(bf16[128,896]{1,0:T(8,128)(2,1)S(1)} %get-tuple-element.201), channel_id=1, source_target_pairs={{0,2},{1,3},{2,0},{3,1},{4,6},{5,7},{6,4},{7,5},{8,10},{9,11},{10,... | collective-permute-start | bytes 688136 | tf_op jit(solution)/shard_map/ppermute | solution.py:754
  54.8 3.0 %collective-permute-start.13 = (bf16[128,896]{1,0:T(8,128)(2,1)S(1)}, bf16[128,896]{1,0:T(8,128)(2,1)S(1)}, u32[]{:S(2)}, u32[]{:S(2)}) collective-permute-start(bf16[128,896]{1,0:T(8,128)(2,1)S(1)} %get-tuple-element.201), channel_id=1, source_target_pairs={{0,4},{1,5},{2,6},{3,7},{4,0},{5,1},{6,2},{7,3},{8,12},{9,13},{10,... | collective-permute-start | bytes 688136 | tf_op jit(solution)/shard_map/ppermute | solution.py:754
  57.7 1.5 collective-permute-start.14
  59.2 6.4 %shard_map.176 = (bf16[128,768]{1,0:T(8,128)(2,1)S(1)}, f32[128,768]{1,0:T(8,128)S(1)}, f32[128,768]{1,0:T(8,128)S(1)}, f32[128,3072]{1,0:T(8,128)S(1)}) custom-call(s32[47]{0:T(128)S(1)} %stack.110.sc, s32[12,128]{1,0:T(8,128)S(1)} %bitcast.53, bf16[128,2304]{1,0:T(8,128)(2,1)S(1)} %get-tuple-element.124.qkv_ref, ...), custom_call_target="tpu_custom_call" | custom-call | flops 3000000 | bytes 9000 | tf_op jit(solution)/shard_map/pallas_call | solution.py:111
  65.6 0.5 collective-permute-start.10
  66.2 7.9 %collective-permute-done.13 = bf16[128,896]{1,0:T(8,128)(2,1)S(1)} collective-permute-done((bf16[128,896]{1,0:T(8,128)(2,1)S(1)}, bf16[128,896]{1,0:T(8,128)(2,1)S(1)}, u32[]{:S(2)}, u32[]{:S(2)}) %collective-permute-start.13) | collective-permute-done | bytes 229408 | tf_op jit(solution)/shard_map/ppermute | solution.py:754
  74.3 1.8 %collective-permute-done.10.p3 = bf16[1536,128]{1,0:T(8,128)(2,1)S(1)} collective-permute-done((bf16[1536,128]{1,0:T(8,128)(2,1)S(1)}, bf16[1536,128]{1,0:T(8,128)(2,1)S(1)}, u32[]{:S(2)}, u32[]{:S(2)}) %collective-permute-start.10) | collective-permute-done | bytes 393248 | tf_op jit(solution)/shard_map/ppermute | solution.py:754
  76.1 1.7 %shard_map.177 = (f32[4,120,768]{2,1,0:T(8,128)S(1)}, bf16[4,120,768]{2,1,0:T(8,128)(2,1)S(1)}) custom-call(s32[47]{0:T(128)S(1)} %stack.110.sc, bf16[1536,128]{1,0:T(8,128)(2,1)S(1)} %get-tuple-element.192.p0, bf16[1536,128]{1,0:T(8,128)(2,1)S(1)} %collective-permute-done.8.p1, bf16[1536,128]{1,0:T(8,128)(2,1)S(1)} %collective-permute-done.9.p2, ...), custom_call_target="tpu_custom_call" | custom-call | flops 600000 | bytes 20000000 | tf_op jit(solution)/shard_map/pallas_call | solution.py:111
  78.0 0.6 collective-permute-start.16
  78.6 0.5 collective-permute-start.17
  79.1 2.5 %collective-permute-start.18 = (bf16[1536,128]{1,0:T(8,128)(2,1)S(1)}, bf16[1536,128]{1,0:T(8,128)(2,1)S(1)}, u32[]{:S(2)}, u32[]{:S(2)}) collective-permute-start(bf16[1536,128]{1,0:T(8,128)(2,1)S(1)} %get-tuple-element.216), channel_id=1, source_target_pairs={{0,24},{8,16},{16,8},{24,0},{1,25},{9,17},{17,9},{25,1},{2,26},{10... | collective-permute-start | bytes 1179656 | tf_op jit(solution)/shard_map/ppermute | solution.py:754
  81.7 0.2 convert_add_fusion
  82.0 2.9 %collective-permute-start.22 = (bf16[2,120,768]{2,1,0:T(8,128)(2,1)S(1)}, bf16[2,120,768]{2,1,0:T(8,128)(2,1)S(1)}, u32[]{:S(2)}, u32[]{:S(2)}) collective-permute-start(bf16[2,120,768]{2,1,0:T(8,128)(2,1)S(1)} %slice.105), channel_id=1, source_target_pairs={{0,2},{1,3},{2,0},{3,1},{4,6},{5,7},{6,4},{7,5},{8,10},{9,11},{10,... | collective-permute-start | bytes 1105928 | tf_op jit(solution)/shard_map/ppermute | solution.py:754
  84.8 10.1 %shard_map.178 = (bf16[136,640]{1,0:T(8,128)(2,1)S(1)}, bf16[136,640]{1,0:T(8,128)(2,1)S(1)}, bf16[136,640]{1,0:T(8,128)(2,1)S(1)}, bf16[136,640]{1,0:T(8,128)(2,1)S(1)}, f32[128,768]{1,0:T(8,128)}) custom-call(s32[47]{0:T(128)S(1)} %stack.110.sc, bf16[8,128,896]{2,1,0:T(8,128)(2,1)S(1)} %constant_dynamic-update-slice_fusion.dn_slot.dn_next, ...), custom_call_target="tpu_custom_call" | custom-call | flops 3000000 | bytes 17000 | tf_op jit(solution)/shard_map/pallas_call | solution.py:111
  95.0 3.3 %collective-permute-done.17.p2 = bf16[1536,128]{1,0:T(8,128)(2,1)S(1)} collective-permute-done((bf16[1536,128]{1,0:T(8,128)(2,1)S(1)}, bf16[1536,128]{1,0:T(8,128)(2,1)S(1)}, u32[]{:S(2)}, u32[]{:S(2)}) %collective-permute-start.17) | collective-permute-done | bytes 393248 | tf_op jit(solution)/shard_map/ppermute | solution.py:754
  98.3 1.5 shard_map.179
  99.9 4.3 %collective-permute-start.23 = (bf16[1,120,768]{2,1,0:T(8,128)(2,1)S(1)}, bf16[1,120,768]{2,1,0:T(8,128)(2,1)S(1)}, u32[]{:S(2)}, u32[]{:S(2)}) collective-permute-start(bf16[1,120,768]{2,1,0:T(8,128)(2,1)S(1)} %slice.108), channel_id=1, source_target_pairs={{0,4},{1,5},{2,6},{3,7},{4,0},{5,1},{6,2},{7,3},{8,12},{9,13},{10,... | collective-permute-start | bytes 552968 | tf_op jit(solution)/shard_map/ppermute | solution.py:754
  104.5 1.6 %collective-permute-start.19 = (bf16[136,640]{1,0:T(8,128)(2,1)S(1)}, bf16[136,640]{1,0:T(8,128)(2,1)S(1)}, u32[]{:S(2)}, u32[]{:S(2)}) collective-permute-start(bf16[136,640]{1,0:T(8,128)(2,1)S(1)} %get-tuple-element.218), channel_id=1, source_target_pairs={{0,8},{8,0},{16,24},{24,16},{1,9},{9,1},{17,25},{25,17},{2,10},{10... | collective-permute-start | bytes 522248 | tf_op jit(solution)/shard_map/ppermute | solution.py:754
  106.1 0.5 collective-permute-start.20
  106.6 1.5 collective-permute-start.21
  108.1 5.5 %collective-permute-done.23 = bf16[1,120,768]{2,1,0:T(8,128)(2,1)S(1)} collective-permute-done((bf16[1,120,768]{2,1,0:T(8,128)(2,1)S(1)}, bf16[1,120,768]{2,1,0:T(8,128)(2,1)S(1)}, u32[]{:S(2)}, u32[]{:S(2)}) %collective-permute-start.23) | collective-permute-done | bytes 184352 | tf_op jit(solution)/shard_map/ppermute | solution.py:754
  113.6 3.7 %collective-permute-done.25 = bf16[2,96,768]{2,1,0:T(8,128)(2,1)S(1)} collective-permute-done((bf16[2,96,768]{2,1,0:T(8,128)(2,1)S(1)}, bf16[2,96,768]{2,1,0:T(8,128)(2,1)S(1)}, u32[]{:S(2)}, u32[]{:S(2)}) %collective-permute-start.25) | collective-permute-done | bytes 294944 | tf_op jit(solution)/shard_map/ppermute | solution.py:754
  117.4 1.5 shard_map.180
  119.0 1.9 %collective-permute-done.26 = bf16[4,104,640]{2,1,0:T(8,128)(2,1)S(1)} collective-permute-done((bf16[4,104,640]{2,1,0:T(8,128)(2,1)S(1)}, bf16[4,104,640]{2,1,0:T(8,128)(2,1)S(1)}, u32[]{:S(2)}, u32[]{:S(2)}) %collective-permute-start.26) | collective-permute-done | bytes 532512 | tf_op jit(solution)/shard_map/ppermute | solution.py:754
  121.0 0.4 collective-permute-start.27
  121.4 1.5 collective-permute-start.32
  122.9 0.5 collective-permute-start.33
  123.4 1.5 collective-permute-start.34
  124.9 1.8 %collective-permute-start.35 = (bf16[1,96,768]{2,1,0:T(8,128)(2,1)S(1)}, bf16[1,96,768]{2,1,0:T(8,128)(2,1)S(1)}, u32[]{:S(2)}, u32[]{:S(2)}) collective-permute-start(bf16[1,96,768]{2,1,0:T(8,128)(2,1)S(1)} %slice.109), channel_id=1, source_target_pairs={{0,4},{1,5},{2,6},{3,7},{4,0},{5,1},{6,2},{7,3},{8,12},{9,13},{10,... | collective-permute-start | bytes 442376 | tf_op jit(solution)/shard_map/ppermute | solution.py:754
  126.7 4.7 %collective-permute-done.27 = bf16[2,104,640]{2,1,0:T(8,128)(2,1)S(1)} collective-permute-done((bf16[2,104,640]{2,1,0:T(8,128)(2,1)S(1)}, bf16[2,104,640]{2,1,0:T(8,128)(2,1)S(1)}, u32[]{:S(2)}, u32[]{:S(2)}) %collective-permute-start.27) | collective-permute-done | bytes 266272 | tf_op jit(solution)/shard_map/ppermute | solution.py:754
  131.5 0.2 collective-permute-start.28
  131.7 5.1 %collective-permute-done.35 = bf16[1,96,768]{2,1,0:T(8,128)(2,1)S(1)} collective-permute-done((bf16[1,96,768]{2,1,0:T(8,128)(2,1)S(1)}, bf16[1,96,768]{2,1,0:T(8,128)(2,1)S(1)}, u32[]{:S(2)}, u32[]{:S(2)}) %collective-permute-start.35) | collective-permute-done | bytes 147488 | tf_op jit(solution)/shard_map/ppermute | solution.py:754
  136.8 2.6 %collective-permute-start.36 = (bf16[96,768]{1,0:T(8,128)(2,1)S(1)}, bf16[96,768]{1,0:T(8,128)(2,1)S(1)}, u32[]{:S(2)}, u32[]{:S(2)}) collective-permute-start(bf16[96,768]{1,0:T(8,128)(2,1)S(1)} %fusion.3.refs_0_), channel_id=1, source_target_pairs={{0,8},{8,0},{16,24},{24,16},{1,9},{9,1},{17,25},{25,17},{2,10},{10... | collective-permute-start | bytes 442376 | tf_op jit(solution)/shard_map/ppermute | solution.py:754
  139.6 1.4 collective-permute-start.38
  141.1 2.0 %collective-permute-start.29 = (bf16[104,640]{1,0:T(8,128)(2,1)S(1)}, bf16[104,640]{1,0:T(8,128)(2,1)S(1)}, u32[]{:S(2)}, u32[]{:S(2)}) collective-permute-start(bf16[104,640]{1,0:T(8,128)(2,1)S(1)} %fusion.4.refs_0_), channel_id=1, source_target_pairs={{0,8},{8,0},{16,24},{24,16},{1,9},{9,1},{17,25},{25,17},{2,10},{10... | collective-permute-start | bytes 399368 | tf_op jit(solution)/shard_map/ppermute | solution.py:754
  143.2 1.4 collective-permute-start.31
  144.6 1.8 %shard_map.182 = (f32[384,768]{1,0:T(8,128)}, f32[96,768]{1,0:T(8,128)}) custom-call(s32[47]{0:T(128)S(1)} %stack.110.sc, bf16[120,768]{1,0:T(8,128)(2,1)S(1)} %fusion.2.refs_0_, bf16[120,768]{1,0:T(8,128)(2,1)S(1)} %collective-permute-done.32.refs_1_, bf16[120,768]{1,0:T(8,128)(2,1)S(1)} %collective-permute-done.33.refs_2_, ...), custom_call_target="tpu_custom_call" | custom-call | bytes 2000 | tf_op jit(solution)/shard_map/pallas_call | solution.py:111
  146.4 2.4 %collective-permute-done.37.refs_2_ = bf16[96,768]{1,0:T(8,128)(2,1)S(1)} collective-permute-done((bf16[96,768]{1,0:T(8,128)(2,1)S(1)}, bf16[96,768]{1,0:T(8,128)(2,1)S(1)}, u32[]{:S(2)}, u32[]{:S(2)}) %collective-permute-start.37) | collective-permute-done | bytes 147488 | tf_op jit(solution)/shard_map/ppermute | solution.py:754
  148.9 1.7 %shard_map.183 = f32[96,3072]{1,0:T(8,128)} custom-call(s32[47]{0:T(128)S(1)} %stack.110.sc, bf16[96,768]{1,0:T(8,128)(2,1)S(1)} %fusion.3.refs_0_, bf16[96,768]{1,0:T(8,128)(2,1)S(1)} %collective-permute-done.36.refs_1_, bf16[96,768]{1,0:T(8,128)(2,1)S(1)} %collective-permute-done.37.refs_2_, bf16[96,768]{1,0:T(8,128)(2,1)S(1)} %collective-permute-done.38.refs_3_), custom_call_target="tpu_custom_call" | custom-call | bytes 2000 | tf_op jit(solution)/shard_map/pallas_call | solution.py:111
  150.6 2.9 %collective-permute-done.30.refs_2_ = bf16[104,640]{1,0:T(8,128)(2,1)S(1)} collective-permute-done((bf16[104,640]{1,0:T(8,128)(2,1)S(1)}, bf16[104,640]{1,0:T(8,128)(2,1)S(1)}, u32[]{:S(2)}, u32[]{:S(2)}) %collective-permute-start.30) | collective-permute-done | bytes 133152 | tf_op jit(solution)/shard_map/ppermute | solution.py:754
  153.4 1.6 %shard_map.181 = (f32[96,2304]{1,0:T(8,128)}, f32[8,640]{1,0:T(8,128)S(1)}) custom-call(s32[47]{0:T(128)S(1)} %stack.110.sc, bf16[104,640]{1,0:T(8,128)(2,1)S(1)} %fusion.4.refs_0_, bf16[104,640]{1,0:T(8,128)(2,1)S(1)} %collective-permute-done.29.refs_1_, bf16[104,640]{1,0:T(8,128)(2,1)S(1)} %collective-permute-done.30.refs_2_, ...), custom_call_target="tpu_custom_call" | custom-call | bytes 2000 | tf_op jit(solution)/shard_map/pallas_call | solution.py:111
  155.1 0.5 slice_bitcast_fusion
  (88 shorter events, 2.4 us)
Async XLA Ops:
  2.1 0.9 copy-start.5
  3.6 14.9 %collective-permute-start.2 = (bf16[136,768]{1,0:T(8,128)(2,1)S(1)}, bf16[136,768]{1,0:T(8,128)(2,1)S(1)}, u32[]{:S(2)}, u32[]{:S(2)}) collective-permute-start(bf16[136,768]{1,0:T(8,128)(2,1)S(1)} %shard_map.170.x_ref), channel_id=1, source_target_pairs={{0,1},{1,0},{2,3},{3,2},{4,5},{5,4},{6,7},{7,6},{8,9},{9,8},{10,11... | collective-permute-start | bytes 626696 | tf_op jit(solution)/shard_map/ppermute | solution.py:754
  4.1 14.4 %collective-permute-start.3 = (bf16[136,768]{1,0:T(8,128)(2,1)S(1)}, bf16[136,768]{1,0:T(8,128)(2,1)S(1)}, u32[]{:S(2)}, u32[]{:S(2)}) collective-permute-start(bf16[136,768]{1,0:T(8,128)(2,1)S(1)} %shard_map.170.x_ref), channel_id=1, source_target_pairs={{0,2},{1,3},{2,0},{3,1},{4,6},{5,7},{6,4},{7,5},{8,10},{9,11},{10,... | collective-permute-start | bytes 626696 | tf_op jit(solution)/shard_map/ppermute | solution.py:754
  6.8 17.9 %collective-permute-start = (bf16[136,768]{1,0:T(8,128)(2,1)S(1)}, bf16[136,768]{1,0:T(8,128)(2,1)S(1)}, u32[]{:S(2)}, u32[]{:S(2)}) collective-permute-start(bf16[136,768]{1,0:T(8,128)(2,1)S(1)} %shard_map.170.x_ref), channel_id=1, source_target_pairs={{0,4},{1,5},{2,6},{3,7},{4,0},{5,1},{6,2},{7,3},{8,12},{9,13},{10,... | collective-permute-start | bytes 626696 | tf_op jit(solution)/shard_map/ppermute | solution.py:754
  9.4 15.3 %collective-permute-start.1 = (bf16[136,768]{1,0:T(8,128)(2,1)S(1)}, bf16[136,768]{1,0:T(8,128)(2,1)S(1)}, u32[]{:S(2)}, u32[]{:S(2)}) collective-permute-start(bf16[136,768]{1,0:T(8,128)(2,1)S(1)} %shard_map.170.x_ref), channel_id=1, source_target_pairs={{0,6},{1,7},{2,4},{3,5},{4,2},{5,3},{6,0},{7,1},{8,14},{9,15},{10,... | collective-permute-start | bytes 626696 | tf_op jit(solution)/shard_map/ppermute | solution.py:754
  10.1 2.0 %copy-start = (bf16[768,2304]{1,0:T(8,128)(2,1)S(1)}, bf16[768,2304]{1,0:T(8,128)(2,1)}, u32[]{:S(2)}) copy-start(bf16[768,2304]{1,0:T(8,128)(2,1)} %w_ref.7) | copy-start | bytes 10616836
  12.1 0.9 copy-start.3
  13.0 0.8 copy-start.6
  13.8 4.7 %copy-start.1 = (bf16[768,2304]{1,0:T(8,128)(2,1)S(1)}, bf16[768,2304]{1,0:T(8,128)(2,1)}, u32[]{:S(2)}) copy-start(bf16[768,2304]{1,0:T(8,128)(2,1)} %w_ref.7) | copy-start | bytes 10616836
  18.6 9.8 %copy-start.7 = (f32[768]{0:T(1024)S(1)}, f32[768]{0:T(1024)}, u32[]{:S(2)}) copy-start(f32[768]{0:T(1024)} %param.18) | copy-start | bytes 9220
  24.8 3.6 %collective-permute-start.4 = (bf16[3,136,768]{2,1,0:T(8,128)(2,1)S(1)}, bf16[3,136,768]{2,1,0:T(8,128)(2,1)S(1)}, u32[]{:S(2)}, u32[]{:S(2)}) collective-permute-start(bf16[3,136,768]{2,1,0:T(8,128)(2,1)S(1)} %pad_maximum_fusion.2), channel_id=1, source_target_pairs={{0,1},{1,0},{2,3},{3,2},{4,5},{5,4},{6,7},{7,6},{8,9},{9,8},{10,11... | collective-permute-start | bytes 1880072 | tf_op jit(solution)/shard_map/ppermute | solution.py:754
  24.9 20.7 %collective-permute-start.5 = (bf16[1536,128]{1,0:T(8,128)(2,1)S(1)}, bf16[1536,128]{1,0:T(8,128)(2,1)S(1)}, u32[]{:S(2)}, u32[]{:S(2)}) collective-permute-start(bf16[1536,128]{1,0:T(8,128)(2,1)S(1)} %get-tuple-element.165.e0), channel_id=1, source_target_pairs={{0,8},{8,0},{16,24},{24,16},{1,9},{9,1},{17,25},{25,17},{2,10},{10... | collective-permute-start | bytes 1179656 | tf_op jit(solution)/shard_map/ppermute | solution.py:754
  26.4 19.6 %collective-permute-start.6 = (bf16[1536,128]{1,0:T(8,128)(2,1)S(1)}, bf16[1536,128]{1,0:T(8,128)(2,1)S(1)}, u32[]{:S(2)}, u32[]{:S(2)}) collective-permute-start(bf16[1536,128]{1,0:T(8,128)(2,1)S(1)} %get-tuple-element.165.e0), channel_id=1, source_target_pairs={{0,16},{8,24},{16,0},{24,8},{1,17},{9,25},{17,1},{25,9},{2,18},{10... | collective-permute-start | bytes 1179656 | tf_op jit(solution)/shard_map/ppermute | solution.py:754
  27.9 18.1 %collective-permute-start.7 = (bf16[1536,128]{1,0:T(8,128)(2,1)S(1)}, bf16[1536,128]{1,0:T(8,128)(2,1)S(1)}, u32[]{:S(2)}, u32[]{:S(2)}) collective-permute-start(bf16[1536,128]{1,0:T(8,128)(2,1)S(1)} %get-tuple-element.165.e0), channel_id=1, source_target_pairs={{0,24},{8,16},{16,8},{24,0},{1,25},{9,17},{17,9},{25,1},{2,26},{10... | collective-permute-start | bytes 1179656 | tf_op jit(solution)/shard_map/ppermute | solution.py:754
  28.4 5.5 %slice-start = ((s8[4718592]{0:T(1024)(128)(4,1)}), s8[4194304]{0:T(1024)(128)(4,1)S(1)}, s32[]{:S(2)}) async-start(s8[4718592]{0:T(1024)(128)(4,1)} %bitcast.43), calls=%async_computation | async-start | bytes 8388608
  28.4 5.5 %slice-start.2 = ((s8[4718592]{0:T(1024)(128)(4,1)}), s8[4194304]{0:T(1024)(128)(4,1)S(1)}, s32[]{:S(2)}) async-start(s8[4718592]{0:T(1024)(128)(4,1)} %bitcast.45), calls=%async_computation.2 | async-start | bytes 8388608
  28.6 5.4 %slice-start.1 = ((s8[4718592]{0:T(1024)(128)(4,1)}), s8[524288]{0:T(1024)(128)(4,1)S(1)}, s32[]{:S(2)}) async-start(s8[4718592]{0:T(1024)(128)(4,1)} %bitcast.43), calls=%async_computation.1 | async-start | bytes 1048576
  28.6 5.4 %slice-start.3 = ((s8[4718592]{0:T(1024)(128)(4,1)}), s8[524288]{0:T(1024)(128)(4,1)S(1)}, s32[]{:S(2)}) async-start(s8[4718592]{0:T(1024)(128)(4,1)} %bitcast.45), calls=%async_computation.3 | async-start | bytes 1048576
  28.6 5.4 %copy-start.2 = (bf16[768,768]{1,0:T(8,128)(2,1)S(1)}, bf16[768,768]{1,0:T(8,128)(2,1)}, u32[]{:S(2)}) copy-start(bf16[768,768]{1,0:T(8,128)(2,1)} %wo_ref.1) | copy-start | bytes 3538948
  28.6 5.3 %copy-start.4 = (bf16[1,128,768]{2,1,0:T(8,128)(2,1)S(1)}, bf16[1,128,768]{2,1,0:T(8,128)(2,1)}, u32[]{:S(2)}) copy-start(bf16[1,128,768]{2,1,0:T(8,128)(2,1)} %param.21) | copy-start | bytes 589828
  47.2 18.4 %collective-permute-start.8 = (bf16[1536,128]{1,0:T(8,128)(2,1)S(1)}, bf16[1536,128]{1,0:T(8,128)(2,1)S(1)}, u32[]{:S(2)}, u32[]{:S(2)}) collective-permute-start(bf16[1536,128]{1,0:T(8,128)(2,1)S(1)} %get-tuple-element.173), channel_id=1, source_target_pairs={{0,8},{8,0},{16,24},{24,16},{1,9},{9,1},{17,25},{25,17},{2,10},{10... | collective-permute-start | bytes 1179656 | tf_op jit(solution)/shard_map/ppermute | solution.py:754
  48.5 17.1 %collective-permute-start.9 = (bf16[1536,128]{1,0:T(8,128)(2,1)S(1)}, bf16[1536,128]{1,0:T(8,128)(2,1)S(1)}, u32[]{:S(2)}, u32[]{:S(2)}) collective-permute-start(bf16[1536,128]{1,0:T(8,128)(2,1)S(1)} %get-tuple-element.174), channel_id=1, source_target_pairs={{0,16},{8,24},{16,0},{24,8},{1,17},{9,25},{17,1},{25,9},{2,18},{10... | collective-permute-start | bytes 1179656 | tf_op jit(solution)/shard_map/ppermute | solution.py:754
  49.9 16.3 %collective-permute-start.12 = (bf16[128,896]{1,0:T(8,128)(2,1)S(1)}, bf16[128,896]{1,0:T(8,128)(2,1)S(1)}, u32[]{:S(2)}, u32[]{:S(2)}) collective-permute-start(bf16[128,896]{1,0:T(8,128)(2,1)S(1)} %get-tuple-element.201), channel_id=1, source_target_pairs={{0,2},{1,3},{2,0},{3,1},{4,6},{5,7},{6,4},{7,5},{8,10},{9,11},{10,... | collective-permute-start | bytes 688136 | tf_op jit(solution)/shard_map/ppermute | solution.py:754
  54.8 19.3 %collective-permute-start.13 = (bf16[128,896]{1,0:T(8,128)(2,1)S(1)}, bf16[128,896]{1,0:T(8,128)(2,1)S(1)}, u32[]{:S(2)}, u32[]{:S(2)}) collective-permute-start(bf16[128,896]{1,0:T(8,128)(2,1)S(1)} %get-tuple-element.201), channel_id=1, source_target_pairs={{0,4},{1,5},{2,6},{3,7},{4,0},{5,1},{6,2},{7,3},{8,12},{9,13},{10,... | collective-permute-start | bytes 688136 | tf_op jit(solution)/shard_map/ppermute | solution.py:754
  57.7 16.4 %collective-permute-start.14 = (bf16[128,896]{1,0:T(8,128)(2,1)S(1)}, bf16[128,896]{1,0:T(8,128)(2,1)S(1)}, u32[]{:S(2)}, u32[]{:S(2)}) collective-permute-start(bf16[128,896]{1,0:T(8,128)(2,1)S(1)} %get-tuple-element.201), channel_id=1, source_target_pairs={{0,6},{1,7},{2,4},{3,5},{4,2},{5,3},{6,0},{7,1},{8,14},{9,15},{10,... | collective-permute-start | bytes 688136 | tf_op jit(solution)/shard_map/ppermute | solution.py:754
  65.6 10.5 %collective-permute-start.10 = (bf16[1536,128]{1,0:T(8,128)(2,1)S(1)}, bf16[1536,128]{1,0:T(8,128)(2,1)S(1)}, u32[]{:S(2)}, u32[]{:S(2)}) collective-permute-start(bf16[1536,128]{1,0:T(8,128)(2,1)S(1)} %get-tuple-element.187), channel_id=1, source_target_pairs={{0,24},{8,16},{16,8},{24,0},{1,25},{9,17},{17,9},{25,1},{2,26},{10... | collective-permute-start | bytes 1179656 | tf_op jit(solution)/shard_map/ppermute | solution.py:754
  74.2 7.3 %collective-permute-start.15 = (bf16[4,128,896]{2,1,0:T(8,128)(2,1)S(1)}, bf16[4,128,896]{2,1,0:T(8,128)(2,1)S(1)}, u32[]{:S(2)}, u32[]{:S(2)}) collective-permute-start(bf16[4,128,896]{2,1,0:T(8,128)(2,1)S(1)} %pad_maximum_fusion.1), channel_id=1, source_target_pairs={{0,1},{1,0},{2,3},{3,2},{4,5},{5,4},{6,7},{7,6},{8,9},{9,8},{10,11... | collective-permute-start | bytes 2752520 | tf_op jit(solution)/shard_map/ppermute | solution.py:754
  77.8 3.9 %collective-permute-start.11 = (bf16[4,120,768]{2,1,0:T(8,128)(2,1)S(1)}, bf16[4,120,768]{2,1,0:T(8,128)(2,1)S(1)}, u32[]{:S(2)}, u32[]{:S(2)}) collective-permute-start(bf16[4,120,768]{2,1,0:T(8,128)(2,1)S(1)} %get-tuple-element.200), channel_id=1, source_target_pairs={{0,1},{1,0},{2,3},{3,2},{4,5},{5,4},{6,7},{7,6},{8,9},{9,8},{10,11... | collective-permute-start | bytes 2211848 | tf_op jit(solution)/shard_map/ppermute | solution.py:754
  78.0 16.9 %collective-permute-start.16 = (bf16[1536,128]{1,0:T(8,128)(2,1)S(1)}, bf16[1536,128]{1,0:T(8,128)(2,1)S(1)}, u32[]{:S(2)}, u32[]{:S(2)}) collective-permute-start(bf16[1536,128]{1,0:T(8,128)(2,1)S(1)} %get-tuple-element.214), channel_id=1, source_target_pairs={{0,8},{8,0},{16,24},{24,16},{1,9},{9,1},{17,25},{25,17},{2,10},{10... | collective-permute-start | bytes 1179656 | tf_op jit(solution)/shard_map/ppermute | solution.py:754
  78.6 19.7 %collective-permute-start.17 = (bf16[1536,128]{1,0:T(8,128)(2,1)S(1)}, bf16[1536,128]{1,0:T(8,128)(2,1)S(1)}, u32[]{:S(2)}, u32[]{:S(2)}) collective-permute-start(bf16[1536,128]{1,0:T(8,128)(2,1)S(1)} %get-tuple-element.215), channel_id=1, source_target_pairs={{0,16},{8,24},{16,0},{24,8},{1,17},{9,25},{17,1},{25,9},{2,18},{10... | collective-permute-start | bytes 1179656 | tf_op jit(solution)/shard_map/ppermute | solution.py:754
  79.1 19.2 %collective-permute-start.18 = (bf16[1536,128]{1,0:T(8,128)(2,1)S(1)}, bf16[1536,128]{1,0:T(8,128)(2,1)S(1)}, u32[]{:S(2)}, u32[]{:S(2)}) collective-permute-start(bf16[1536,128]{1,0:T(8,128)(2,1)S(1)} %get-tuple-element.216), channel_id=1, source_target_pairs={{0,24},{8,16},{16,8},{24,0},{1,25},{9,17},{17,9},{25,1},{2,26},{10... | collective-permute-start | bytes 1179656 | tf_op jit(solution)/shard_map/ppermute | solution.py:754
  82.0 17.9 %collective-permute-start.22 = (bf16[2,120,768]{2,1,0:T(8,128)(2,1)S(1)}, bf16[2,120,768]{2,1,0:T(8,128)(2,1)S(1)}, u32[]{:S(2)}, u32[]{:S(2)}) collective-permute-start(bf16[2,120,768]{2,1,0:T(8,128)(2,1)S(1)} %slice.105), channel_id=1, source_target_pairs={{0,2},{1,3},{2,0},{3,1},{4,6},{5,7},{6,4},{7,5},{8,10},{9,11},{10,... | collective-permute-start | bytes 1105928 | tf_op jit(solution)/shard_map/ppermute | solution.py:754
  99.7 4.5 %collective-permute-start.24 = (bf16[4,96,768]{2,1,0:T(8,128)(2,1)S(1)}, bf16[4,96,768]{2,1,0:T(8,128)(2,1)S(1)}, u32[]{:S(2)}, u32[]{:S(2)}) collective-permute-start(bf16[4,96,768]{2,1,0:T(8,128)(2,1)S(1)} %get-tuple-element.227), channel_id=1, source_target_pairs={{0,1},{1,0},{2,3},{3,2},{4,5},{5,4},{6,7},{7,6},{8,9},{9,8},{10,11... | collective-permute-start | bytes 1769480 | tf_op jit(solution)/shard_map/ppermute | solution.py:754
  99.9 13.6 %collective-permute-start.23 = (bf16[1,120,768]{2,1,0:T(8,128)(2,1)S(1)}, bf16[1,120,768]{2,1,0:T(8,128)(2,1)S(1)}, u32[]{:S(2)}, u32[]{:S(2)}) collective-permute-start(bf16[1,120,768]{2,1,0:T(8,128)(2,1)S(1)} %slice.108), channel_id=1, source_target_pairs={{0,4},{1,5},{2,6},{3,7},{4,0},{5,1},{6,2},{7,3},{8,12},{9,13},{10,... | collective-permute-start | bytes 552968 | tf_op jit(solution)/shard_map/ppermute | solution.py:754
  104.4 12.9 %collective-permute-start.25 = (bf16[2,96,768]{2,1,0:T(8,128)(2,1)S(1)}, bf16[2,96,768]{2,1,0:T(8,128)(2,1)S(1)}, u32[]{:S(2)}, u32[]{:S(2)}) collective-permute-start(bf16[2,96,768]{2,1,0:T(8,128)(2,1)S(1)} %slice.106), channel_id=1, source_target_pairs={{0,2},{1,3},{2,0},{3,1},{4,6},{5,7},{6,4},{7,5},{8,10},{9,11},{10,... | collective-permute-start | bytes 884744 | tf_op jit(solution)/shard_map/ppermute | solution.py:754
  104.5 12.9 %collective-permute-start.19 = (bf16[136,640]{1,0:T(8,128)(2,1)S(1)}, bf16[136,640]{1,0:T(8,128)(2,1)S(1)}, u32[]{:S(2)}, u32[]{:S(2)}) collective-permute-start(bf16[136,640]{1,0:T(8,128)(2,1)S(1)} %get-tuple-element.218), channel_id=1, source_target_pairs={{0,8},{8,0},{16,24},{24,16},{1,9},{9,1},{17,25},{25,17},{2,10},{10... | collective-permute-start | bytes 522248 | tf_op jit(solution)/shard_map/ppermute | solution.py:754
  106.1 11.3 %collective-permute-start.20 = (bf16[136,640]{1,0:T(8,128)(2,1)S(1)}, bf16[136,640]{1,0:T(8,128)(2,1)S(1)}, u32[]{:S(2)}, u32[]{:S(2)}) collective-permute-start(bf16[136,640]{1,0:T(8,128)(2,1)S(1)} %get-tuple-element.219), channel_id=1, source_target_pairs={{0,16},{8,24},{16,0},{24,8},{1,17},{9,25},{17,1},{25,9},{2,18},{10... | collective-permute-start | bytes 522248 | tf_op jit(solution)/shard_map/ppermute | solution.py:754
  106.6 10.8 %collective-permute-start.21 = (bf16[136,640]{1,0:T(8,128)(2,1)S(1)}, bf16[136,640]{1,0:T(8,128)(2,1)S(1)}, u32[]{:S(2)}, u32[]{:S(2)}) collective-permute-start(bf16[136,640]{1,0:T(8,128)(2,1)S(1)} %get-tuple-element.220), channel_id=1, source_target_pairs={{0,24},{8,16},{16,8},{24,0},{1,25},{9,17},{17,9},{25,1},{2,26},{10... | collective-permute-start | bytes 522248 | tf_op jit(solution)/shard_map/ppermute | solution.py:754
  118.9 2.0 %collective-permute-start.26 = (bf16[4,104,640]{2,1,0:T(8,128)(2,1)S(1)}, bf16[4,104,640]{2,1,0:T(8,128)(2,1)S(1)}, u32[]{:S(2)}, u32[]{:S(2)}) collective-permute-start(bf16[4,104,640]{2,1,0:T(8,128)(2,1)S(1)} %get-tuple-element.233), channel_id=1, source_target_pairs={{0,1},{1,0},{2,3},{3,2},{4,5},{5,4},{6,7},{7,6},{8,9},{9,8},{10,11... | collective-permute-start | bytes 1597448 | tf_op jit(solution)/shard_map/ppermute | solution.py:754
  121.0 10.3 %collective-permute-start.27 = (bf16[2,104,640]{2,1,0:T(8,128)(2,1)S(1)}, bf16[2,104,640]{2,1,0:T(8,128)(2,1)S(1)}, u32[]{:S(2)}, u32[]{:S(2)}) collective-permute-start(bf16[2,104,640]{2,1,0:T(8,128)(2,1)S(1)} %slice.107), channel_id=1, source_target_pairs={{0,2},{1,3},{2,0},{3,1},{4,6},{5,7},{6,4},{7,5},{8,10},{9,11},{10,... | collective-permute-start | bytes 798728 | tf_op jit(solution)/shard_map/ppermute | solution.py:754
  121.4 18.0 %collective-permute-start.32 = (bf16[120,768]{1,0:T(8,128)(2,1)S(1)}, bf16[120,768]{1,0:T(8,128)(2,1)S(1)}, u32[]{:S(2)}, u32[]{:S(2)}) collective-permute-start(bf16[120,768]{1,0:T(8,128)(2,1)S(1)} %fusion.2.refs_0_), channel_id=1, source_target_pairs={{0,8},{8,0},{16,24},{24,16},{1,9},{9,1},{17,25},{25,17},{2,10},{10... | collective-permute-start | bytes 552968 | tf_op jit(solution)/shard_map/ppermute | solution.py:754
  122.9 18.1 %collective-permute-start.33 = (bf16[120,768]{1,0:T(8,128)(2,1)S(1)}, bf16[120,768]{1,0:T(8,128)(2,1)S(1)}, u32[]{:S(2)}, u32[]{:S(2)}) collective-permute-start(bf16[120,768]{1,0:T(8,128)(2,1)S(1)} %fusion.2.refs_0_), channel_id=1, source_target_pairs={{0,16},{8,24},{16,0},{24,8},{1,17},{9,25},{17,1},{25,9},{2,18},{10... | collective-permute-start | bytes 552968 | tf_op jit(solution)/shard_map/ppermute | solution.py:754
  123.4 19.6 %collective-permute-start.34 = (bf16[120,768]{1,0:T(8,128)(2,1)S(1)}, bf16[120,768]{1,0:T(8,128)(2,1)S(1)}, u32[]{:S(2)}, u32[]{:S(2)}) collective-permute-start(bf16[120,768]{1,0:T(8,128)(2,1)S(1)} %fusion.2.refs_0_), channel_id=1, source_target_pairs={{0,24},{8,16},{16,8},{24,0},{1,25},{9,17},{17,9},{25,1},{2,26},{10... | collective-permute-start | bytes 552968 | tf_op jit(solution)/shard_map/ppermute | solution.py:754
  124.9 11.8 %collective-permute-start.35 = (bf16[1,96,768]{2,1,0:T(8,128)(2,1)S(1)}, bf16[1,96,768]{2,1,0:T(8,128)(2,1)S(1)}, u32[]{:S(2)}, u32[]{:S(2)}) collective-permute-start(bf16[1,96,768]{2,1,0:T(8,128)(2,1)S(1)} %slice.109), channel_id=1, source_target_pairs={{0,4},{1,5},{2,6},{3,7},{4,0},{5,1},{6,2},{7,3},{8,12},{9,13},{10,... | collective-permute-start | bytes 442376 | tf_op jit(solution)/shard_map/ppermute | solution.py:754
  131.5 8.1 %collective-permute-start.28 = (bf16[1,104,640]{2,1,0:T(8,128)(2,1)S(1)}, bf16[1,104,640]{2,1,0:T(8,128)(2,1)S(1)}, u32[]{:S(2)}, u32[]{:S(2)}) collective-permute-start(bf16[1,104,640]{2,1,0:T(8,128)(2,1)S(1)} %slice.110), channel_id=1, source_target_pairs={{0,4},{1,5},{2,6},{3,7},{4,0},{5,1},{6,2},{7,3},{8,12},{9,13},{10,... | collective-permute-start | bytes 399368 | tf_op jit(solution)/shard_map/ppermute | solution.py:754
  136.8 6.4 %collective-permute-start.36 = (bf16[96,768]{1,0:T(8,128)(2,1)S(1)}, bf16[96,768]{1,0:T(8,128)(2,1)S(1)}, u32[]{:S(2)}, u32[]{:S(2)}) collective-permute-start(bf16[96,768]{1,0:T(8,128)(2,1)S(1)} %fusion.3.refs_0_), channel_id=1, source_target_pairs={{0,8},{8,0},{16,24},{24,16},{1,9},{9,1},{17,25},{25,17},{2,10},{10... | collective-permute-start | bytes 442376 | tf_op jit(solution)/shard_map/ppermute | solution.py:754
  139.4 9.4 %collective-permute-start.37 = (bf16[96,768]{1,0:T(8,128)(2,1)S(1)}, bf16[96,768]{1,0:T(8,128)(2,1)S(1)}, u32[]{:S(2)}, u32[]{:S(2)}) collective-permute-start(bf16[96,768]{1,0:T(8,128)(2,1)S(1)} %fusion.3.refs_0_), channel_id=1, source_target_pairs={{0,16},{8,24},{16,0},{24,8},{1,17},{9,25},{17,1},{25,9},{2,18},{10... | collective-permute-start | bytes 442376 | tf_op jit(solution)/shard_map/ppermute | solution.py:754
  139.6 9.3 %collective-permute-start.38 = (bf16[96,768]{1,0:T(8,128)(2,1)S(1)}, bf16[96,768]{1,0:T(8,128)(2,1)S(1)}, u32[]{:S(2)}, u32[]{:S(2)}) collective-permute-start(bf16[96,768]{1,0:T(8,128)(2,1)S(1)} %fusion.3.refs_0_), channel_id=1, source_target_pairs={{0,24},{8,16},{16,8},{24,0},{1,25},{9,17},{17,9},{25,1},{2,26},{10... | collective-permute-start | bytes 442376 | tf_op jit(solution)/shard_map/ppermute | solution.py:754
  141.1 9.5 %collective-permute-start.29 = (bf16[104,640]{1,0:T(8,128)(2,1)S(1)}, bf16[104,640]{1,0:T(8,128)(2,1)S(1)}, u32[]{:S(2)}, u32[]{:S(2)}) collective-permute-start(bf16[104,640]{1,0:T(8,128)(2,1)S(1)} %fusion.4.refs_0_), channel_id=1, source_target_pairs={{0,8},{8,0},{16,24},{24,16},{1,9},{9,1},{17,25},{25,17},{2,10},{10... | collective-permute-start | bytes 399368 | tf_op jit(solution)/shard_map/ppermute | solution.py:754
  143.0 10.4 %collective-permute-start.30 = (bf16[104,640]{1,0:T(8,128)(2,1)S(1)}, bf16[104,640]{1,0:T(8,128)(2,1)S(1)}, u32[]{:S(2)}, u32[]{:S(2)}) collective-permute-start(bf16[104,640]{1,0:T(8,128)(2,1)S(1)} %fusion.4.refs_0_), channel_id=1, source_target_pairs={{0,16},{8,24},{16,0},{24,8},{1,17},{9,25},{17,1},{25,9},{2,18},{10... | collective-permute-start | bytes 399368 | tf_op jit(solution)/shard_map/ppermute | solution.py:754
  143.2 10.2 %collective-permute-start.31 = (bf16[104,640]{1,0:T(8,128)(2,1)S(1)}, bf16[104,640]{1,0:T(8,128)(2,1)S(1)}, u32[]{:S(2)}, u32[]{:S(2)}) collective-permute-start(bf16[104,640]{1,0:T(8,128)(2,1)S(1)} %fusion.4.refs_0_), channel_id=1, source_target_pairs={{0,24},{8,16},{16,8},{24,0},{1,25},{9,17},{17,9},{25,1},{2,26},{10... | collective-permute-start | bytes 399368 | tf_op jit(solution)/shard_map/ppermute | solution.py:754

commit v3 on v2

--- a/solution.py
+++ b/solution.py
@@ -23,6 +23,7 @@
 ROWS_2 = 96
 ROWS_B = 104
 MIB = 1 << 20
+AFTER = {'b1': ['d4', 'a2'], 'b2': ['a2', 'a3', 'd4'], 'W2': ['L'], 'p1': ['b1', 'b2', 'b3', 'a1', 'a2', 'a3'], 'p2': ['b1', 'b3', 'd2', 'b2'], 'p3': ['b2', 'd2', 'b1'], 'W3': ['t1'], 'L': ['W1', 'a1', 'a2', 'r1', 'E'], 'h1': ['t2', 'g1', 'g2', 'g3', 's3', 'W3'], 'h2': ['t2', 'g1', 'g2', 'g3', 's3', 'p2', 'W3'], 'h3': ['g2', 'g3', 'W3'], 'W1': ['d4', 'd2'], 't2': ['r3', 'r2', 'b1', 'p3'], 's1': ['W1', 'a1', 'a2', 'OB'], 'g2': ['L', 'W2'], 'i1': ['g3', 't3'], 'i2': ['g3', 't3', 'r3', 't1', 'W3'], 'S3': ['g2', 'g3', 'S2'], 'i3': ['W3'], 'a2': ['E'], 'r2': ['r1'], 'r3': ['b1', 'b2', 'b3'], 'a1': ['E'], 'a3': ['E'], 'late': []}
 
 
 def nn(a, b):
@@ -66,7 +67,10 @@
 
 
 def phi_pair(pair, proj):
-    linear = nn(lanes(pair, pair), proj)
+    return phi_of(pair, nn(lanes(pair, pair), proj))
+
+
+def phi_of(pair, linear):
     wide = pair.astype(F32)
     square = wide * wide
     first = iota(square.shape, 1) < HD
@@ -139,24 +143,24 @@
     return jnp.concatenate([lanes(high, none), lanes(none, high), lanes(low, none), lanes(none, low)], 0)
 
 
-def pack_kernel(sc, x_ref, tag_ref, out_ref):
+def pack_kernel(sc, x_ref, tag_ref, out_ref, tags_ref):
     out_ref[0:T, :] = x_ref[...]
-    tags = tag_ref[...].astype(F32)
-    wide = [lanes(*[tags[h : h + 1, :] for h in range(6 * r, 6 * r + 6)]) for r in range(2)]
+    rows = [tag_ref[h].astype(F32) for h in range(H)]
+    wide = [lanes(*rows[6 * r : 6 * r + 6]) for r in range(2)]
     out_ref[T : T + 8, :] = jnp.concatenate(wide + [jnp.zeros((6, D), F32)], 0).astype(BF)
+    tags_ref[...] = jnp.concatenate(rows + [jnp.zeros((4, T), F32)], 0)
 
 
 def packed(scalars, own, tags):
-    out = sds((T + 8, D), BF)
+    outs = (sds((T + 8, D), BF), sds((16, T), F32))
     return call(
-        pack_kernel, scalars, (own, tags), [whole(own.shape), whole(tags.shape)], out, whole(out.shape), (1,),
-        vmem=2,
+        pack_kernel, scalars, (own, tags), [whole(own.shape), whole(tags.shape)], outs,
+        [whole(o.shape) for o in outs], (1,), vmem=2,
     )
 
 
 def tag_pair(ref):
-    rows = jnp.concatenate([ref[...].astype(F32), jnp.zeros((4, T), F32)], 0)
-    return rows, rows.T
+    return ref[...], ref[...].T
 
 
 def own_kernel(
@@ -216,7 +220,8 @@
 def others_kernel(begin, sc, x_ref, gain_ref, w_ref, proj_ref, *refs):
     tags_ref, u_ref, v_ref, phi_ref, sums_ref, norms_ref = refs[-6:]
     slot = pl.program_id(0)
-    span = sc[8 + begin + slot]
+    at = begin + slot
+    span = sc[8 + at]
 
     @pl.when(slot == 0)
     def _():
@@ -226,37 +231,38 @@
             sums_ref[...] = jnp.zeros_like(sums_ref)
             norms_ref[...] = jnp.zeros_like(norms_ref)
 
-    unit, _ = norm_parts(x_ref[0, 0:T, :].astype(F32))
-    wide = x_ref[0, T : T + 8, :].astype(F32)
+    unit, _ = norm_parts(x_ref[slot, 0:T, :].astype(F32))
+    wide = x_ref[slot, T : T + 8, :].astype(F32)
     rows = [wide[h // 6 : h // 6 + 1, 128 * (h % 6) : 128 * (h % 6) + 128] for h in range(H)]
-    tags_ref[0] = jnp.concatenate(rows + [jnp.zeros((4, 128), F32)], 0)
+    tags_ref[at] = jnp.concatenate(rows + [jnp.zeros((4, 128), F32)], 0)
     low = (unit * gain_ref[...]).astype(BF)
     earlier = span < sc[0]
     offset = pl.multiple_of(jnp.where(earlier, D, 0), D)
-    u_ref[0] = nn(low, w_ref[:, pl.ds(offset, D)]).astype(BF)
-    proj = proj_ref[...]
+    u_ref[at] = nn(low, w_ref[:, pl.ds(offset, D)]).astype(BF)
+    pairs = [u_ref[at, :, 128 * p : 128 * p + 128] for p in range(PAIRS)]
+    linear = nn(jnp.concatenate([lanes(a, a) for a in pairs], 0), proj_ref[...])
     for p in range(PAIRS):
-        phis = phi_pair(u_ref[0, :, 128 * p : 128 * p + 128], proj)
+        phis = phi_of(pairs[p], linear[T * p : T * p + T])
         for half in range(2):
             h = 2 * p + half
-            phi_ref[0, :, M * h : M * h + M] = phis[half].astype(BF)
+            phi_ref[at, :, M * h : M * h + M] = phis[half].astype(BF)
 
     @pl.when(earlier)
     def _():
         value = nn(low, w_ref[:, 2 * D : 3 * D])
-        v_ref[0] = value.astype(BF)
-        valid = iota((D, T), 1) + span * T < sc[1]
-        turned = jnp.where(valid, value.T, 0.0).astype(BF)
+        v_ref[at] = value.astype(BF)
+        valid = iota((T, 1), 0) + span * T < sc[1]
+        turned = jnp.where(valid, value, 0.0).T.astype(BF)
+        ones = jnp.where(iota((16, T), 1) + span * T < sc[1], 1.0, 0.0).astype(BF)
         for h in range(H):
-            sums_ref[HD * h : HD * h + HD, :] += nn(
-                turned[HD * h : HD * h + HD, :], phi_ref[0, :, M * h : M * h + M]
-            )
-        ones = jnp.where(iota((8, T), 1) + span * T < sc[1], 1.0, 0.0).astype(BF)
-        norms_ref[...] += nn(ones, phi_ref[0])
+            hm = slice(M * h, M * h + M)
+            total = nn(jnp.concatenate([turned[HD * h : HD * h + HD, :], ones], 0), phi_ref[at, :, hm])
+            sums_ref[HD * h : HD * h + HD, :] += total[0:HD]
+            norms_ref[:, hm] += total[HD : HD + 8]
 
     @pl.when(~earlier)
     def _():
-        v_ref[0] = jnp.zeros((T, D), BF)
+        v_ref[at] = jnp.zeros((T, D), BF)
 
 
 def others_forward(scalars, begin, pieces, gain, qkv_weight, proj, so_far=()):
@@ -265,24 +271,17 @@
         sds((spans, 16, T), F32), sds((spans, T, D), BF), sds((spans, T, D), BF), sds((spans, T, HM), BF),
         sds((D, M), F32), sds((8, HM), F32),
     )
-    step = lambda i, sc: (begin + i, 0, 0)
-    specs = [pl.BlockSpec((1, T + 8, D), lambda i, sc: (i, 0, 0))]
-    specs += [whole(a.shape) for a in (gain, qkv_weight, proj)]
-    aliases = {}
-    if so_far:
-        specs += [pl.BlockSpec(memory_space=pl.ANY)] * 4 + [whole(a.shape) for a in so_far[4:]]
-        aliases = {5: 0, 6: 1, 7: 2, 8: 3}
+    args = (pieces, gain, qkv_weight, proj, *so_far)
     return call(
-        functools.partial(others_kernel, begin), scalars, (pieces, gain, qkv_weight, proj, *so_far), specs,
-        outs,
-        [pl.BlockSpec((1, 16, T), step), pl.BlockSpec((1, T, D), step), pl.BlockSpec((1, T, D), step),
-         pl.BlockSpec((1, T, HM), step), whole((D, M)), whole((8, HM))],
-        (count,), vmem=8, flops=count * 600_000_000, size=count * 1_400_000 + 3_500_000, aliases=aliases,
-    )
-
-
-def own_cols(tags_ref):
-    return tag_pair(tags_ref)[1].astype(BF)
+        functools.partial(others_kernel, begin), scalars, args, [whole(a.shape) for a in args], outs,
+        [whole(o.shape) for o in outs], (count,), vmem=8, flops=0, size=0,
+        aliases={5: 0, 6: 1, 7: 2, 8: 3} if so_far else {},
+    )
+
+
+def rows_of(wide, begin):
+    rows = [wide[begin + h // 6 : begin + h // 6 + 1, 128 * (h % 6) : 128 * (h % 6) + 128] for h in range(H)]
+    return jnp.concatenate(rows + [jnp.zeros((4, 128), F32)], 0)
 
 
 def middle_kernel(
@@ -291,14 +290,14 @@
     hid_ref, pre_ref, nm_ref, att_ref, out_ref, dmid_ref, dn_low_ref, dn_ref, dd_ref, expo_ref, blend_ref, gain_out,
     mid_s, nm_s, acc_s, dnm_s, num_s, den_s,
 ):
-    step = pl.program_id(0)
+    step, prev_at = pl.program_id(0), sc[2]
     first = iota((T, 128), 1) < HD
     valid = iota((T, 1), 0) + sc[0] * T < sc[1]
 
     @pl.when(step == 0)
     def _():
         _, own = tag_pair(tags_ref)
-        prev = tags_prev[0]
+        prev = tags_prev[prev_at]
         prev_tag = [prev[h : h + 1, EDGE:T] for h in range(H)]
         edge_first = iota((EDGE, 128), 1) < HD
         edge_ok = (sc[4] > 0) & (iota((EDGE, EDGE), 1) + (sc[0] * T - EDGE) < sc[1])
@@ -308,7 +307,7 @@
             at = slice(128 * p, 128 * p + 128)
             high, lowp = split(sums_ref[at, :])
             query = qkv_ref[0:EDGE, at]
-            key, value = up_prev[0, :, at], vp_prev[0, :, at]
+            key, value = up_prev[prev_at, EDGE:T, at], vp_prev[prev_at, EDGE:T, at]
             nums = []
             for half in range(2):
                 h = 2 * p + half
@@ -317,7 +316,7 @@
                 total = nt(phi_q, high) + nt(phi_q, lowp)
                 den = jnp.sum(phi_q.astype(F32) * norms_ref[0:1, hm], -1, keepdims=True)
                 expo = jnp.exp(nt(masked(edge_first, half, query), key) * HD**-0.5)
-                approx = nt(phi_q[0:EDGE], phi_prev[0, :, hm])
+                approx = nt(phi_q[0:EDGE], phi_prev[prev_at, EDGE:T, hm])
                 matched = edge_ok & (own[0:EDGE, h : h + 1] == prev_tag[h])
                 blend = jnp.where(matched, expo - approx, 0.0)
                 expo_ref[h] = jnp.where(matched, expo, 0.0)
@@ -358,8 +357,9 @@
     hidden_low = hidden.astype(BF)
     acc_s[...] += nn(hidden_low, wdown_ref[...])
     dnm_s[...] += nt(grad_pre, wup_ref[...])
-    hid_ref[...] = hidden_low
-    pre_ref[...] = grad_pre
+    cols = pl.ds(pl.multiple_of(D * step, D), D)
+    hid_ref[:, cols] = hidden_low
+    pre_ref[:, cols] = grad_pre
 
     @pl.when(step == 3)
     def _():
@@ -379,35 +379,29 @@
             den = jnp.where(first, dens[:, 2 * p : 2 * p + 1], dens[:, 2 * p + 1 : 2 * p + 2])
             dnum = jnp.where(valid, datt[:, at] / den, 0.0)
             dn_ref[:, at] = dnum
-            dn_low_ref[:, at] = dnum.astype(BF)
+            dn_low_ref[0:T, at] = dnum.astype(BF)
             prod = dnum * num_s[:, at]
             for half in range(2):
                 h = 2 * p + half
                 total = jnp.sum(masked(first, half, prod), -1, keepdims=True)
                 ddens = columns_to(ddens, h, -total / dens[:, h : h + 1])
         dd_ref[...] = ddens
-        dn_low_ref[:, D : D + 16] = ddens[:, 0:16].astype(BF)
-        dn_low_ref[:, D + 16 : D + 32] = own_cols(tags_ref)
-        dn_low_ref[:, D + 32 : D + 128] = jnp.zeros((T, 96), BF)
+        ends, tags = ddens.T, tag_pair(tags_ref)[0]
+        wide = [lanes(*[a[h : h + 1, :] for h in range(b, b + 6)]) for a in (ends, tags) for b in (0, 6)]
+        dn_low_ref[T : T + 8, :] = jnp.concatenate(wide + [jnp.zeros((4, D), F32)], 0).astype(BF)
 
 
 def middle(scalars, own, qkv, phi_q, sums, norms, num, den, tags, others, gain, wo, wup, wdown, cot):
     tags_all, u, v, phi = others
-    prev = lambda i, sc: (sc[2], 1, 0)
     outs = (
         sds((T, 4 * D), BF), sds((T, 4 * D), BF), sds((T, D), BF), sds((T, D), BF),
-        sds((T, D), BF), sds((T, D), F32), sds((T, D + 128), BF),
+        sds((T, D), BF), sds((T, D), F32), sds((T + 8, D), BF),
         sds((T, D), F32), sds((T, 128), F32), sds((H, EDGE, EDGE), F32), sds((H, EDGE, EDGE), BF),
         sds((8, D), F32),
     )
     args = (own, qkv, phi_q, sums, norms, num, den, tags, tags_all, u, v, phi, gain, wo, wup, wdown, cot)
-    specs = [whole(a.shape) for a in args[:8]] + [
-        pl.BlockSpec((1, 16, T), lambda i, sc: (sc[2], 0, 0)),
-        pl.BlockSpec((1, EDGE, D), prev), pl.BlockSpec((1, EDGE, D), prev),
-        pl.BlockSpec((1, EDGE, HM), prev),
-        whole(gain.shape), whole(wo.shape),
-        pl.BlockSpec((D, D), lambda i, sc: (0, i)), pl.BlockSpec((D, D), lambda i, sc: (i, 0)),
-        whole(cot.shape),
+    specs = [whole(a.shape) for a in args[:14]] + [
+        pl.BlockSpec((D, D), lambda i, sc: (0, i)), pl.BlockSpec((D, D), lambda i, sc: (i, 0)), whole(cot.shape),
     ]
     scratch = [
         pltpu.VMEM((T, D), F32), pltpu.VMEM((T, D), BF), pltpu.VMEM((T, D), F32),
@@ -415,7 +409,7 @@
     ]
     return call(
         middle_kernel, scalars, args, specs, outs,
-        [pl.BlockSpec((T, D), lambda i, sc: (0, i))] * 2 + [whole(o.shape) for o in outs[2:]], (4,), scratch,
+        [whole(o.shape) for o in outs], (4,), scratch,
         vmem=12, flops=3_500_000_000, size=20_000_000,
     )
 
@@ -459,11 +453,12 @@
     sums_ref, norms_ref, tags_prev, up_prev, vp_prev, phi_prev, expo_e, blend_e,
     dq_ref, dk_ref, dv_ref, dphi_ref,
 ):
+    prev_at = sc[2]
     rows, cols = tag_pair(tags_ref)
     first = iota((T, 128), 1) < HD
     query_at, key_at = iota((T, T), 0), iota((T, T), 1)
     allowed = (key_at <= query_at) & (key_at + sc[0] * T < sc[1])
-    prev_tag = tags_prev[0]
+    prev_tag = tags_prev[prev_at]
     edge_first = iota((EDGE, 128), 1) < HD
     edge_ok = (sc[4] > 0) & (iota((EDGE, EDGE), 1) + (sc[0] * T - EDGE) < sc[1])
     proj = proj_ref[...]
@@ -472,7 +467,7 @@
         query, key, value = (
             qkv_ref[:, part * D + 128 * p : part * D + 128 * p + 128] for part in range(3)
         )
-        key_e, value_e = up_prev[0, :, at], vp_prev[0, :, at]
+        key_e, value_e = up_prev[prev_at, EDGE:T, at], vp_prev[prev_at, EDGE:T, at]
         high, low = split(dn_ref[:, at])
         both = lanes(high, low)
         s_high, s_low = split(sums_ref[at, :])
@@ -501,7 +496,7 @@
             da_e = jnp.where(matched_e, -edge, 0.0).astype(BF)
             dqs.append(dq + jnp.concatenate([nn(ds_e, key_e), jnp.zeros((EDGE, 128), F32)], 0))
             grads.append(
-                dphi + jnp.concatenate([nn(da_e, phi_prev[0, :, hm]), jnp.zeros((EDGE, M), F32)], 0)
+                dphi + jnp.concatenate([nn(da_e, phi_prev[prev_at, EDGE:T, hm]), jnp.zeros((EDGE, M), F32)], 0)
             )
             phis.append(phi_q)
         dq_ref[:, at] = (pick(first, dqs) + phi_back(query, grads, phis, proj)).astype(BF)
@@ -511,17 +506,11 @@
 
 def own_back(scalars, tags, qkv, phi_q, phi_k, proj, expo, blend, dnum, dden, sums, norms, others, expo_e, blend_e):
     tags_all, u, v, phi = others
-    prev = lambda i, sc: (sc[2], 1, 0)
     args = (
         tags, qkv, phi_q, phi_k, proj, expo, blend, dnum, dden, sums, norms, tags_all, u, v, phi, expo_e,
         blend_e,
     )
-    specs = [whole(a.shape) for a in args[:11]] + [
-        pl.BlockSpec((1, 16, T), lambda i, sc: (sc[2], 0, 0)),
-        pl.BlockSpec((1, EDGE, D), prev), pl.BlockSpec((1, EDGE, D), prev),
-        pl.BlockSpec((1, EDGE, HM), prev),
-        whole(expo_e.shape), whole(blend_e.shape),
-    ]
+    specs = [whole(a.shape) for a in args]
     outs = (sds((T, D), BF), sds((T, D), F32), sds((T, D), F32), sds((T, HM), F32))
     return call(
         own_back_kernel, scalars, args, specs, outs, [whole(o.shape) for o in outs], (1,),
@@ -530,8 +519,8 @@
 
 
 def last_kernel(
-    sc, dn_slot, phi_slot, x_ref, tags_ref, qkv_ref, phik_ref, proj_ref, dq_ref, dk_ref, dv_ref, dphi_ref,
-    u_next, phi_next, dn_next, dmid_ref, gain_ref, w_ref, gmlp_ref,
+    sc, dn_ref, phi_ref, x_ref, tags_ref, qkv_ref, phik_ref, proj_ref, dq_ref, dk_ref, dv_ref, dphi_ref,
+    u_ref, dmid_ref, gain_ref, w_ref, gmlp_ref,
     a0, a1, a2, a3, grad_ref, sums_s, norms_s, dqkv_s,
 ):
     slot = pl.program_id(0)
@@ -544,29 +533,33 @@
 
     @pl.when(span > sc[0])
     def _():
-        turned = dn_slot[0].astype(F32).T.astype(BF)
+        turned = dn_ref[slot + 1, 0:T, :].astype(F32).T.astype(BF)
+        ends = rows_of(dn_ref[slot + 1, T : T + 8, :].astype(F32), 0).astype(BF)
         for h in range(H):
             hm = slice(M * h, M * h + M)
-            sums_s[HD * h : HD * h + HD, :] += nn(turned[HD * h : HD * h + HD, :], phi_slot[0, :, hm])
-        norms_s[...] += nn(turned[D : D + 16, :], phi_slot[0])
+            total = nn(
+                jnp.concatenate([turned[HD * h : HD * h + HD, :], ends], 0), phi_ref[sc[40 + slot], :, hm]
+            )
+            sums_s[HD * h : HD * h + HD, :] += total[0:HD]
+            norms_s[:, hm] += total[HD : HD + 16]
 
     @pl.when(slot == pl.num_programs(0) - 1)
     def _():
-        me = sc[6]
+        me, next_at, dn_at = sc[6], sc[3], sc[7]
         rows = tags_ref[...].astype(F32)
-        next_cols = dn_next[0, :, D + 16 : D + 32].astype(F32)
+        next_cols = rows_of(dn_ref[dn_at, T : T + 8, :].astype(F32), 2).T
         first = iota((T, 128), 1) < HD
         edge_first = iota((EDGE, 128), 1) < HD
         valid = iota((T, 1), 0) + sc[0] * T < sc[1]
         edge_ok = (sc[5] > 0) & (iota((EDGE, EDGE), 1) + (sc[0] * T + EDGE) < sc[1])
         proj = proj_ref[...]
-        ddn = dn_next[0, :, D : D + 128].astype(F32)
+        ddn = rows_of(dn_ref[dn_at, T : T + 8, :].astype(F32), 0).T[0:EDGE]
         dqkv_s[:, 0:D] = dq_ref[...]
         for p in range(PAIRS):
             at = slice(128 * p, 128 * p + 128)
             key, value = (qkv_ref[:, part * D + 128 * p : part * D + 128 * p + 128] for part in (1, 2))
             high, low = split(sums_s[at, :])
-            query_n, dnum_n = u_next[0, :, at], dn_next[0, :, at]
+            query_n, dnum_n = u_ref[next_at, 0:EDGE, at], dn_ref[dn_at, 0:EDGE, at]
             grads, phis, dks, dvs = [], [], [], []
             for half in range(2):
                 h = 2 * p + half
@@ -577,7 +570,7 @@
                 carry = nn(mine, high) + nn(mine, low) + norms_s[h : h + 1, hm]
                 dv = nt(phi_kb, high) + nt(phi_kb, low)
                 q_h, d_h = masked(edge_first, half, query_n), masked(edge_first, half, dnum_n)
-                phi_n = phi_next[0, :, hm]
+                phi_n = phi_ref[next_at, 0:EDGE, hm]
                 expo = jnp.exp(nt(q_h, key[EDGE:]) * HD**-0.5)
                 approx = nt(phi_n, phi_kb[EDGE:])
                 matched = edge_ok & (next_cols[0:EDGE, h : h + 1] == rows[h : h + 1, EDGE:128])
@@ -618,20 +611,10 @@
 def last(scalars, dn_pieces, others, own, tags, qkv, phi_k, proj, dq, dk, dv, dphi, dmid, gain, qkv_weight, gmlp):
     _, u, v, phi = others
     count = dn_pieces.shape[0] - 1
-    follow = lambda i, sc: (sc[3], 0, 0)
     args = (
-        dn_pieces, phi, own, tags, qkv, phi_k, proj, dq, dk, dv, dphi, u, phi, dn_pieces, dmid, gain,
-        qkv_weight, gmlp,
-    )
-    specs = [
-        pl.BlockSpec((1, T, D + 128), lambda i, sc: (i + 1, 0, 0)),
-        pl.BlockSpec((1, T, HM), lambda i, sc: (sc[40 + i], 0, 0)),
-    ]
-    specs += [whole(a.shape) for a in args[2:11]]
-    specs += [
-        pl.BlockSpec((1, EDGE, D), follow), pl.BlockSpec((1, EDGE, HM), follow),
-        pl.BlockSpec((1, EDGE, D + 128), lambda i, sc: (sc[7], 0, 0)),
-    ] + [whole(a.shape) for a in args[14:]]
+        dn_pieces, phi, own, tags, qkv, phi_k, proj, dq, dk, dv, dphi, u, dmid, gain, qkv_weight, gmlp,
+    )
+    specs = [whole(a.shape) for a in args]
     outs = tuple([sds((T + 8, WIN), BF)] * 4) + (sds((T, D), F32),)
     return call(
         last_kernel, scalars, args, specs, outs, [whole(o.shape) for o in outs], (count,),
@@ -788,8 +771,7 @@
     own, cot = tokens[0], cotangent[0]
     gain_in, gain_mid = attn_gain[None], mlp_gain[None]
 
-    tags = buckets[0]
-    own = packed(scalars, own, tags)
+    own, tags = packed(scalars, own, jnp.transpose(buckets, (1, 0, 2)))
     mate, near, far_a, far_b = (swap(own, "seq", bits) for bits in (1, 2, 4, 6))
     early, qkv, phi_q, phi_k, expo, blend, num, den, proj = own_forward(
         scalars, own, gain_in, qkv_weight, feature_proj, cot, tags
@@ -812,43 +794,86 @@
     results, early_parts = lax.optimization_barrier((results, early_parts))
     early = (early, *early_parts)
     layer_out, dmid, dn_low, dnum, dden, expo_e, blend_e, gmlp = results[4:]
-    pays = exchange(scalars, *results[0:4], dmid)
-    pay_1, pay_2 = pays[0:4], pays[4:8]
-    dn_far = [swap(dn_low, "seq", bits) for bits in (2, 4, 6)]
-    parts_1 = [pay_1[0], swap(pay_1[1], "dp", 1), swap(pay_1[2], "dp", 2)]
-    dq, dk, dv, dphi = own_back(
-        scalars, tags, qkv, phi_q, phi_k, proj, expo, blend, dnum, dden, sums, norms, others,
-        expo_e, blend_e,
-    )
-    parts_1, last_1, dk = lax.optimization_barrier((parts_1, pay_1[3], dk))
-    parts_1.append(swap(last_1, "dp", 3))
-    dn_half = jnp.stack([dn_low, *dn_far])
-    dn_pieces = jnp.concatenate([dn_half, swap(dn_half, "seq", 1)], 0)
-    parts_1, pay_2 = lax.optimization_barrier((parts_1, pay_2))
-    parts_2 = [pay_2[0]] + [swap(pay_2[k], "dp", k) for k in (1, 2, 3)]
-    keep, send = weights(first_kernel, scalars, (*parts_1, *early), ROWS_1, D, [(D, D), (384, 384)])
-    total_1 = keep + swap(send, "seq", 1).astype(F32)
-    total_1, dn_pieces = lax.optimization_barrier((total_1, dn_pieces))
-    *pay_3, grad_tokens = last(
-        scalars, dn_pieces, others, own, tags, qkv, phi_k, proj, dq, dk, dv, dphi, dmid, gain_in,
-        qkv_weight, gmlp,
-    )
-    pay_3, parts_2 = lax.optimization_barrier((pay_3, parts_2))
-    share_1 = reduce_spans(total_1[0:2], total_1[2:4].astype(BF), (2, 4))
-    parts_3 = [pay_3[0]] + [swap(pay_3[k], "dp", k) for k in (1, 2, 3)]
-    keep, send = weights(second_kernel, scalars, parts_2, ROWS_2, D, [(D, D)])
-    total_2 = keep + swap(send, "seq", 1).astype(F32)
-    total_2 = total_2[0:2] + swap(total_2[2:4].astype(BF), "seq", 2).astype(F32)
-    parts_3, share_1, total_2 = lax.optimization_barrier((parts_3, share_1, total_2))
-    share_2 = reduce_spans(total_2[0:1], total_2[1:2].astype(BF), (4,))
-    share_3 = reduce_spans(*weights(third_kernel, scalars, (*parts_3, *early), ROWS_B, WIN, [(D, WIN)]))
-
-    def everywhere(share):
-        return [share] + [swap(share, "dp", k) for k in (1, 2, 3)]
-
-    down, out = spread(fill_first, scalars, everywhere(share_1), [(384, D), (96, D)])
-    (up,) = spread(fill_second, scalars, everywhere(share_2), [(96, 4 * D)])
-    grad_qkv, gains = spread(fill_third, scalars, everywhere(share_3), [(96, 3 * D), (8, WIN)])
+    made = {}
+
+    def after(node, value):
+        needs = [made[n] for n in AFTER.get(node, ()) if n in made]
+        return lax.optimization_barrier((value, needs))[0] if needs else value
+
+    def move(node, value, axis, bits):
+        made[node] = swap(after(node, value), axis, bits)
+        return made[node]
+
+    def run(node, work, value, *rest):
+        made[node] = work(after(node, value), *rest)
+        return made[node]
+
+    def around(node, four):
+        return [four[0]] + [move(node + str(k), four[k], "dp", k) for k in (1, 2, 3)]
+
+    dn_4, dn_6 = (move("d" + str(bits), dn_low, "seq", bits) for bits in (4, 6))
+    pays = run("E", lambda a: exchange(scalars, *results[0:3], a, dmid), results[3])
+    halves = run(
+        "OB",
+        lambda a: own_back(
+            scalars, tags, qkv, phi_q, phi_k, proj, expo, blend, dnum, a, sums, norms, others, expo_e, blend_e
+        ),
+        dden,
+    )
+    parts_1 = around("a", pays[0:4])
+    dn_half = jnp.stack([dn_low, move("d2", dn_low, "seq", 2), dn_4, dn_6])
+    dn_pieces = jnp.concatenate([dn_half, move("c", dn_half, "seq", 1)], 0)
+    parts_2 = around("b", pays[4:8])
+
+    def first_weights():
+        return run(
+            "W1",
+            lambda a: weights(
+                first_kernel, scalars, (a, *parts_1[1:], *early), ROWS_1, D, [(D, D), (384, 384)]
+            ),
+            parts_1[0],
+        )
+
+    if "late" not in AFTER:
+        keep_1, send_1 = first_weights()
+        total_1 = keep_1 + move("r1", send_1, "seq", 1).astype(F32)
+    *pay_3, grad_tokens = run(
+        "L",
+        lambda a: last(
+            scalars, dn_pieces, others, own, tags, qkv, phi_k, proj, *halves, dmid, gain_in, qkv_weight, a
+        ),
+        gmlp,
+    )
+    if "late" in AFTER:
+        keep_1, send_1 = first_weights()
+        total_1 = keep_1 + move("r1", send_1, "seq", 1).astype(F32)
+    total_1 = total_1[0:2] + move("s1", total_1[2:4].astype(BF), "seq", 2).astype(F32)
+    parts_3 = around("p", pay_3)
+    share_1 = (total_1[0] + move("t1", total_1[1].astype(BF), "seq", 4).astype(F32)).astype(BF)
+    keep_2, send_2 = run(
+        "W2", lambda a: weights(second_kernel, scalars, (a, *parts_2[1:]), ROWS_2, D, [(D, D)]), parts_2[0]
+    )
+    total_2 = keep_2 + move("r2", send_2, "seq", 1).astype(F32)
+    total_2 = total_2[0:2] + move("s2", total_2[2:4].astype(BF), "seq", 2).astype(F32)
+    keep_3, send_3 = run(
+        "W3",
+        lambda a: weights(third_kernel, scalars, (a, *parts_3[1:], *early), ROWS_B, WIN, [(D, WIN)]),
+        parts_3[0],
+    )
+    total_3 = keep_3 + move("r3", send_3, "seq", 1).astype(F32)
+    share_2 = (total_2[0] + move("t2", total_2[1].astype(BF), "seq", 4).astype(F32)).astype(BF)
+    total_3 = total_3[0:2] + move("s3", total_3[2:4].astype(BF), "seq", 2).astype(F32)
+    parts_1 = around("g", [share_1] * 4)
+    share_3 = (total_3[0] + move("t3", total_3[1].astype(BF), "seq", 4).astype(F32)).astype(BF)
+    parts_2 = around("h", [share_2] * 4)
+    parts_3 = around("i", [share_3] * 4)
+    down, out = run(
+        "S1", lambda a: spread(fill_first, scalars, [a, *parts_1[1:]], [(384, D), (96, D)]), parts_1[0]
+    )
+    (up,) = run("S2", lambda a: spread(fill_second, scalars, [a, *parts_2[1:]], [(96, 4 * D)]), parts_2[0])
+    grad_qkv, gains = run(
+        "S3", lambda a: spread(fill_third, scalars, [a, *parts_3[1:]], [(96, 3 * D), (8, WIN)]), parts_3[0]
+    )
     gains = gains[0:4].reshape(2, 2 * WIN)[:, 0:D]
     mine = lax.dynamic_slice_in_dim(gains, seq * 96, 96, 1)
     return (

time: 156 us -> 145 us (0.929)
  waiting for transfers between devices: 43.5 us -> 31 us
  starting transfers between devices: 50 us -> 52 us
    ppermute x39, waiting for transfers between devices: 43.5 us -> 31 us  [swap(): return lax.ppermute(array, axis, [(i, i ^ bits) for i in range(size)])]
    ppermute x39, starting transfers between devices: 50 us -> 52 us  [swap(): return lax.ppermute(array, axis, [(i, i ^ bits) for i in range(size)])]
    unnamed x29 -> x30, local copies, waits for them, and re-layouts: 5.54 us -> 5.5 us
  transfers between devices with their start and end apart: 39 -> 39, of which waited for: 13 -> 10; matrix products, arithmetic and copies ran while one was open for 1% -> 1% of each run, Pallas kernels for 30% -> 33%
where the time goes in v3:
time: 145 us; the launch traced here: 144 us
  starting transfers between devices  52 us (36%)
  Pallas kernels  51.3 us (35%)
  waiting for transfers between devices  31 us (21%)
  local copies, waits for them, and re-layouts  7.15 us (5%)
  between operations  1.82 us (1%)
    ppermute x39, starting transfers between devices, swap(): return lax.ppermute(array, axis, [(i, i ^ bits) for i in range(size)])  52 us
    pallas_call x14, Pallas kernels, call(): pl.pallas_call(kernel, out_shape=outs, grid_spec=pltpu.PrefetchScalarGrid...  51.3 us
    ppermute x39, waiting for transfers between devices, swap(): return lax.ppermute(array, axis, [(i, i ^ bits) for i in range(size)])  31 us
    unnamed x30, local copies, waits for them, and re-layouts  5.5 us
  transfers between devices with their start and end apart: 39, of which 10 were waited for; matrix products, arithmetic and copies ran while one was open for 1% of the time, Pallas kernels for 33%

profile of v3, /device:TPU:0, one launch (start us, length us, event | category | flops | bytes accessed | tf_op | source)
XLA Modules:
  0.0 144.3 jit_solution(13014586393929474422)
XLA Ops:
  1.3 0.1 stack.110.sc
  1.5 0.9 copy-done.5
  2.4 0.7 copy-done.7
  3.1 0.6 shard_map.170
  3.6 0.5 collective-permute-start.2
  4.2 2.6 %collective-permute-start.3 = (bf16[136,768]{1,0:T(8,128)(2,1)S(1)}, bf16[136,768]{1,0:T(8,128)(2,1)S(1)}, u32[]{:S(2)}, u32[]{:S(2)}) collective-permute-start(bf16[136,768]{1,0:T(8,128)(2,1)S(1)} %get-tuple-element.121.x_ref), channel_id=1, source_target_pairs={{0,2},{1,3},{2,0},{3,1},{4,6},{5,7},{6,4},{7,5},{8,10},{9,11},{10,... | collective-permute-start | bytes 626696 | tf_op jit(solution)/shard_map/ppermute | solution.py:737
  6.8 2.6 %collective-permute-start = (bf16[136,768]{1,0:T(8,128)(2,1)S(1)}, bf16[136,768]{1,0:T(8,128)(2,1)S(1)}, u32[]{:S(2)}, u32[]{:S(2)}) collective-permute-start(bf16[136,768]{1,0:T(8,128)(2,1)S(1)} %get-tuple-element.121.x_ref), channel_id=1, source_target_pairs={{0,4},{1,5},{2,6},{3,7},{4,0},{5,1},{6,2},{7,3},{8,12},{9,13},{10,... | collective-permute-start | bytes 626696 | tf_op jit(solution)/shard_map/ppermute | solution.py:737
  9.4 0.7 broadcast_in_dim.12.gain_ref
  10.1 2.0 %copy-done = bf16[768,2304]{1,0:T(8,128)(2,1)S(1)} copy-done((bf16[768,2304]{1,0:T(8,128)(2,1)S(1)}, bf16[768,2304]{1,0:T(8,128)(2,1)}, u32[]{:S(2)}) %copy-start) | copy-done | bytes 3538968
  12.1 0.9 copy-done.3
  13.0 0.8 copy-done.6
  13.9 4.6 %shard_map.171 = (bf16[1536,128]{1,0:T(8,128)(2,1)S(1)}, bf16[128,2304]{1,0:T(8,128)(2,1)S(1)}, f32[128,3072]{1,0:T(8,128)S(1)}, f32[128,3072]{1,0:T(8,128)S(1)}...) custom-call(s32[47]{0:T(128)S(1)} %stack.110.sc, ...), custom_call_target="tpu_custom_call" | custom-call | flops 2000000 | bytes 9000 | tf_op jit(solution)/shard_map/pallas_call | solution.py:115
  18.6 2.4 %shard_map.172 = (f32[7,16,128]{2,1,0:T(8,128)S(1)}, bf16[7,128,768]{2,1,0:T(8,128)(2,1)S(1)}, bf16[7,128,768]{2,1,0:T(8,128)(2,1)S(1)}, bf16[7,128,3072]{2,1,0:...) custom-call(s32[47]{0:T(128)S(1)} %stack.110.sc, bf16[2,136,768]{2,1,0:T(8,128)(2,1)S(1)} %pad_maximum_fusion.3.x_ref, ...), custom_call_target="tpu_custom_call" | custom-call | tf_op jit(solution)/shard_map/pallas_call | solution.py:115
  21.0 3.7 %collective-permute-done = bf16[136,768]{1,0:T(8,128)(2,1)S(1)} collective-permute-done((bf16[136,768]{1,0:T(8,128)(2,1)S(1)}, bf16[136,768]{1,0:T(8,128)(2,1)S(1)}, u32[]{:S(2)}, u32[]{:S(2)}) %collective-permute-start) | collective-permute-done | bytes 208928 | tf_op jit(solution)/shard_map/ppermute | solution.py:737
  24.9 1.6 %collective-permute-start.5 = (bf16[1536,128]{1,0:T(8,128)(2,1)S(1)}, bf16[1536,128]{1,0:T(8,128)(2,1)S(1)}, u32[]{:S(2)}, u32[]{:S(2)}) collective-permute-start(bf16[1536,128]{1,0:T(8,128)(2,1)S(1)} %get-tuple-element.164.e0), channel_id=1, source_target_pairs={{0,8},{8,0},{16,24},{24,16},{1,9},{9,1},{17,25},{25,17},{2,10},{10... | collective-permute-start | bytes 1179656 | tf_op jit(solution)/shard_map/ppermute | solution.py:737
  26.4 1.5 %collective-permute-start.6 = (bf16[1536,128]{1,0:T(8,128)(2,1)S(1)}, bf16[1536,128]{1,0:T(8,128)(2,1)S(1)}, u32[]{:S(2)}, u32[]{:S(2)}) collective-permute-start(bf16[1536,128]{1,0:T(8,128)(2,1)S(1)} %get-tuple-element.164.e0), channel_id=1, source_target_pairs={{0,16},{8,24},{16,0},{24,8},{1,17},{9,25},{17,1},{25,9},{2,18},{10... | collective-permute-start | bytes 1179656 | tf_op jit(solution)/shard_map/ppermute | solution.py:737
  27.9 0.5 collective-permute-start.7
  28.6 5.1 %shard_map.173 = (f32[7,16,128]{2,1,0:T(8,128)S(1)}, bf16[7,128,768]{2,1,0:T(8,128)(2,1)S(1)}, bf16[7,128,768]{2,1,0:T(8,128)(2,1)S(1)}, bf16[7,128,3072]{2,1,0:...) custom-call(s32[47]{0:T(128)S(1)} %stack.110.sc, ...), custom_call_target="tpu_custom_call", output_to_operand_aliasing={{0}: (5, {}), {1}: (6, {}), {2}: (7, {}), {3}: (8, {})} | custom-call | tf_op jit(solution)/shard_map/pallas_call | solution.py:115
  33.8 11.4 %shard_map.174 = (bf16[128,3072]{1,0:T(8,128)(2,1)S(1)}, bf16[128,3072]{1,0:T(8,128)(2,1)S(1)}, bf16[128,768]{1,0:T(8,128)(2,1)S(1)}, bf16[128,768]{1,0:T(8,128)...) custom-call(s32[47]{0:T(128)S(1)} %stack.110.sc, ...), custom_call_target="tpu_custom_call" | custom-call | flops 3500000 | bytes 20000 | tf_op jit(solution)/shard_map/pallas_call | solution.py:115
  45.2 0.8 collective-permute-done.6.e2
  46.0 1.2 shard_map.176
  47.2 1.6 %collective-permute-start.13 = (bf16[1536,128]{1,0:T(8,128)(2,1)S(1)}, bf16[1536,128]{1,0:T(8,128)(2,1)S(1)}, u32[]{:S(2)}, u32[]{:S(2)}) collective-permute-start(bf16[1536,128]{1,0:T(8,128)(2,1)S(1)} %get-tuple-element.193), channel_id=1, source_target_pairs={{0,16},{8,24},{16,0},{24,8},{1,17},{9,25},{17,1},{25,9},{2,18},{10... | collective-permute-start | bytes 1179656 | tf_op jit(solution)/shard_map/ppermute | solution.py:737
  48.8 0.7 collective-permute-start.12
  49.5 1.3 collective-permute-start.14
  50.8 4.3 %collective-permute-start.8 = (bf16[136,768]{1,0:T(8,128)(2,1)S(1)}, bf16[136,768]{1,0:T(8,128)(2,1)S(1)}, u32[]{:S(2)}, u32[]{:S(2)}) collective-permute-start(bf16[136,768]{1,0:T(8,128)(2,1)S(1)} %get-tuple-element.166), channel_id=1, source_target_pairs={{0,2},{1,3},{2,0},{3,1},{4,6},{5,7},{6,4},{7,5},{8,10},{9,11},{10,... | collective-permute-start | bytes 626696 | tf_op jit(solution)/shard_map/ppermute | solution.py:737
  55.0 2.6 %collective-permute-start.9 = (bf16[136,768]{1,0:T(8,128)(2,1)S(1)}, bf16[136,768]{1,0:T(8,128)(2,1)S(1)}, u32[]{:S(2)}, u32[]{:S(2)}) collective-permute-start(bf16[136,768]{1,0:T(8,128)(2,1)S(1)} %get-tuple-element.166), channel_id=1, source_target_pairs={{0,4},{1,5},{2,6},{3,7},{4,0},{5,1},{6,2},{7,3},{8,12},{9,13},{10,... | collective-permute-start | bytes 626696 | tf_op jit(solution)/shard_map/ppermute | solution.py:737
  57.6 6.4 %shard_map.175 = (bf16[128,768]{1,0:T(8,128)(2,1)S(1)}, f32[128,768]{1,0:T(8,128)S(1)}, f32[128,768]{1,0:T(8,128)S(1)}, f32[128,3072]{1,0:T(8,128)S(1)}) custom-call(s32[47]{0:T(128)S(1)} %stack.110.sc, f32[16,128]{1,0:T(8,128)S(1)} %get-tuple-element.122.tag_ref.tags_ref, bf16[128,2304]{1,0:T(8,128)(2,1)S(1)} %get-tuple-element.123.qkv_ref, ...), custom_call_target="tpu_custom_call" | custom-call | flops 3000000 | bytes 9000 | tf_op jit(solution)/shard_map/pallas_call | solution.py:115
  64.0 1.5 %collective-permute-start.10 = (bf16[136,768]{1,0:T(8,128)(2,1)S(1)}, bf16[136,768]{1,0:T(8,128)(2,1)S(1)}, u32[]{:S(2)}, u32[]{:S(2)}) collective-permute-start(bf16[136,768]{1,0:T(8,128)(2,1)S(1)} %get-tuple-element.166), channel_id=1, source_target_pairs={{0,6},{1,7},{2,4},{3,5},{4,2},{5,3},{6,0},{7,1},{8,14},{9,15},{10,... | collective-permute-start | bytes 626696 | tf_op jit(solution)/shard_map/ppermute | solution.py:737
  65.6 2.4 %collective-permute-start.20 = (bf16[1536,128]{1,0:T(8,128)(2,1)S(1)}, bf16[1536,128]{1,0:T(8,128)(2,1)S(1)}, u32[]{:S(2)}, u32[]{:S(2)}) collective-permute-start(bf16[1536,128]{1,0:T(8,128)(2,1)S(1)} %get-tuple-element.191), channel_id=1, source_target_pairs={{0,24},{8,16},{16,8},{24,0},{1,25},{9,17},{17,9},{25,1},{2,26},{10... | collective-permute-start | bytes 1179656 | tf_op jit(solution)/shard_map/ppermute | solution.py:737
  68.0 1.7 %shard_map.178 = (f32[4,120,768]{2,1,0:T(8,128)S(1)}, bf16[4,120,768]{2,1,0:T(8,128)(2,1)S(1)}) custom-call(s32[47]{0:T(128)S(1)} %stack.110.sc, bf16[1536,128]{1,0:T(8,128)(2,1)S(1)} %get-tuple-element.197.p0, bf16[1536,128]{1,0:T(8,128)(2,1)S(1)} %collective-permute-done.12.p1, bf16[1536,128]{1,0:T(8,128)(2,1)S(1)} %collective-permute-done.13.p2, ...), custom_call_target="tpu_custom_call" | custom-call | flops 600000 | bytes 20000000 | tf_op jit(solution)/shard_map/pallas_call | solution.py:115
  69.9 2.1 %collective-permute-done.10 = bf16[136,768]{1,0:T(8,128)(2,1)S(1)} collective-permute-done((bf16[136,768]{1,0:T(8,128)(2,1)S(1)}, bf16[136,768]{1,0:T(8,128)(2,1)S(1)}, u32[]{:S(2)}, u32[]{:S(2)}) %collective-permute-start.10) | collective-permute-done | bytes 208928 | tf_op jit(solution)/shard_map/ppermute | solution.py:737
  72.2 1.6 %collective-permute-start.19 = (bf16[1536,128]{1,0:T(8,128)(2,1)S(1)}, bf16[1536,128]{1,0:T(8,128)(2,1)S(1)}, u32[]{:S(2)}, u32[]{:S(2)}) collective-permute-start(bf16[1536,128]{1,0:T(8,128)(2,1)S(1)} %get-tuple-element.208), channel_id=1, source_target_pairs={{0,16},{8,24},{16,0},{24,8},{1,17},{9,25},{17,1},{25,9},{2,18},{10... | collective-permute-start | bytes 1179656 | tf_op jit(solution)/shard_map/ppermute | solution.py:737
  73.7 1.5 %collective-permute-start.18 = (bf16[1536,128]{1,0:T(8,128)(2,1)S(1)}, bf16[1536,128]{1,0:T(8,128)(2,1)S(1)}, u32[]{:S(2)}, u32[]{:S(2)}) collective-permute-start(bf16[1536,128]{1,0:T(8,128)(2,1)S(1)} %get-tuple-element.207), channel_id=1, source_target_pairs={{0,8},{8,0},{16,24},{24,16},{1,9},{9,1},{17,25},{25,17},{2,10},{10... | collective-permute-start | bytes 1179656 | tf_op jit(solution)/shard_map/ppermute | solution.py:737
  75.2 0.2 convert_add_fusion
  75.5 5.1 %collective-permute-start.16 = (bf16[2,120,768]{2,1,0:T(8,128)(2,1)S(1)}, bf16[2,120,768]{2,1,0:T(8,128)(2,1)S(1)}, u32[]{:S(2)}, u32[]{:S(2)}) collective-permute-start(bf16[2,120,768]{2,1,0:T(8,128)(2,1)S(1)} %slice.115), channel_id=1, source_target_pairs={{0,2},{1,3},{2,0},{3,1},{4,6},{5,7},{6,4},{7,5},{8,10},{9,11},{10,... | collective-permute-start | bytes 1105928 | tf_op jit(solution)/shard_map/ppermute | solution.py:737
  80.7 9.9 %shard_map.177 = (bf16[136,640]{1,0:T(8,128)(2,1)S(1)}, bf16[136,640]{1,0:T(8,128)(2,1)S(1)}, bf16[136,640]{1,0:T(8,128)(2,1)S(1)}, bf16[136,640]{1,0:T(8,128)(2,1)S(1)}, f32[128,768]{1,0:T(8,128)}) custom-call(s32[47]{0:T(128)S(1)} %stack.110.sc, bf16[8,136,768]{2,1,0:T(8,128)(2,1)S(1)} %constant_dynamic-update-slice_fusion.dn_ref, ...), custom_call_target="tpu_custom_call" | custom-call | flops 3000000 | bytes 17000 | tf_op jit(solution)/shard_map/pallas_call | solution.py:115
  90.5 1.5 %shard_map.180 = (f32[4,96,768]{2,1,0:T(8,128)S(1)}, bf16[4,96,768]{2,1,0:T(8,128)(2,1)S(1)}) custom-call(s32[47]{0:T(128)S(1)} %stack.110.sc, bf16[1536,128]{1,0:T(8,128)(2,1)S(1)} %get-tuple-element.217.p0, bf16[1536,128]{1,0:T(8,128)(2,1)S(1)} %collective-permute-done.18.p1, bf16[1536,128]{1,0:T(8,128)(2,1)S(1)} %collective-permute-done.19.p2, ...), custom_call_target="tpu_custom_call" | custom-call | flops 600000 | bytes 20000000 | tf_op jit(solution)/shard_map/pallas_call | solution.py:115
  92.2 1.1 collective-permute-start.17
  93.3 2.2 %collective-permute-start.23 = (bf16[136,640]{1,0:T(8,128)(2,1)S(1)}, bf16[136,640]{1,0:T(8,128)(2,1)S(1)}, u32[]{:S(2)}, u32[]{:S(2)}) collective-permute-start(bf16[136,640]{1,0:T(8,128)(2,1)S(1)} %get-tuple-element.213), channel_id=1, source_target_pairs={{0,24},{8,16},{16,8},{24,0},{1,25},{9,17},{17,9},{25,1},{2,26},{10... | collective-permute-start | bytes 522248 | tf_op jit(solution)/shard_map/ppermute | solution.py:737
  95.4 0.6 collective-permute-start.22
  96.0 0.8 collective-permute-start.21
  96.7 7.0 %collective-permute-done.17 = bf16[120,768]{1,0:T(8,128)(2,1)S(1)} collective-permute-done((bf16[120,768]{1,0:T(8,128)(2,1)S(1)}, bf16[120,768]{1,0:T(8,128)(2,1)S(1)}, u32[]{:S(2)}, u32[]{:S(2)}) %collective-permute-start.17) | collective-permute-done | bytes 184352 | tf_op jit(solution)/shard_map/ppermute | solution.py:737
  103.8 0.7 collective-permute-done.22.p2
  104.4 1.5 %shard_map.179 = (f32[4,104,640]{2,1,0:T(8,128)S(1)}, bf16[4,104,640]{2,1,0:T(8,128)(2,1)S(1)}) custom-call(s32[47]{0:T(128)S(1)} %stack.110.sc, bf16[136,640]{1,0:T(8,128)(2,1)S(1)} %get-tuple-element.205.p0, bf16[136,640]{1,0:T(8,128)(2,1)S(1)} %collective-permute-done.21.p1, bf16[136,640]{1,0:T(8,128)(2,1)S(1)} %collective-permute-done.22.p2, ...), custom_call_target="tpu_custom_call" | custom-call | flops 600000 | bytes 20000000 | tf_op jit(solution)/shard_map/pallas_call | solution.py:115
  106.1 1.9 %collective-permute-start.30 = (bf16[2,96,768]{2,1,0:T(8,128)(2,1)S(1)}, bf16[2,96,768]{2,1,0:T(8,128)(2,1)S(1)}, u32[]{:S(2)}, u32[]{:S(2)}) collective-permute-start(bf16[2,96,768]{2,1,0:T(8,128)(2,1)S(1)} %slice.116), channel_id=1, source_target_pairs={{0,2},{1,3},{2,0},{3,1},{4,6},{5,7},{6,4},{7,5},{8,10},{9,11},{10,... | collective-permute-start | bytes 884744 | tf_op jit(solution)/shard_map/ppermute | solution.py:737
  108.1 1.8 %collective-permute-start.28 = (bf16[120,768]{1,0:T(8,128)(2,1)S(1)}, bf16[120,768]{1,0:T(8,128)(2,1)S(1)}, u32[]{:S(2)}, u32[]{:S(2)}) collective-permute-start(bf16[120,768]{1,0:T(8,128)(2,1)S(1)} %fusion.1.refs_0_), channel_id=1, source_target_pairs={{0,24},{8,16},{16,8},{24,0},{1,25},{9,17},{17,9},{25,1},{2,26},{10... | collective-permute-start | bytes 552968 | tf_op jit(solution)/shard_map/ppermute | solution.py:737
  109.9 1.2 collective-permute-start.32
  111.0 0.6 collective-permute-start.27
  111.8 0.2 collective-permute-start.25
  112.0 4.0 %collective-permute-done.30 = bf16[2,96,768]{2,1,0:T(8,128)(2,1)S(1)} collective-permute-done((bf16[2,96,768]{2,1,0:T(8,128)(2,1)S(1)}, bf16[2,96,768]{2,1,0:T(8,128)(2,1)S(1)}, u32[]{:S(2)}, u32[]{:S(2)}) %collective-permute-start.30) | collective-permute-done | bytes 294944 | tf_op jit(solution)/shard_map/ppermute | solution.py:737
  116.1 2.0 %collective-permute-start.31 = (bf16[96,768]{1,0:T(8,128)(2,1)S(1)}, bf16[96,768]{1,0:T(8,128)(2,1)S(1)}, u32[]{:S(2)}, u32[]{:S(2)}) collective-permute-start(bf16[96,768]{1,0:T(8,128)(2,1)S(1)} %fusion.7), channel_id=1, source_target_pairs={{0,4},{1,5},{2,6},{3,7},{4,0},{5,1},{6,2},{7,3},{8,12},{9,13},{10,... | collective-permute-start | bytes 442376 | tf_op jit(solution)/shard_map/ppermute | solution.py:737
  118.0 6.5 %collective-permute-done.25 = bf16[2,104,640]{2,1,0:T(8,128)(2,1)S(1)} collective-permute-done((bf16[2,104,640]{2,1,0:T(8,128)(2,1)S(1)}, bf16[2,104,640]{2,1,0:T(8,128)(2,1)S(1)}, u32[]{:S(2)}, u32[]{:S(2)}) %collective-permute-start.25) | collective-permute-done | bytes 266272 | tf_op jit(solution)/shard_map/ppermute | solution.py:737
  124.8 2.6 %collective-permute-start.35 = (bf16[96,768]{1,0:T(8,128)(2,1)S(1)}, bf16[96,768]{1,0:T(8,128)(2,1)S(1)}, u32[]{:S(2)}, u32[]{:S(2)}) collective-permute-start(bf16[96,768]{1,0:T(8,128)(2,1)S(1)} %fusion.3.refs_0_), channel_id=1, source_target_pairs={{0,24},{8,16},{16,8},{24,0},{1,25},{9,17},{17,9},{25,1},{2,26},{10... | collective-permute-start | bytes 442376 | tf_op jit(solution)/shard_map/ppermute | solution.py:737
  127.4 1.4 collective-permute-start.34
  128.7 4.0 %collective-permute-done.26 = bf16[104,640]{1,0:T(8,128)(2,1)S(1)} collective-permute-done((bf16[104,640]{1,0:T(8,128)(2,1)S(1)}, bf16[104,640]{1,0:T(8,128)(2,1)S(1)}, u32[]{:S(2)}, u32[]{:S(2)}) %collective-permute-start.26) | collective-permute-done | bytes 133152 | tf_op jit(solution)/shard_map/ppermute | solution.py:737
  132.8 1.9 %collective-permute-start.38 = (bf16[104,640]{1,0:T(8,128)(2,1)S(1)}, bf16[104,640]{1,0:T(8,128)(2,1)S(1)}, u32[]{:S(2)}, u32[]{:S(2)}) collective-permute-start(bf16[104,640]{1,0:T(8,128)(2,1)S(1)} %fusion.5.refs_0_), channel_id=1, source_target_pairs={{0,24},{8,16},{16,8},{24,0},{1,25},{9,17},{17,9},{25,1},{2,26},{10... | collective-permute-start | bytes 399368 | tf_op jit(solution)/shard_map/ppermute | solution.py:737
  134.7 0.9 collective-permute-start.37
  135.6 0.7 collective-permute-start.36
  136.3 1.8 %shard_map.183 = (f32[384,768]{1,0:T(8,128)}, f32[96,768]{1,0:T(8,128)}) custom-call(s32[47]{0:T(128)S(1)} %stack.110.sc, bf16[120,768]{1,0:T(8,128)(2,1)S(1)} %fusion.1.refs_0_, bf16[120,768]{1,0:T(8,128)(2,1)S(1)} %collective-permute-done.32.refs_1_, bf16[120,768]{1,0:T(8,128)(2,1)S(1)} %collective-permute-done.27.refs_2_, ...), custom_call_target="tpu_custom_call" | custom-call | bytes 2000 | tf_op jit(solution)/shard_map/pallas_call | solution.py:115
  138.2 1.7 %shard_map.181 = f32[96,3072]{1,0:T(8,128)} custom-call(s32[47]{0:T(128)S(1)} %stack.110.sc, bf16[96,768]{1,0:T(8,128)(2,1)S(1)} %fusion.3.refs_0_, bf16[96,768]{1,0:T(8,128)(2,1)S(1)} %collective-permute-done.33.refs_1_, bf16[96,768]{1,0:T(8,128)(2,1)S(1)} %collective-permute-done.34.refs_2_, bf16[96,768]{1,0:T(8,128)(2,1)S(1)} %collective-permute-done.35.refs_3_), custom_call_target="tpu_custom_call" | custom-call | bytes 2000 | tf_op jit(solution)/shard_map/pallas_call | solution.py:115
  139.9 0.3 collective-permute-done.38.refs_3_
  140.1 1.9 %collective-permute-done.37.refs_2_ = bf16[104,640]{1,0:T(8,128)(2,1)S(1)} collective-permute-done((bf16[104,640]{1,0:T(8,128)(2,1)S(1)}, bf16[104,640]{1,0:T(8,128)(2,1)S(1)}, u32[]{:S(2)}, u32[]{:S(2)}) %collective-permute-start.37) | collective-permute-done | bytes 133152 | tf_op jit(solution)/shard_map/ppermute | solution.py:737
  142.1 1.6 %shard_map.182 = (f32[96,2304]{1,0:T(8,128)}, f32[8,640]{1,0:T(8,128)S(1)}) custom-call(s32[47]{0:T(128)S(1)} %stack.110.sc, bf16[104,640]{1,0:T(8,128)(2,1)S(1)} %fusion.5.refs_0_, bf16[104,640]{1,0:T(8,128)(2,1)S(1)} %collective-permute-done.36.refs_1_, bf16[104,640]{1,0:T(8,128)(2,1)S(1)} %collective-permute-done.37.refs_2_, ...), custom_call_target="tpu_custom_call" | custom-call | bytes 2000 | tf_op jit(solution)/shard_map/pallas_call | solution.py:115
  143.8 0.5 slice_bitcast_fusion.3
  (89 shorter events, 1.8 us)
Async XLA Ops:
  1.4 0.9 copy-start.5
  2.4 0.7 copy-start.7
  3.6 14.9 %collective-permute-start.2 = (bf16[136,768]{1,0:T(8,128)(2,1)S(1)}, bf16[136,768]{1,0:T(8,128)(2,1)S(1)}, u32[]{:S(2)}, u32[]{:S(2)}) collective-permute-start(bf16[136,768]{1,0:T(8,128)(2,1)S(1)} %get-tuple-element.121.x_ref), channel_id=1, source_target_pairs={{0,1},{1,0},{2,3},{3,2},{4,5},{5,4},{6,7},{7,6},{8,9},{9,8},{10,11... | collective-permute-start | bytes 626696 | tf_op jit(solution)/shard_map/ppermute | solution.py:737
  4.2 14.4 %collective-permute-start.3 = (bf16[136,768]{1,0:T(8,128)(2,1)S(1)}, bf16[136,768]{1,0:T(8,128)(2,1)S(1)}, u32[]{:S(2)}, u32[]{:S(2)}) collective-permute-start(bf16[136,768]{1,0:T(8,128)(2,1)S(1)} %get-tuple-element.121.x_ref), channel_id=1, source_target_pairs={{0,2},{1,3},{2,0},{3,1},{4,6},{5,7},{6,4},{7,5},{8,10},{9,11},{10,... | collective-permute-start | bytes 626696 | tf_op jit(solution)/shard_map/ppermute | solution.py:737
  6.8 17.9 %collective-permute-start = (bf16[136,768]{1,0:T(8,128)(2,1)S(1)}, bf16[136,768]{1,0:T(8,128)(2,1)S(1)}, u32[]{:S(2)}, u32[]{:S(2)}) collective-permute-start(bf16[136,768]{1,0:T(8,128)(2,1)S(1)} %get-tuple-element.121.x_ref), channel_id=1, source_target_pairs={{0,4},{1,5},{2,6},{3,7},{4,0},{5,1},{6,2},{7,3},{8,12},{9,13},{10,... | collective-permute-start | bytes 626696 | tf_op jit(solution)/shard_map/ppermute | solution.py:737
  9.4 15.3 %collective-permute-start.1 = (bf16[136,768]{1,0:T(8,128)(2,1)S(1)}, bf16[136,768]{1,0:T(8,128)(2,1)S(1)}, u32[]{:S(2)}, u32[]{:S(2)}) collective-permute-start(bf16[136,768]{1,0:T(8,128)(2,1)S(1)} %get-tuple-element.121.x_ref), channel_id=1, source_target_pairs={{0,6},{1,7},{2,4},{3,5},{4,2},{5,3},{6,0},{7,1},{8,14},{9,15},{10,... | collective-permute-start | bytes 626696 | tf_op jit(solution)/shard_map/ppermute | solution.py:737
  10.1 2.0 %copy-start = (bf16[768,2304]{1,0:T(8,128)(2,1)S(1)}, bf16[768,2304]{1,0:T(8,128)(2,1)}, u32[]{:S(2)}) copy-start(bf16[768,2304]{1,0:T(8,128)(2,1)} %w_ref.7) | copy-start | bytes 10616836
  12.1 0.9 copy-start.3
  13.0 0.8 copy-start.6
  13.9 4.7 %copy-start.1 = (bf16[768,2304]{1,0:T(8,128)(2,1)S(1)}, bf16[768,2304]{1,0:T(8,128)(2,1)}, u32[]{:S(2)}) copy-start(bf16[768,2304]{1,0:T(8,128)(2,1)} %w_ref.7) | copy-start | bytes 10616836
  18.6 9.8 %copy-start.8 = (f32[768]{0:T(1024)S(1)}, f32[768]{0:T(1024)}, u32[]{:S(2)}) copy-start(f32[768]{0:T(1024)} %param.18) | copy-start | bytes 9220
  24.8 3.6 %collective-permute-start.4 = (bf16[3,136,768]{2,1,0:T(8,128)(2,1)S(1)}, bf16[3,136,768]{2,1,0:T(8,128)(2,1)S(1)}, u32[]{:S(2)}, u32[]{:S(2)}) collective-permute-start(bf16[3,136,768]{2,1,0:T(8,128)(2,1)S(1)} %pad_maximum_fusion.2), channel_id=1, source_target_pairs={{0,1},{1,0},{2,3},{3,2},{4,5},{5,4},{6,7},{7,6},{8,9},{9,8},{10,11... | collective-permute-start | bytes 1880072 | tf_op jit(solution)/shard_map/ppermute | solution.py:737
  24.9 20.4 %collective-permute-start.5 = (bf16[1536,128]{1,0:T(8,128)(2,1)S(1)}, bf16[1536,128]{1,0:T(8,128)(2,1)S(1)}, u32[]{:S(2)}, u32[]{:S(2)}) collective-permute-start(bf16[1536,128]{1,0:T(8,128)(2,1)S(1)} %get-tuple-element.164.e0), channel_id=1, source_target_pairs={{0,8},{8,0},{16,24},{24,16},{1,9},{9,1},{17,25},{25,17},{2,10},{10... | collective-permute-start | bytes 1179656 | tf_op jit(solution)/shard_map/ppermute | solution.py:737
  26.4 19.6 %collective-permute-start.6 = (bf16[1536,128]{1,0:T(8,128)(2,1)S(1)}, bf16[1536,128]{1,0:T(8,128)(2,1)S(1)}, u32[]{:S(2)}, u32[]{:S(2)}) collective-permute-start(bf16[1536,128]{1,0:T(8,128)(2,1)S(1)} %get-tuple-element.164.e0), channel_id=1, source_target_pairs={{0,16},{8,24},{16,0},{24,8},{1,17},{9,25},{17,1},{25,9},{2,18},{10... | collective-permute-start | bytes 1179656 | tf_op jit(solution)/shard_map/ppermute | solution.py:737
  27.9 18.1 %collective-permute-start.7 = (bf16[1536,128]{1,0:T(8,128)(2,1)S(1)}, bf16[1536,128]{1,0:T(8,128)(2,1)S(1)}, u32[]{:S(2)}, u32[]{:S(2)}) collective-permute-start(bf16[1536,128]{1,0:T(8,128)(2,1)S(1)} %get-tuple-element.164.e0), channel_id=1, source_target_pairs={{0,24},{8,16},{16,8},{24,0},{1,25},{9,17},{17,9},{25,1},{2,26},{10... | collective-permute-start | bytes 1179656 | tf_op jit(solution)/shard_map/ppermute | solution.py:737
  28.4 5.3 %slice-start = ((s8[4718592]{0:T(1024)(128)(4,1)}), s8[4194304]{0:T(1024)(128)(4,1)S(1)}, s32[]{:S(2)}) async-start(s8[4718592]{0:T(1024)(128)(4,1)} %bitcast.59), calls=%async_computation | async-start | bytes 8388608
  28.4 5.3 %slice-start.2 = ((s8[4718592]{0:T(1024)(128)(4,1)}), s8[4194304]{0:T(1024)(128)(4,1)S(1)}, s32[]{:S(2)}) async-start(s8[4718592]{0:T(1024)(128)(4,1)} %bitcast.61), calls=%async_computation.2 | async-start | bytes 8388608
  28.6 5.2 %slice-start.1 = ((s8[4718592]{0:T(1024)(128)(4,1)}), s8[524288]{0:T(1024)(128)(4,1)S(1)}, s32[]{:S(2)}) async-start(s8[4718592]{0:T(1024)(128)(4,1)} %bitcast.59), calls=%async_computation.1 | async-start | bytes 1048576
  28.6 5.2 %slice-start.3 = ((s8[4718592]{0:T(1024)(128)(4,1)}), s8[524288]{0:T(1024)(128)(4,1)S(1)}, s32[]{:S(2)}) async-start(s8[4718592]{0:T(1024)(128)(4,1)} %bitcast.61), calls=%async_computation.3 | async-start | bytes 1048576
  28.6 5.2 %copy-start.2 = (bf16[768,768]{1,0:T(8,128)(2,1)S(1)}, bf16[768,768]{1,0:T(8,128)(2,1)}, u32[]{:S(2)}) copy-start(bf16[768,768]{1,0:T(8,128)(2,1)} %wo_ref.1) | copy-start | bytes 3538948
  28.6 5.2 %copy-start.4 = (bf16[1,128,768]{2,1,0:T(8,128)(2,1)S(1)}, bf16[1,128,768]{2,1,0:T(8,128)(2,1)}, u32[]{:S(2)}) copy-start(bf16[1,128,768]{2,1,0:T(8,128)(2,1)} %param.21) | copy-start | bytes 589828
  47.2 20.8 %collective-permute-start.13 = (bf16[1536,128]{1,0:T(8,128)(2,1)S(1)}, bf16[1536,128]{1,0:T(8,128)(2,1)S(1)}, u32[]{:S(2)}, u32[]{:S(2)}) collective-permute-start(bf16[1536,128]{1,0:T(8,128)(2,1)S(1)} %get-tuple-element.193), channel_id=1, source_target_pairs={{0,16},{8,24},{16,0},{24,8},{1,17},{9,25},{17,1},{25,9},{2,18},{10... | collective-permute-start | bytes 1179656 | tf_op jit(solution)/shard_map/ppermute | solution.py:737
  48.8 19.2 %collective-permute-start.12 = (bf16[1536,128]{1,0:T(8,128)(2,1)S(1)}, bf16[1536,128]{1,0:T(8,128)(2,1)S(1)}, u32[]{:S(2)}, u32[]{:S(2)}) collective-permute-start(bf16[1536,128]{1,0:T(8,128)(2,1)S(1)} %get-tuple-element.192), channel_id=1, source_target_pairs={{0,8},{8,0},{16,24},{24,16},{1,9},{9,1},{17,25},{25,17},{2,10},{10... | collective-permute-start | bytes 1179656 | tf_op jit(solution)/shard_map/ppermute | solution.py:737
  49.5 18.5 %collective-permute-start.14 = (bf16[1536,128]{1,0:T(8,128)(2,1)S(1)}, bf16[1536,128]{1,0:T(8,128)(2,1)S(1)}, u32[]{:S(2)}, u32[]{:S(2)}) collective-permute-start(bf16[1536,128]{1,0:T(8,128)(2,1)S(1)} %get-tuple-element.198), channel_id=1, source_target_pairs={{0,24},{8,16},{16,8},{24,0},{1,25},{9,17},{17,9},{25,1},{2,26},{10... | collective-permute-start | bytes 1179656 | tf_op jit(solution)/shard_map/ppermute | solution.py:737
  50.8 13.3 %collective-permute-start.8 = (bf16[136,768]{1,0:T(8,128)(2,1)S(1)}, bf16[136,768]{1,0:T(8,128)(2,1)S(1)}, u32[]{:S(2)}, u32[]{:S(2)}) collective-permute-start(bf16[136,768]{1,0:T(8,128)(2,1)S(1)} %get-tuple-element.166), channel_id=1, source_target_pairs={{0,2},{1,3},{2,0},{3,1},{4,6},{5,7},{6,4},{7,5},{8,10},{9,11},{10,... | collective-permute-start | bytes 626696 | tf_op jit(solution)/shard_map/ppermute | solution.py:737
  55.0 10.5 %collective-permute-start.9 = (bf16[136,768]{1,0:T(8,128)(2,1)S(1)}, bf16[136,768]{1,0:T(8,128)(2,1)S(1)}, u32[]{:S(2)}, u32[]{:S(2)}) collective-permute-start(bf16[136,768]{1,0:T(8,128)(2,1)S(1)} %get-tuple-element.166), channel_id=1, source_target_pairs={{0,4},{1,5},{2,6},{3,7},{4,0},{5,1},{6,2},{7,3},{8,12},{9,13},{10,... | collective-permute-start | bytes 626696 | tf_op jit(solution)/shard_map/ppermute | solution.py:737
  64.0 7.9 %collective-permute-start.10 = (bf16[136,768]{1,0:T(8,128)(2,1)S(1)}, bf16[136,768]{1,0:T(8,128)(2,1)S(1)}, u32[]{:S(2)}, u32[]{:S(2)}) collective-permute-start(bf16[136,768]{1,0:T(8,128)(2,1)S(1)} %get-tuple-element.166), channel_id=1, source_target_pairs={{0,6},{1,7},{2,4},{3,5},{4,2},{5,3},{6,0},{7,1},{8,14},{9,15},{10,... | collective-permute-start | bytes 626696 | tf_op jit(solution)/shard_map/ppermute | solution.py:737
  65.6 24.9 %collective-permute-start.20 = (bf16[1536,128]{1,0:T(8,128)(2,1)S(1)}, bf16[1536,128]{1,0:T(8,128)(2,1)S(1)}, u32[]{:S(2)}, u32[]{:S(2)}) collective-permute-start(bf16[1536,128]{1,0:T(8,128)(2,1)S(1)} %get-tuple-element.191), channel_id=1, source_target_pairs={{0,24},{8,16},{16,8},{24,0},{1,25},{9,17},{17,9},{25,1},{2,26},{10... | collective-permute-start | bytes 1179656 | tf_op jit(solution)/shard_map/ppermute | solution.py:737
  69.8 5.5 %collective-permute-start.15 = (bf16[4,120,768]{2,1,0:T(8,128)(2,1)S(1)}, bf16[4,120,768]{2,1,0:T(8,128)(2,1)S(1)}, u32[]{:S(2)}, u32[]{:S(2)}) collective-permute-start(bf16[4,120,768]{2,1,0:T(8,128)(2,1)S(1)} %get-tuple-element.203), channel_id=1, source_target_pairs={{0,1},{1,0},{2,3},{3,2},{4,5},{5,4},{6,7},{7,6},{8,9},{9,8},{10,11... | collective-permute-start | bytes 2211848 | tf_op jit(solution)/shard_map/ppermute | solution.py:737
  72.0 8.6 %collective-permute-start.11 = (bf16[4,136,768]{2,1,0:T(8,128)(2,1)S(1)}, bf16[4,136,768]{2,1,0:T(8,128)(2,1)S(1)}, u32[]{:S(2)}, u32[]{:S(2)}) collective-permute-start(bf16[4,136,768]{2,1,0:T(8,128)(2,1)S(1)} %pad_maximum_fusion.1), channel_id=1, source_target_pairs={{0,1},{1,0},{2,3},{3,2},{4,5},{5,4},{6,7},{7,6},{8,9},{9,8},{10,11... | collective-permute-start | bytes 2506760 | tf_op jit(solution)/shard_map/ppermute | solution.py:737
  72.2 18.4 %collective-permute-start.19 = (bf16[1536,128]{1,0:T(8,128)(2,1)S(1)}, bf16[1536,128]{1,0:T(8,128)(2,1)S(1)}, u32[]{:S(2)}, u32[]{:S(2)}) collective-permute-start(bf16[1536,128]{1,0:T(8,128)(2,1)S(1)} %get-tuple-element.208), channel_id=1, source_target_pairs={{0,16},{8,24},{16,0},{24,8},{1,17},{9,25},{17,1},{25,9},{2,18},{10... | collective-permute-start | bytes 1179656 | tf_op jit(solution)/shard_map/ppermute | solution.py:737
  73.7 16.8 %collective-permute-start.18 = (bf16[1536,128]{1,0:T(8,128)(2,1)S(1)}, bf16[1536,128]{1,0:T(8,128)(2,1)S(1)}, u32[]{:S(2)}, u32[]{:S(2)}) collective-permute-start(bf16[1536,128]{1,0:T(8,128)(2,1)S(1)} %get-tuple-element.207), channel_id=1, source_target_pairs={{0,8},{8,0},{16,24},{24,16},{1,9},{9,1},{17,25},{25,17},{2,10},{10... | collective-permute-start | bytes 1179656 | tf_op jit(solution)/shard_map/ppermute | solution.py:737
  75.5 16.6 %collective-permute-start.16 = (bf16[2,120,768]{2,1,0:T(8,128)(2,1)S(1)}, bf16[2,120,768]{2,1,0:T(8,128)(2,1)S(1)}, u32[]{:S(2)}, u32[]{:S(2)}) collective-permute-start(bf16[2,120,768]{2,1,0:T(8,128)(2,1)S(1)} %slice.115), channel_id=1, source_target_pairs={{0,2},{1,3},{2,0},{3,1},{4,6},{5,7},{6,4},{7,5},{8,10},{9,11},{10,... | collective-permute-start | bytes 1105928 | tf_op jit(solution)/shard_map/ppermute | solution.py:737
  92.0 14.0 %collective-permute-start.29 = (bf16[4,96,768]{2,1,0:T(8,128)(2,1)S(1)}, bf16[4,96,768]{2,1,0:T(8,128)(2,1)S(1)}, u32[]{:S(2)}, u32[]{:S(2)}) collective-permute-start(bf16[4,96,768]{2,1,0:T(8,128)(2,1)S(1)} %get-tuple-element.221), channel_id=1, source_target_pairs={{0,1},{1,0},{2,3},{3,2},{4,5},{5,4},{6,7},{7,6},{8,9},{9,8},{10,11... | collective-permute-start | bytes 1769480 | tf_op jit(solution)/shard_map/ppermute | solution.py:737
  92.2 11.6 %collective-permute-start.17 = (bf16[120,768]{1,0:T(8,128)(2,1)S(1)}, bf16[120,768]{1,0:T(8,128)(2,1)S(1)}, u32[]{:S(2)}, u32[]{:S(2)}) collective-permute-start(bf16[120,768]{1,0:T(8,128)(2,1)S(1)} %fusion.6), channel_id=1, source_target_pairs={{0,4},{1,5},{2,6},{3,7},{4,0},{5,1},{6,2},{7,3},{8,12},{9,13},{10,... | collective-permute-start | bytes 552968 | tf_op jit(solution)/shard_map/ppermute | solution.py:737
  93.3 10.5 %collective-permute-start.23 = (bf16[136,640]{1,0:T(8,128)(2,1)S(1)}, bf16[136,640]{1,0:T(8,128)(2,1)S(1)}, u32[]{:S(2)}, u32[]{:S(2)}) collective-permute-start(bf16[136,640]{1,0:T(8,128)(2,1)S(1)} %get-tuple-element.213), channel_id=1, source_target_pairs={{0,24},{8,16},{16,8},{24,0},{1,25},{9,17},{17,9},{25,1},{2,26},{10... | collective-permute-start | bytes 522248 | tf_op jit(solution)/shard_map/ppermute | solution.py:737
  95.4 9.0 %collective-permute-start.22 = (bf16[136,640]{1,0:T(8,128)(2,1)S(1)}, bf16[136,640]{1,0:T(8,128)(2,1)S(1)}, u32[]{:S(2)}, u32[]{:S(2)}) collective-permute-start(bf16[136,640]{1,0:T(8,128)(2,1)S(1)} %get-tuple-element.211), channel_id=1, source_target_pairs={{0,16},{8,24},{16,0},{24,8},{1,17},{9,25},{17,1},{25,9},{2,18},{10... | collective-permute-start | bytes 522248 | tf_op jit(solution)/shard_map/ppermute | solution.py:737
  96.0 8.4 %collective-permute-start.21 = (bf16[136,640]{1,0:T(8,128)(2,1)S(1)}, bf16[136,640]{1,0:T(8,128)(2,1)S(1)}, u32[]{:S(2)}, u32[]{:S(2)}) collective-permute-start(bf16[136,640]{1,0:T(8,128)(2,1)S(1)} %get-tuple-element.209), channel_id=1, source_target_pairs={{0,8},{8,0},{16,24},{24,16},{1,9},{9,1},{17,25},{25,17},{2,10},{10... | collective-permute-start | bytes 522248 | tf_op jit(solution)/shard_map/ppermute | solution.py:737
  105.9 5.8 %collective-permute-start.24 = (bf16[4,104,640]{2,1,0:T(8,128)(2,1)S(1)}, bf16[4,104,640]{2,1,0:T(8,128)(2,1)S(1)}, u32[]{:S(2)}, u32[]{:S(2)}) collective-permute-start(bf16[4,104,640]{2,1,0:T(8,128)(2,1)S(1)} %get-tuple-element.216), channel_id=1, source_target_pairs={{0,1},{1,0},{2,3},{3,2},{4,5},{5,4},{6,7},{7,6},{8,9},{9,8},{10,11... | collective-permute-start | bytes 1597448 | tf_op jit(solution)/shard_map/ppermute | solution.py:737
  106.1 9.9 %collective-permute-start.30 = (bf16[2,96,768]{2,1,0:T(8,128)(2,1)S(1)}, bf16[2,96,768]{2,1,0:T(8,128)(2,1)S(1)}, u32[]{:S(2)}, u32[]{:S(2)}) collective-permute-start(bf16[2,96,768]{2,1,0:T(8,128)(2,1)S(1)} %slice.116), channel_id=1, source_target_pairs={{0,2},{1,3},{2,0},{3,1},{4,6},{5,7},{6,4},{7,5},{8,10},{9,11},{10,... | collective-permute-start | bytes 884744 | tf_op jit(solution)/shard_map/ppermute | solution.py:737
  108.1 16.7 %collective-permute-start.28 = (bf16[120,768]{1,0:T(8,128)(2,1)S(1)}, bf16[120,768]{1,0:T(8,128)(2,1)S(1)}, u32[]{:S(2)}, u32[]{:S(2)}) collective-permute-start(bf16[120,768]{1,0:T(8,128)(2,1)S(1)} %fusion.1.refs_0_), channel_id=1, source_target_pairs={{0,24},{8,16},{16,8},{24,0},{1,25},{9,17},{17,9},{25,1},{2,26},{10... | collective-permute-start | bytes 552968 | tf_op jit(solution)/shard_map/ppermute | solution.py:737
  109.9 17.5 %collective-permute-start.32 = (bf16[120,768]{1,0:T(8,128)(2,1)S(1)}, bf16[120,768]{1,0:T(8,128)(2,1)S(1)}, u32[]{:S(2)}, u32[]{:S(2)}) collective-permute-start(bf16[120,768]{1,0:T(8,128)(2,1)S(1)} %fusion.1.refs_0_), channel_id=1, source_target_pairs={{0,8},{8,0},{16,24},{24,16},{1,9},{9,1},{17,25},{25,17},{2,10},{10... | collective-permute-start | bytes 552968 | tf_op jit(solution)/shard_map/ppermute | solution.py:737
  111.0 13.7 %collective-permute-start.27 = (bf16[120,768]{1,0:T(8,128)(2,1)S(1)}, bf16[120,768]{1,0:T(8,128)(2,1)S(1)}, u32[]{:S(2)}, u32[]{:S(2)}) collective-permute-start(bf16[120,768]{1,0:T(8,128)(2,1)S(1)} %fusion.1.refs_0_), channel_id=1, source_target_pairs={{0,16},{8,24},{16,0},{24,8},{1,17},{9,25},{17,1},{25,9},{2,18},{10... | collective-permute-start | bytes 552968 | tf_op jit(solution)/shard_map/ppermute | solution.py:737
  111.8 12.8 %collective-permute-start.25 = (bf16[2,104,640]{2,1,0:T(8,128)(2,1)S(1)}, bf16[2,104,640]{2,1,0:T(8,128)(2,1)S(1)}, u32[]{:S(2)}, u32[]{:S(2)}) collective-permute-start(bf16[2,104,640]{2,1,0:T(8,128)(2,1)S(1)} %slice.117), channel_id=1, source_target_pairs={{0,2},{1,3},{2,0},{3,1},{4,6},{5,7},{6,4},{7,5},{8,10},{9,11},{10,... | collective-permute-start | bytes 798728 | tf_op jit(solution)/shard_map/ppermute | solution.py:737
  116.1 8.7 %collective-permute-start.31 = (bf16[96,768]{1,0:T(8,128)(2,1)S(1)}, bf16[96,768]{1,0:T(8,128)(2,1)S(1)}, u32[]{:S(2)}, u32[]{:S(2)}) collective-permute-start(bf16[96,768]{1,0:T(8,128)(2,1)S(1)} %fusion.7), channel_id=1, source_target_pairs={{0,4},{1,5},{2,6},{3,7},{4,0},{5,1},{6,2},{7,3},{8,12},{9,13},{10,... | collective-permute-start | bytes 442376 | tf_op jit(solution)/shard_map/ppermute | solution.py:737
  124.7 8.1 %collective-permute-start.26 = (bf16[104,640]{1,0:T(8,128)(2,1)S(1)}, bf16[104,640]{1,0:T(8,128)(2,1)S(1)}, u32[]{:S(2)}, u32[]{:S(2)}) collective-permute-start(bf16[104,640]{1,0:T(8,128)(2,1)S(1)} %fusion.8), channel_id=1, source_target_pairs={{0,4},{1,5},{2,6},{3,7},{4,0},{5,1},{6,2},{7,3},{8,12},{9,13},{10,... | collective-permute-start | bytes 399368 | tf_op jit(solution)/shard_map/ppermute | solution.py:737
  124.8 10.8 %collective-permute-start.35 = (bf16[96,768]{1,0:T(8,128)(2,1)S(1)}, bf16[96,768]{1,0:T(8,128)(2,1)S(1)}, u32[]{:S(2)}, u32[]{:S(2)}) collective-permute-start(bf16[96,768]{1,0:T(8,128)(2,1)S(1)} %fusion.3.refs_0_), channel_id=1, source_target_pairs={{0,24},{8,16},{16,8},{24,0},{1,25},{9,17},{17,9},{25,1},{2,26},{10... | collective-permute-start | bytes 442376 | tf_op jit(solution)/shard_map/ppermute | solution.py:737
  127.4 10.8 %collective-permute-start.34 = (bf16[96,768]{1,0:T(8,128)(2,1)S(1)}, bf16[96,768]{1,0:T(8,128)(2,1)S(1)}, u32[]{:S(2)}, u32[]{:S(2)}) collective-permute-start(bf16[96,768]{1,0:T(8,128)(2,1)S(1)} %fusion.3.refs_0_), channel_id=1, source_target_pairs={{0,16},{8,24},{16,0},{24,8},{1,17},{9,25},{17,1},{25,9},{2,18},{10... | collective-permute-start | bytes 442376 | tf_op jit(solution)/shard_map/ppermute | solution.py:737
  128.7 9.4 %collective-permute-start.33 = (bf16[96,768]{1,0:T(8,128)(2,1)S(1)}, bf16[96,768]{1,0:T(8,128)(2,1)S(1)}, u32[]{:S(2)}, u32[]{:S(2)}) collective-permute-start(bf16[96,768]{1,0:T(8,128)(2,1)S(1)} %fusion.3.refs_0_), channel_id=1, source_target_pairs={{0,8},{8,0},{16,24},{24,16},{1,9},{9,1},{17,25},{25,17},{2,10},{10... | collective-permute-start | bytes 442376 | tf_op jit(solution)/shard_map/ppermute | solution.py:737
  132.8 7.4 %collective-permute-start.38 = (bf16[104,640]{1,0:T(8,128)(2,1)S(1)}, bf16[104,640]{1,0:T(8,128)(2,1)S(1)}, u32[]{:S(2)}, u32[]{:S(2)}) collective-permute-start(bf16[104,640]{1,0:T(8,128)(2,1)S(1)} %fusion.5.refs_0_), channel_id=1, source_target_pairs={{0,24},{8,16},{16,8},{24,0},{1,25},{9,17},{17,9},{25,1},{2,26},{10... | collective-permute-start | bytes 399368 | tf_op jit(solution)/shard_map/ppermute | solution.py:737
  134.7 7.4 %collective-permute-start.37 = (bf16[104,640]{1,0:T(8,128)(2,1)S(1)}, bf16[104,640]{1,0:T(8,128)(2,1)S(1)}, u32[]{:S(2)}, u32[]{:S(2)}) collective-permute-start(bf16[104,640]{1,0:T(8,128)(2,1)S(1)} %fusion.5.refs_0_), channel_id=1, source_target_pairs={{0,16},{8,24},{16,0},{24,8},{1,17},{9,25},{17,1},{25,9},{2,18},{10... | collective-permute-start | bytes 399368 | tf_op jit(solution)/shard_map/ppermute | solution.py:737
  135.6 6.5 %collective-permute-start.36 = (bf16[104,640]{1,0:T(8,128)(2,1)S(1)}, bf16[104,640]{1,0:T(8,128)(2,1)S(1)}, u32[]{:S(2)}, u32[]{:S(2)}) collective-permute-start(bf16[104,640]{1,0:T(8,128)(2,1)S(1)} %fusion.5.refs_0_), channel_id=1, source_target_pairs={{0,8},{8,0},{16,24},{24,16},{1,9},{9,1},{17,25},{25,17},{2,10},{10... | collective-permute-start | bytes 399368 | tf_op jit(solution)/shard_map/ppermute | solution.py:737
